TPU v7x, 1024 devices: a whole 4x4x32 slice. The times are simulated.
1024 devices in a mesh: dp: 32 (over z), task: 8 (over y, core), mp: 4 (over x).
Axes of the slice: x: 4, y: 4, z: 32, core: 2. Of those that a mesh axis runs over, the one named last changes fastest.
Arguments:
- tokens: bfloat16 [49152, 2048], P(('dp', 'task')), may hold values from -6 to 6
- expert_ids: int32 [49152, 2], P(('dp', 'task')), may hold values from 0 to 31, all different within a row; in each aligned block of 192 rows (0 to 191, 192 to 383, ...) at most 15 rows name the same one
- gate_levels: int32 [49152, 2], P(('dp', 'task')), may hold values from 1 to 15
- expert_weight: bfloat16 [32, 2048, 4096], P('dp', None, 'mp'), may hold values from -0.125 to 0.125
- tower_weight: bfloat16 [8, 4096, 256], P(None, 'mp'), may hold values from -0.09375 to 0.09375
- tower_out: float32 [8, 256], P('task'), may hold values from -1.5 to 1.5
- cotangent: float32 [8, 49152], P('task', 'dp'), may hold values from -24 to 24
Outputs:
- predictions: float32 [8, 49152], P('task', 'dp')
- mix_grad: bfloat16 [49152, 4096], P(('dp', 'task'), 'mp')
Inputs may be any that keep to these rules, and one draw needn't show every extreme that they name: `expert_ids`: each row names 2 different experts; in each aligned block of 192 rows (the rows of one device) no expert is named by more than 15 rows, and some expert reaches 15 in some block.
All inputs are finite; a program needn't handle non-finite values.
Results may differ from a plain program's by a relative error of at most 0.02.
Values may be sent and summed in bfloat16 or wider, within the bound.
No kernel may reach another device: no remote copies, remote signals or barrier semaphores. Data moves between devices by JAX's collectives and lax.ppermute only.
A program may use at most 64 MiB of HBM per device.

v0:
```python
import jax
import jax.numpy as jnp
from jax import lax
from jax.sharding import PartitionSpec as P


def body(tokens, expert_ids, gate_levels, expert_weight, tower_weight, tower_out, cotangent):
    experts_here = lax.axis_size("dp")
    tok_dev, top = expert_ids.shape
    width = tokens.shape[1]
    routes = tok_dev * top
    capacity = max(2, 5 * routes // (4 * experts_here))
    flat_ids = expert_ids.reshape(routes)
    onehot = (flat_ids[:, None] == jnp.arange(experts_here, dtype=jnp.int32)[None, :]).astype(
        jnp.int32
    )
    rank = jnp.cumsum(onehot, axis=0) - 1
    position = jnp.sum(onehot * rank, axis=1)
    dest = flat_ids * capacity + position
    token_rows = tokens[jnp.arange(routes, dtype=jnp.int32) // top]
    outgoing = jnp.zeros((experts_here * capacity, width), jnp.bfloat16).at[dest].set(token_rows)
    outgoing = outgoing.reshape(experts_here, capacity, width)
    own_weight = expert_weight[0]
    pre = jnp.einsum(
        "sid,dh->sih",
        lax.all_to_all(outgoing, "dp", split_axis=0, concat_axis=0, tiled=True),
        own_weight,
        preferred_element_type=jnp.float32,
    )
    hidden = jax.nn.silu(pre).astype(jnp.bfloat16)
    back = lax.all_to_all(hidden, "dp", split_axis=0, concat_axis=0, tiled=True)
    out_cols = back.shape[2]
    picked = back.reshape(experts_here * capacity, out_cols)[dest].reshape(tok_dev, top, out_cols)
    levels = gate_levels.astype(jnp.float32)
    gates = levels / jnp.sum(levels, axis=1, keepdims=True)
    mix = jnp.sum(picked.astype(jnp.float32) * gates[:, :, None], axis=1).astype(jnp.bfloat16)
    tower_index = lax.axis_index("task")
    own_tower = lax.dynamic_index_in_dim(tower_weight, tower_index, 0, keepdims=False)
    partial_z = jnp.dot(
        lax.all_gather(mix, "task", axis=0, tiled=True),
        own_tower,
        preferred_element_type=jnp.float32,
    )
    z_full = lax.psum(partial_z.astype(jnp.bfloat16), "mp").astype(jnp.float32)
    sig = jax.nn.sigmoid(z_full)
    out_vec = tower_out[0]
    predictions = jnp.dot(z_full * sig, out_vec, preferred_element_type=jnp.float32)[None, :]
    dz_rows = (
        cotangent[0][:, None] * out_vec[None, :] * sig * (1.0 + z_full * (1.0 - sig))
    ).astype(jnp.bfloat16)
    grad_sum = lax.psum_scatter(
        jnp.dot(dz_rows, own_tower.T, preferred_element_type=jnp.float32).astype(jnp.bfloat16),
        "task",
        scatter_dimension=0,
        tiled=True,
    )
    return (predictions, grad_sum)


def solution(mesh):
    return jax.shard_map(
        body,
        mesh=mesh,
        in_specs=(
            P(("dp", "task"), None),
            P(("dp", "task"), None),
            P(("dp", "task"), None),
            P("dp", None, "mp"),
            P(None, "mp", None),
            P("task", None),
            P("task", "dp"),
        ),
        out_specs=(P("task", "dp"), P(("dp", "task"), "mp")),
        check_vma=False,
    )
```

profile of v0, /device:TPU:1, one launch (start us, length us, event | category | flops | bytes accessed | tf_op | source)
XLA Modules:
  0.0 553.3 jit_solution(14098462831189964506)
XLA Ops:
  7.2 0.0 copy-start
  7.2 0.8 broadcast_multiply_fusion
  7.9 0.8 copy.18
  8.7 0.1 eq.25
  8.9 0.1 eq.29
  9.1 0.1 copy.17
  9.2 0.1 mul.60
  9.3 0.9 reduce-window.6
  10.2 0.2 slice_reduce_fusion
  10.5 0.1 fusion.28
  10.6 0.0 copy-done
  10.6 9.3 %scatter_custom_fusion = bf16[480,2048]{1,0:T(8,128)(2,1)} fusion(s32[384]{0:T(512)S(1)} %fusion.30, bf16[192,2048]{1,0:T(8,128)(2,1)S(1)} %copy-done, s32[1024]{0:T(1024)S(1)} %pad_clamp_fusion.1, bf16[]{:T(256)} %constant.37.clone.1), kind=kCustom, calls=%fused_computation.19 | custom fusion | bytes 1966082 | tf_op jit(solution)/shard_map/scatter | solution.py:21
  19.9 1.8 reshape.108
  21.8 0.0 copy-start.3
  21.8 224.4 %all_to_all.10 = bf16[32,15,2048]{2,1,0:T(8,128)(2,1)S(1)} all-to-all(bf16[32,15,2048]{2,1,0:T(8,128)(2,1)S(1)} %reshape.108), channel_id=1, replica_groups=mesh['dp'=32,'task'=8,'mp'=4] {'dp'}, dimensions={0} | all-to-all | bytes 3932160 | tf_op jit(solution)/shard_map/all_to_all | solution.py:26
  246.2 0.0 copy-done.3
  246.2 3.2 multiply_convert_fusion
  249.4 0.0 copy-start.1
  249.4 1.5 copy.22
  251.0 7.5 %all-to-all-start.1 = ((bf16[32,15,1024]{2,1,0:T(8,128)(2,1)}), bf16[32,15,1024]{2,1,0:T(8,128)(2,1)S(1)}, u32[]{:S(2)}, u32[]{:S(2)}) async-start(bf16[32,15,1024]{2,1,0:T(8,128)(2,1)} %copy.22), calls=%async_computation.1 | async-start | bytes 2097152 | tf_op jit(solution)/shard_map/all_to_all | solution.py:31
  258.4 0.0 all-gather.2.cloned.1.call-start
  258.5 0.0 copy-done.1
  258.5 0.1 copy.23
  258.7 104.7 %all-to-all-done.1 = bf16[32,15,1024]{2,1,0:T(8,128)(2,1)S(1)} async-done(((bf16[32,15,1024]{2,1,0:T(8,128)(2,1)}), bf16[32,15,1024]{2,1,0:T(8,128)(2,1)S(1)}, u32[]{:S(2)}, u32[]{:S(2)}) %all-to-all-start.1) | async-done | bytes 983072 | tf_op jit(solution)/shard_map/all_to_all | solution.py:31
  363.4 0.3 reshape.109
  363.7 2.7 gather_fusion
  366.4 2.1 reshape.110
  368.6 2.8 multiply_reduce_fusion
  371.3 0.0 all-gather.2.cloned.1.call-update
  371.4 0.0 all-reduce.2.cloned.1.call-start
  371.4 0.0 copy-start.2
  371.4 0.0 copy-start.5
  371.4 32.7 %all-gather.2.cloned.1.call-done = bf16[1536,1024]{1,0:T(8,128)(2,1)} async-done(((bf16[192,1024]{1,0:T(8,128)(2,1)}), bf16[1536,1024]{1,0:T(8,128)(2,1)}) %all-gather.2.cloned.1.call-update) | async-done | bytes 3145744 | tf_op jit(solution)/shard_map/all_gather | solution.py:40
  404.1 3.8 convolution_convert_fusion.1
  408.0 0.0 all-reduce.2.cloned.1.call-update
  408.0 0.0 reduce-scatter.2.cloned.1.call-start
  408.1 0.0 copy-done.2
  408.1 78.4 %all-reduce.2.cloned.1.call-done = bf16[1536,256]{1,0:T(8,128)(2,1)} async-done(((bf16[1536,256]{1,0:T(8,128)(2,1)}), bf16[1536,256]{1,0:T(8,128)(2,1)}) %all-reduce.2.cloned.1.call-update) | async-done | bytes 786448 | tf_op jit(solution)/shard_map/psum | solution.py:44
  486.5 0.0 copy-done.5
  486.5 4.3 convolution_convert_fusion
  490.8 0.0 copy-start.4
  490.8 0.0 reduce-scatter.2.cloned.1.call-update
  490.8 1.1 copy-done.4
  491.9 1.1 fusion.6
  493.0 53.8 %reduce-scatter.2.cloned.1.call-done = bf16[192,1024]{1,0:T(8,128)(2,1)} async-done(((bf16[1536,1024]{1,0:T(8,128)(2,1)}), bf16[192,1024]{1,0:T(8,128)(2,1)}) %reduce-scatter.2.cloned.1.call-update) | async-done | bytes 393232 | tf_op jit(solution)/shard_map/reduce_scatter | solution.py:51
  (9 shorter events, 0.2 us)
Async XLA Ops:
  7.2 3.5 copy-start
  21.8 224.4 %copy-start.3 = (bf16[1,2048,1024]{2,1,0:T(8,128)(2,1)S(1)}, bf16[1,2048,1024]{2,1,0:T(8,128)(2,1)}, u32[]{:S(2)}) copy-start(bf16[1,2048,1024]{2,1,0:T(8,128)(2,1)} %param.10) | copy-start | bytes 12582916
  249.4 9.1 %copy-start.1 = (s32[192,2]{0,1:T(2,128)S(1)}, s32[192,2]{0,1:T(2,128)}, u32[]{:S(2)}) copy-start(s32[192,2]{0,1:T(2,128)} %param.9) | copy-start | bytes 4612
  251.0 112.4 %all-to-all-start.1 = ((bf16[32,15,1024]{2,1,0:T(8,128)(2,1)}), bf16[32,15,1024]{2,1,0:T(8,128)(2,1)S(1)}, u32[]{:S(2)}, u32[]{:S(2)}) async-start(bf16[32,15,1024]{2,1,0:T(8,128)(2,1)} %copy.22), calls=%async_computation.1 | async-start | bytes 2097152 | tf_op jit(solution)/shard_map/all_to_all | solution.py:31
  258.4 145.7 %all-gather.2.cloned.1.call-start = ((), (), s32[]{:S(2)}) async-start(), calls=%async_computation.3 | async-start | bytes 3538944 | tf_op jit(solution)/shard_map/all_gather | solution.py:40
  371.4 115.1 %all-reduce.2.cloned.1.call-start = ((), (), s32[]{:S(2)}) async-start(), calls=%async_computation.4 | async-start | bytes 1572864 | tf_op jit(solution)/shard_map/psum | solution.py:44
  371.4 36.6 %copy-start.2 = (f32[1,1536]{1,0:T(1,128)S(1)}, f32[1,1536]{1,0:T(1,128)}, u32[]{:S(2)}) copy-start(f32[1,1536]{1,0:T(1,128)} %param.13) | copy-start | bytes 18436
  371.4 115.1 %copy-start.5 = (f32[1,256]{1,0:T(1,128)S(1)}, f32[1,256]{1,0:T(1,128)}, u32[]{:S(2)}) copy-start(f32[1,256]{1,0:T(1,128)} %param.12) | copy-start | bytes 3076
  408.0 138.8 %reduce-scatter.2.cloned.1.call-start = ((), (), s32[]{:S(2)}) async-start(), calls=%async_computation.5 | async-start | bytes 3538944 | tf_op jit(solution)/shard_map/reduce_scatter | solution.py:51
  490.8 1.1 copy-start.4
Sparse Core Ops, SparseCore 0:
  371.5 32.5 all-gather.1
  408.1 78.3 all-reduce.1
  490.9 55.8 reduce-scatter.1
where the time goes:
time: 554 us; the launch traced here: 553 us
  waiting for transfers between devices  270 us (49%)
  blocking collectives  224 us (40%)
  local copies, waits for them, and re-layouts  20.6 us (4%)
  between operations  13.9 us (3%)
  matrix products  12.5 us (2%)
  starting transfers between devices  7.59 us (1%)
    all_to_all x1, blocking collectives, body(): lax.all_to_all(outgoing, 'dp', split_axis=0, concat_axis=0, tiled=True)  224 us
    all_to_all x1, waiting for transfers between devices, body(): back = lax.all_to_all(hidden, 'dp', split_axis=0, concat_axis=0, tiled=True)  105 us
    psum x1, waiting for transfers between devices, body(): z_full = lax.psum(partial_z.astype(jnp.bfloat16), 'mp').astype(jnp.float32)  78.4 us
    reduce_scatter x1, waiting for transfers between devices, body(): lax.psum_scatter(jnp.dot(dz_rows, own_tower.T, preferred_element_type=jnp...  53.8 us
    all_gather x1, waiting for transfers between devices, body(): lax.all_gather(mix, 'task', axis=0, tiled=True)  32.7 us
  transfers between devices with their start and end apart: 4, of which 4 were waited for; matrix products, arithmetic and copies ran while one was open for 0% of the time, Pallas kernels for 0%

commit v1 on v0

v1 whole, which is shorter than its diff:
```python
import functools

import jax
import jax.numpy as jnp
from jax import lax
from jax.experimental import pallas as pl
from jax.experimental.pallas import tpu as pltpu
from jax.sharding import PartitionSpec as P

F32 = jnp.float32
BF16 = jnp.bfloat16
VMEM = pl.BlockSpec(memory_space=pltpu.VMEM)
SMEM = pl.BlockSpec(memory_space=pltpu.SMEM)
LANES = (((1,), (1,)), ((), ()))
ROWS = (((0,), (0,)), ((), ()))


def slot_rows(ids_ref, experts, pitch):
    top, count = ids_ref.shape
    earlier = (
        lax.broadcasted_iota(jnp.int32, (count, count), 0)
        < lax.broadcasted_iota(jnp.int32, (count, count), 1)
    ).astype(F32).astype(BF16)
    names = lax.broadcasted_iota(jnp.int32, (experts, count), 0)
    seen = jnp.zeros((experts, 1), F32)
    slots = []
    for k in range(top):
        row = ids_ref[k : k + 1, :]
        hit = (names == row).astype(F32)
        before = jnp.dot(hit.astype(BF16), earlier, preferred_element_type=F32)
        rank = jnp.sum(hit * (before + seen), axis=0, keepdims=True)
        seen = seen + jnp.sum(hit, axis=1, keepdims=True)
        slots.append(row * pitch + rank.astype(jnp.int32))
    return slots


def dispatch_kernel(experts, pitch, col_ref, ids_ref, tok_ref, out_ref):
    slots = slot_rows(ids_ref, experts, pitch)
    count = ids_ref.shape[1]
    here = lax.broadcasted_iota(jnp.int32, (experts * pitch, count), 0)
    pick = functools.reduce(jnp.logical_or, [here == s for s in slots])
    pick = pick.astype(F32).astype(BF16)
    out_ref[...] = jnp.dot(pick, tok_ref[...], preferred_element_type=F32).astype(BF16)


def expert_kernel(n, me_ref, *refs):
    ins, (w_ref, tw_ref), outs, hid_ref = refs[:n], refs[n : n + 2], refs[n + 2 : -1], refs[-1]
    me = me_ref[0]
    depth = ins[0].shape[1]
    tile = tw_ref.shape[2]
    per = tw_ref.shape[0] // n

    @pl.loop(0, w_ref.shape[1] // tile)
    def _(c):
        cols = pl.ds(pl.multiple_of(c * tile, tile), tile)
        total = None
        for s in range(n):
            first = pl.multiple_of(lax.rem(me - s + n, n) * depth, depth)
            part = jnp.dot(ins[s][...], w_ref[pl.ds(first, depth), cols], preferred_element_type=F32)
            total = part if total is None else total + part
        hid_ref[:, cols] = (total / (1.0 + jnp.exp(-total))).astype(BF16)

    for s in range(n):
        to = lax.rem(me + s, n)
        for i in range(per):
            outs[s][:, i * tile : (i + 1) * tile] = jnp.dot(
                hid_ref[...], tw_ref[to * per + i], preferred_element_type=F32
            ).astype(BF16)


def combine_kernel(experts, pitch, ids_ref, lev_ref, back_ref, out_ref):
    slots = slot_rows(ids_ref, experts, pitch)
    levels = lev_ref[...].astype(F32)
    gates = levels / jnp.sum(levels, axis=0, keepdims=True)
    here = lax.broadcasted_iota(jnp.int32, (experts * pitch, ids_ref.shape[1]), 0)
    share = sum(jnp.where(here == s, gates[k : k + 1, :], 0.0) for k, s in enumerate(slots))
    high = share.astype(BF16)
    low = (share - high.astype(F32)).astype(BF16)
    rows = back_ref[...]
    z = lax.dot_general(high, rows, ROWS, preferred_element_type=F32)
    z = z + lax.dot_general(low, rows, ROWS, preferred_element_type=F32)
    out_ref[...] = z.astype(BF16)


def tower_kernel(n, me_ref, side_ref, *refs):
    ins, tw_ref, pred_ref, grad_ref, acc_ref = refs[:n], refs[n], refs[n + 1], refs[n + 2], refs[n + 3]
    me = me_ref[0]
    count = ins[0].shape[0]
    tile = tw_ref.shape[2]
    per = tw_ref.shape[0] // n
    cot = jnp.transpose(side_ref[:, :256])[:count]
    lane = lax.broadcasted_iota(jnp.int32, cot.shape, 1)
    for s in range(n):
        for i in range(per):
            t = lax.rem(me - s + n, n) * per + i
            z = ins[s][:, i * tile : (i + 1) * tile].astype(F32)
            out_vec = side_ref[pl.ds(t, 1), 256:]
            sig = 1.0 / (1.0 + jnp.exp(-z))
            pred_ref[pl.ds(t, 1), :] = lax.dot_general(
                out_vec, z * sig, LANES, precision=lax.Precision.HIGHEST, preferred_element_type=F32
            )
            c = jnp.sum(jnp.where(lane == t, cot, 0.0), axis=1, keepdims=True)
            dz = (c * out_vec * sig * (1.0 + z * (1.0 - sig))).astype(BF16)
            part = lax.dot_general(dz, tw_ref[t], LANES, preferred_element_type=F32)
            if s == 0 and i == 0:
                acc_ref[...] = part
            else:
                acc_ref[...] += part
    grad_ref[...] = acc_ref[...].astype(BF16)


def body(tokens, expert_ids, gate_levels, expert_weight, tower_weight, tower_out, cotangent):
    experts = lax.axis_size("dp")
    tasks = lax.axis_size("task")
    n = lax.axis_size("mp")
    count, top = expert_ids.shape
    width = tokens.shape[1]
    part = width // n
    towers, units, tile = tower_weight.shape
    cols = towers * tile // n
    cap = max(2, 5 * count * top // (4 * experts))
    pitch = -(-cap // 8) * 8
    rows = experts * pitch
    me = lax.axis_index("mp").astype(jnp.int32).reshape(1)
    ids = expert_ids.T
    levels = gate_levels.T

    side = jnp.concatenate(
        [
            jnp.pad(cotangent.reshape(tasks, count), ((0, 0), (0, 256 - count))),
            jnp.broadcast_to(tower_out, (tasks, tile)),
        ],
        axis=1,
    )
    side = lax.all_to_all(side, "task", split_axis=0, concat_axis=0, tiled=True)

    out = pl.pallas_call(
        functools.partial(dispatch_kernel, experts, pitch),
        out_shape=jax.ShapeDtypeStruct((rows, part), BF16),
        grid_spec=pltpu.PrefetchScalarGridSpec(
            num_scalar_prefetch=1,
            grid=(1,),
            in_specs=[
                pl.BlockSpec((top, count), lambda g, m: (0, 0)),
                pl.BlockSpec((count, part), lambda g, m: (0, m[0])),
            ],
            out_specs=pl.BlockSpec((rows, part), lambda g, m: (0, 0)),
        ),
        name="dispatch",
    )(me, ids, tokens)

    def over_dp(a):
        a = a.reshape(experts, pitch, a.shape[1])
        return lax.all_to_all(a, "dp", split_axis=0, concat_axis=0, tiled=True).reshape(rows, -1)

    def shift(a, s):
        return lax.ppermute(a, "mp", [(i, (i + s) % n) for i in range(n)])

    mine = over_dp(out)
    pieces = [mine] + [shift(mine, s) for s in range(1, n)]
    outs = pl.pallas_call(
        functools.partial(expert_kernel, n),
        out_shape=[jax.ShapeDtypeStruct((rows, cols), BF16)] * n,
        in_specs=[SMEM] + [VMEM] * (n + 2),
        out_specs=[VMEM] * n,
        scratch_shapes=[pltpu.VMEM((rows, units), BF16)],
        compiler_params=pltpu.CompilerParams(vmem_limit_bytes=40 << 20),
        cost_estimate=pl.CostEstimate(
            flops=2 * rows * units * (width + towers * tile),
            bytes_accessed=2 * units * (width + towers * tile),
            transcendentals=rows * units,
        ),
        name="expert",
    )(me, *pieces, expert_weight[0], tower_weight)
    total = sum([outs[0].astype(F32)] + [shift(outs[s], s).astype(F32) for s in range(1, n)])
    back = over_dp(total.astype(BF16))

    z = pl.pallas_call(
        functools.partial(combine_kernel, experts, pitch),
        out_shape=jax.ShapeDtypeStruct((count, cols), BF16),
        in_specs=[VMEM] * 3,
        out_specs=VMEM,
        name="combine",
    )(ids, levels, back)
    zs = [z] + [shift(z, s) for s in range(1, n)]

    pred, grad = pl.pallas_call(
        functools.partial(tower_kernel, n),
        out_shape=[
            jax.ShapeDtypeStruct((towers, count), F32),
            jax.ShapeDtypeStruct((count, units), BF16),
        ],
        in_specs=[SMEM] + [VMEM] * (n + 2),
        out_specs=[VMEM] * 2,
        scratch_shapes=[pltpu.VMEM((count, units), F32)],
        compiler_params=pltpu.CompilerParams(vmem_limit_bytes=40 << 20),
        name="tower",
    )(me, side, *zs, tower_weight)
    pred = lax.all_to_all(pred, "task", split_axis=0, concat_axis=0, tiled=True)
    return pred.reshape(1, tasks * count), grad


def solution(mesh):
    return jax.shard_map(
        body,
        mesh=mesh,
        in_specs=(
            P(("dp", "task"), None),
            P(("dp", "task"), None),
            P(("dp", "task"), None),
            P("dp", None, "mp"),
            P(None, "mp", None),
            P("task", None),
            P("task", "dp"),
        ),
        out_specs=(P("task", "dp"), P(("dp", "task"), "mp")),
        check_vma=False,
    )
```

time: 554 us -> 277 us (0.50)
  waiting for transfers between devices: 270 us -> 102 us
  blocking collectives: 224 us -> 112 us
  starting transfers between devices: 7.59 us -> 37.1 us
  Pallas kernels: 0 us -> 13.5 us
  between operations: 13.9 us -> 0.79 us
  matrix products: 12.5 us -> 0 us
  local copies, waits for them, and re-layouts: 20.6 us -> 9.06 us
    all_to_all x1 -> x3, blocking collectives: 224 us -> 112 us  [the longest x1 93.6 us: over_dp(): lax.all_to_all(a, 'dp', split_axis=0, concat_axis=0, tiled=True)]
    psum x1 -> x0, waiting for transfers between devices: 78.4 us -> none  [body(): z_full = lax.psum(partial_z.astype(jnp.bfloat16), 'mp').astype(jnp.float32)]
    reduce_scatter x1 -> x0, waiting for transfers between devices: 53.8 us -> none  [body(): lax.psum_scatter(jnp.dot(dz_rows, own_tower.T, preferred_element_type=jnp...]
    all_to_all x1, waiting for transfers between devices: 105 us -> 64.3 us  [over_dp(): lax.all_to_all(a, 'dp', split_axis=0, concat_axis=0, tiled=True)]
    ppermute x0 -> x9, waiting for transfers between devices: none -> 38.2 us  [shift(): return lax.ppermute(a, 'mp', [(i, (i + s) % n) for i in range(n)])]
    ppermute x0 -> x9, starting transfers between devices: none -> 33.2 us  [shift(): return lax.ppermute(a, 'mp', [(i, (i + s) % n) for i in range(n)])]
    all_gather x1 -> x0, waiting for transfers between devices: 32.7 us -> none  [body(): lax.all_gather(mix, 'task', axis=0, tiled=True)]
    pallas_call x0 -> x4, Pallas kernels: none -> 13.5 us  [the longest x1 5.34 us: body(): pl.pallas_call(functools.partial(expert_kernel, n), out_shape=[jax.ShapeD...]
  transfers between devices with their start and end apart: 4 -> 10, of which waited for: 4 -> 7; matrix products, arithmetic and copies ran while one was open for 0% -> 0% of each run, Pallas kernels for 0% -> 0%
where the time goes in v1:
time: 277 us; the launch traced here: 276 us
  blocking collectives  112 us (40%)
  waiting for transfers between devices  102 us (37%)
  starting transfers between devices  37.1 us (13%)
  Pallas kernels  13.5 us (5%)
  local copies, waits for them, and re-layouts  9.06 us (3%)
    all_to_all x1, blocking collectives, over_dp(): lax.all_to_all(a, 'dp', split_axis=0, concat_axis=0, tiled=True)  93.6 us
    all_to_all x1, waiting for transfers between devices, over_dp(): lax.all_to_all(a, 'dp', split_axis=0, concat_axis=0, tiled=True)  64.3 us
    ppermute x9, waiting for transfers between devices, shift(): return lax.ppermute(a, 'mp', [(i, (i + s) % n) for i in range(n)])  38.2 us
    ppermute x9, starting transfers between devices, shift(): return lax.ppermute(a, 'mp', [(i, (i + s) % n) for i in range(n)])  33.2 us
    all_to_all x1, blocking collectives, body(): side = lax.all_to_all(side, 'task', split_axis=0, concat_axis=0, tiled=True)  11.1 us
    unnamed x15, local copies, waits for them, and re-layouts  8.28 us
    all_to_all x1, blocking collectives, body(): pred = lax.all_to_all(pred, 'task', split_axis=0, concat_axis=0, tiled=True)  7.68 us
  transfers between devices with their start and end apart: 10, of which 7 were waited for; matrix products, arithmetic and copies ran while one was open for 0% of the time, Pallas kernels for 0%

profile of v1, /device:TPU:1, one launch (start us, length us, event | category | flops | bytes accessed | tf_op | source)
XLA Modules:
  0.0 276.4 jit_solution(10502964457722767652)
XLA Ops:
  0.6 2.2 dispatch.1
  2.8 93.6 %all_to_all.30 = bf16[32,16,512]{2,1,0:T(8,128)(2,1)S(1)} all-to-all(bf16[32,16,512]{2,1,0:T(8,128)(2,1)} %bitcast.21), channel_id=1, replica_groups=mesh['dp'=32,'task'=8,'mp'=4] {'dp'}, dimensions={0} | all-to-all | bytes 1048576 | tf_op jit(solution)/shard_map/all_to_all | solution.py:154
  96.4 3.1 %collective-permute-start = (bf16[512,512]{1,0:T(8,128)(2,1)S(1)}, bf16[512,512]{1,0:T(8,128)(2,1)S(1)}, u32[]{:S(2)}, u32[]{:S(2)}) collective-permute-start(bf16[512,512]{1,0:T(8,128)(2,1)S(1)} %bitcast.13), channel_id=1, source_target_pairs={{0,1},{1,2},{2,3},{3,0},{4,5},{5,6},{6,7},{7,4},{8,9},{9,10},{10,1... | collective-permute-start | bytes 1572872 | tf_op jit(solution)/shard_map/ppermute | solution.py:157
  99.5 4.3 %collective-permute-start.1 = (bf16[512,512]{1,0:T(8,128)(2,1)S(1)}, bf16[512,512]{1,0:T(8,128)(2,1)S(1)}, u32[]{:S(2)}, u32[]{:S(2)}) collective-permute-start(bf16[512,512]{1,0:T(8,128)(2,1)S(1)} %bitcast.14), channel_id=1, source_target_pairs={{0,2},{1,3},{2,0},{3,1},{4,6},{5,7},{6,4},{7,5},{8,10},{9,11},{10,... | collective-permute-start | bytes 1572872 | tf_op jit(solution)/shard_map/ppermute | solution.py:157
  103.9 3.1 %collective-permute-start.2 = (bf16[512,512]{1,0:T(8,128)(2,1)S(1)}, bf16[512,512]{1,0:T(8,128)(2,1)S(1)}, u32[]{:S(2)}, u32[]{:S(2)}) collective-permute-start(bf16[512,512]{1,0:T(8,128)(2,1)S(1)} %bitcast.15), channel_id=1, source_target_pairs={{0,3},{1,0},{2,1},{3,2},{4,7},{5,4},{6,5},{7,6},{8,11},{9,8},{10,9... | collective-permute-start | bytes 1572872 | tf_op jit(solution)/shard_map/ppermute | solution.py:157
  106.9 4.4 %collective-permute-done.refs_1_ = bf16[512,512]{1,0:T(8,128)(2,1)S(1)} collective-permute-done((bf16[512,512]{1,0:T(8,128)(2,1)S(1)}, bf16[512,512]{1,0:T(8,128)(2,1)S(1)}, u32[]{:S(2)}, u32[]{:S(2)}) %collective-permute-start) | collective-permute-done | bytes 524320 | tf_op jit(solution)/shard_map/ppermute | solution.py:157
  111.4 12.2 %collective-permute-done.1.refs_2_ = bf16[512,512]{1,0:T(8,128)(2,1)S(1)} collective-permute-done((bf16[512,512]{1,0:T(8,128)(2,1)S(1)}, bf16[512,512]{1,0:T(8,128)(2,1)S(1)}, u32[]{:S(2)}, u32[]{:S(2)}) %collective-permute-start.1) | collective-permute-done | bytes 524320 | tf_op jit(solution)/shard_map/ppermute | solution.py:157
  123.6 2.4 collective-permute-done.2.refs_3_
  126.0 0.0 copy-start
  126.0 2.2 copy-done
  128.2 0.0 copy-start.3
  128.2 2.2 copy-done.3
  130.4 0.0 copy-start.5
  130.4 0.0 copy-start.6
  130.4 5.3 %expert.1 = (bf16[512,512]{1,0:T(8,128)(2,1)S(1)}, bf16[512,512]{1,0:T(8,128)(2,1)S(1)}, bf16[512,512]{1,0:T(8,128)(2,1)S(1)}, bf16[512,512]{1,0:T(8,128)(2,1)S(1)}) custom-call(s32[1]{0:T(128)} %bitcast.col_ref.me_ref, bf16[512,512]{1,0:T(8,128)(2,1)S(1)} %bitcast.16, bf16[512,512]{1,0:T(8,128)(2,1)S(1)} %collective-permute-done.refs_1_, ...), custom_call_target="tpu_custom_call" | custom-call | flops 4294967296 | bytes 8388608 | tf_op jit(solution)/shard_map/expert/pallas_call | solution.py:161
  135.8 5.1 %collective-permute-start.3 = (bf16[512,512]{1,0:T(8,128)(2,1)S(1)}, bf16[512,512]{1,0:T(8,128)(2,1)S(1)}, u32[]{:S(2)}, u32[]{:S(2)}) collective-permute-start(bf16[512,512]{1,0:T(8,128)(2,1)S(1)} %get-tuple-element.9), channel_id=1, source_target_pairs={{0,1},{1,2},{2,3},{3,0},{4,5},{5,6},{6,7},{7,4},{8,9},{9,10},{10,1... | collective-permute-start | bytes 1572872 | tf_op jit(solution)/shard_map/ppermute | solution.py:157
  140.8 3.3 %collective-permute-start.4 = (bf16[512,512]{1,0:T(8,128)(2,1)S(1)}, bf16[512,512]{1,0:T(8,128)(2,1)S(1)}, u32[]{:S(2)}, u32[]{:S(2)}) collective-permute-start(bf16[512,512]{1,0:T(8,128)(2,1)S(1)} %get-tuple-element.10), channel_id=1, source_target_pairs={{0,2},{1,3},{2,0},{3,1},{4,6},{5,7},{6,4},{7,5},{8,10},{9,11},{10,... | collective-permute-start | bytes 1572872 | tf_op jit(solution)/shard_map/ppermute | solution.py:157
  144.2 2.9 %collective-permute-start.5 = (bf16[512,512]{1,0:T(8,128)(2,1)S(1)}, bf16[512,512]{1,0:T(8,128)(2,1)S(1)}, u32[]{:S(2)}, u32[]{:S(2)}) collective-permute-start(bf16[512,512]{1,0:T(8,128)(2,1)S(1)} %get-tuple-element.11), channel_id=1, source_target_pairs={{0,3},{1,0},{2,1},{3,2},{4,7},{5,4},{6,5},{7,6},{8,11},{9,8},{10,9... | collective-permute-start | bytes 1572872 | tf_op jit(solution)/shard_map/ppermute | solution.py:157
  147.1 5.2 %collective-permute-done.3 = bf16[512,512]{1,0:T(8,128)(2,1)S(1)} collective-permute-done((bf16[512,512]{1,0:T(8,128)(2,1)S(1)}, bf16[512,512]{1,0:T(8,128)(2,1)S(1)}, u32[]{:S(2)}, u32[]{:S(2)}) %collective-permute-start.3) | collective-permute-done | bytes 524320 | tf_op jit(solution)/shard_map/ppermute | solution.py:157
  152.3 12.8 %collective-permute-done.4 = bf16[512,512]{1,0:T(8,128)(2,1)S(1)} collective-permute-done((bf16[512,512]{1,0:T(8,128)(2,1)S(1)}, bf16[512,512]{1,0:T(8,128)(2,1)S(1)}, u32[]{:S(2)}, u32[]{:S(2)}) %collective-permute-start.4) | collective-permute-done | bytes 524320 | tf_op jit(solution)/shard_map/ppermute | solution.py:157
  165.0 1.1 collective-permute-done.5
  166.2 1.1 add_convert_fusion
  167.2 3.9 %all-to-all-start.2 = ((bf16[32,16,512]{2,1,0:T(8,128)(2,1)}), bf16[32,16,512]{2,1,0:T(8,128)(2,1)S(1)}, u32[]{:S(2)}, u32[]{:S(2)}) async-start(bf16[32,16,512]{2,1,0:T(8,128)(2,1)} %bitcast.7), calls=%async_computation.2 | async-start | bytes 1048576 | tf_op jit(solution)/shard_map/all_to_all | solution.py:154
  171.1 0.0 copy-done.5
  171.2 0.1 reshape.31
  171.2 0.0 copy-done.6
  171.2 64.3 %all-to-all-done.2 = bf16[32,16,512]{2,1,0:T(8,128)(2,1)S(1)} async-done(((bf16[32,16,512]{2,1,0:T(8,128)(2,1)}), bf16[32,16,512]{2,1,0:T(8,128)(2,1)S(1)}, u32[]{:S(2)}, u32[]{:S(2)}) %all-to-all-start.2) | async-done | bytes 524320 | tf_op jit(solution)/shard_map/all_to_all | solution.py:154
  235.5 0.0 copy-start.4
  235.5 0.8 copy-done.4
  236.3 2.4 combine.1.refs_0_
  238.7 5.2 %collective-permute-start.6 = (bf16[192,512]{1,0:T(8,128)(2,1)}, bf16[192,512]{1,0:T(8,128)(2,1)S(1)}, u32[]{:S(2)}, u32[]{:S(2)}) collective-permute-start(bf16[192,512]{1,0:T(8,128)(2,1)} %combine.1.refs_0_), channel_id=1, source_target_pairs={{0,1},{1,2},{2,3},{3,0},{4,5},{5,6},{6,7},{7,4},{8,9},{9,10},{10,1... | collective-permute-start | bytes 589832 | tf_op jit(solution)/shard_map/ppermute | solution.py:157
  243.9 3.3 %collective-permute-start.7 = (bf16[192,512]{1,0:T(8,128)(2,1)}, bf16[192,512]{1,0:T(8,128)(2,1)S(1)}, u32[]{:S(2)}, u32[]{:S(2)}) collective-permute-start(bf16[192,512]{1,0:T(8,128)(2,1)} %combine.1.refs_0_), channel_id=1, source_target_pairs={{0,2},{1,3},{2,0},{3,1},{4,6},{5,7},{6,4},{7,5},{8,10},{9,11},{10,... | collective-permute-start | bytes 589832 | tf_op jit(solution)/shard_map/ppermute | solution.py:157
  247.3 2.9 %collective-permute-start.8 = (bf16[192,512]{1,0:T(8,128)(2,1)}, bf16[192,512]{1,0:T(8,128)(2,1)S(1)}, u32[]{:S(2)}, u32[]{:S(2)}) collective-permute-start(bf16[192,512]{1,0:T(8,128)(2,1)} %combine.1.refs_0_), channel_id=1, source_target_pairs={{0,3},{1,0},{2,1},{3,2},{4,7},{5,4},{6,5},{7,6},{8,11},{9,8},{10,9... | collective-permute-start | bytes 589832 | tf_op jit(solution)/shard_map/ppermute | solution.py:157
  250.2 11.1 %all_to_all.31 = f32[8,1,512]{2,1,0:T(1,128)S(1)} all-to-all(f32[8,1,512]{2,1,0:T(1,128)S(1)} %all_to_all.19), channel_id=1, replica_groups=mesh['dp'=32,'task'=8,'mp'=4] {'task'}, dimensions={0} | all-to-all | bytes 32768 | tf_op jit(solution)/shard_map/all_to_all | solution.py:135
  261.3 0.0 collective-permute-done.6.refs_1_
  261.3 0.0 collective-permute-done.7.refs_2_
  261.3 0.0 collective-permute-done.8.refs_3_
  261.3 0.0 copy-start.1
  261.4 2.2 copy-done.1
  263.5 0.0 copy-start.2
  263.5 0.9 copy-done.2
  264.5 3.6 %tower.1 = (f32[8,192]{1,0:T(8,128)S(1)}, bf16[192,1024]{1,0:T(8,128)(2,1)}) custom-call(s32[1]{0:T(128)} %bitcast.col_ref.me_ref, f32[8,512]{1,0:T(8,128)S(1)} %bitcast.17, bf16[192,512]{1,0:T(8,128)(2,1)S(1)} %copy-done.2, bf16[192,512]{1,0:T(8,128)(2,1)S(1)} %collective-permute-done.6.refs_1_, bf16[192,512]{1,0:T(8,128)(2,1)S(1)} %collective-permute-done.7.refs_2_, ...), custom_call_target="tpu_custom_call" | custom-call | tf_op jit(solution)/shard_map/tower/pallas_call | solution.py:187
  268.1 7.7 %all_to_all.32 = f32[8,1,192]{2,1,0:T(1,128)S(1)} all-to-all(f32[8,1,192]{2,1,0:T(1,128)S(1)} %copy.9), channel_id=1, replica_groups=mesh['dp'=32,'task'=8,'mp'=4] {'task'}, dimensions={0} | all-to-all | bytes 12288 | tf_op jit(solution)/shard_map/all_to_all | solution.py:199
  275.8 0.7 reshape.36
  (7 shorter events, 0.1 us)
Async XLA Ops:
  96.4 15.0 %collective-permute-start = (bf16[512,512]{1,0:T(8,128)(2,1)S(1)}, bf16[512,512]{1,0:T(8,128)(2,1)S(1)}, u32[]{:S(2)}, u32[]{:S(2)}) collective-permute-start(bf16[512,512]{1,0:T(8,128)(2,1)S(1)} %bitcast.13), channel_id=1, source_target_pairs={{0,1},{1,2},{2,3},{3,0},{4,5},{5,6},{6,7},{7,4},{8,9},{9,10},{10,1... | collective-permute-start | bytes 1572872 | tf_op jit(solution)/shard_map/ppermute | solution.py:157
  99.5 24.1 %collective-permute-start.1 = (bf16[512,512]{1,0:T(8,128)(2,1)S(1)}, bf16[512,512]{1,0:T(8,128)(2,1)S(1)}, u32[]{:S(2)}, u32[]{:S(2)}) collective-permute-start(bf16[512,512]{1,0:T(8,128)(2,1)S(1)} %bitcast.14), channel_id=1, source_target_pairs={{0,2},{1,3},{2,0},{3,1},{4,6},{5,7},{6,4},{7,5},{8,10},{9,11},{10,... | collective-permute-start | bytes 1572872 | tf_op jit(solution)/shard_map/ppermute | solution.py:157
  103.9 22.2 %collective-permute-start.2 = (bf16[512,512]{1,0:T(8,128)(2,1)S(1)}, bf16[512,512]{1,0:T(8,128)(2,1)S(1)}, u32[]{:S(2)}, u32[]{:S(2)}) collective-permute-start(bf16[512,512]{1,0:T(8,128)(2,1)S(1)} %bitcast.15), channel_id=1, source_target_pairs={{0,3},{1,0},{2,1},{3,2},{4,7},{5,4},{6,5},{7,6},{8,11},{9,8},{10,9... | collective-permute-start | bytes 1572872 | tf_op jit(solution)/shard_map/ppermute | solution.py:157
  126.0 2.2 copy-start
  128.2 2.2 copy-start.3
  130.4 40.7 %copy-start.5 = (f32[1,1536]{1,0:T(1,128)S(1)}, f32[1,1536]{1,0:T(1,128)}, u32[]{:S(2)}) copy-start(f32[1,1536]{1,0:T(1,128)} %param.13) | copy-start | bytes 18436
  130.4 40.8 %copy-start.6 = (f32[1,256]{1,0:T(1,128)S(1)}, f32[1,256]{1,0:T(1,128)}, u32[]{:S(2)}) copy-start(f32[1,256]{1,0:T(1,128)} %param.12) | copy-start | bytes 3076
  135.8 16.5 %collective-permute-start.3 = (bf16[512,512]{1,0:T(8,128)(2,1)S(1)}, bf16[512,512]{1,0:T(8,128)(2,1)S(1)}, u32[]{:S(2)}, u32[]{:S(2)}) collective-permute-start(bf16[512,512]{1,0:T(8,128)(2,1)S(1)} %get-tuple-element.9), channel_id=1, source_target_pairs={{0,1},{1,2},{2,3},{3,0},{4,5},{5,6},{6,7},{7,4},{8,9},{9,10},{10,1... | collective-permute-start | bytes 1572872 | tf_op jit(solution)/shard_map/ppermute | solution.py:157
  140.8 24.2 %collective-permute-start.4 = (bf16[512,512]{1,0:T(8,128)(2,1)S(1)}, bf16[512,512]{1,0:T(8,128)(2,1)S(1)}, u32[]{:S(2)}, u32[]{:S(2)}) collective-permute-start(bf16[512,512]{1,0:T(8,128)(2,1)S(1)} %get-tuple-element.10), channel_id=1, source_target_pairs={{0,2},{1,3},{2,0},{3,1},{4,6},{5,7},{6,4},{7,5},{8,10},{9,11},{10,... | collective-permute-start | bytes 1572872 | tf_op jit(solution)/shard_map/ppermute | solution.py:157
  144.2 22.0 %collective-permute-start.5 = (bf16[512,512]{1,0:T(8,128)(2,1)S(1)}, bf16[512,512]{1,0:T(8,128)(2,1)S(1)}, u32[]{:S(2)}, u32[]{:S(2)}) collective-permute-start(bf16[512,512]{1,0:T(8,128)(2,1)S(1)} %get-tuple-element.11), channel_id=1, source_target_pairs={{0,3},{1,0},{2,1},{3,2},{4,7},{5,4},{6,5},{7,6},{8,11},{9,8},{10,9... | collective-permute-start | bytes 1572872 | tf_op jit(solution)/shard_map/ppermute | solution.py:157
  167.2 68.3 %all-to-all-start.2 = ((bf16[32,16,512]{2,1,0:T(8,128)(2,1)}), bf16[32,16,512]{2,1,0:T(8,128)(2,1)S(1)}, u32[]{:S(2)}, u32[]{:S(2)}) async-start(bf16[32,16,512]{2,1,0:T(8,128)(2,1)} %bitcast.7), calls=%async_computation.2 | async-start | bytes 1048576 | tf_op jit(solution)/shard_map/all_to_all | solution.py:154
  235.5 0.8 copy-start.4
  238.7 22.6 %collective-permute-start.6 = (bf16[192,512]{1,0:T(8,128)(2,1)}, bf16[192,512]{1,0:T(8,128)(2,1)S(1)}, u32[]{:S(2)}, u32[]{:S(2)}) collective-permute-start(bf16[192,512]{1,0:T(8,128)(2,1)} %combine.1.refs_0_), channel_id=1, source_target_pairs={{0,1},{1,2},{2,3},{3,0},{4,5},{5,6},{6,7},{7,4},{8,9},{9,10},{10,1... | collective-permute-start | bytes 589832 | tf_op jit(solution)/shard_map/ppermute | solution.py:157
  243.9 17.4 %collective-permute-start.7 = (bf16[192,512]{1,0:T(8,128)(2,1)}, bf16[192,512]{1,0:T(8,128)(2,1)S(1)}, u32[]{:S(2)}, u32[]{:S(2)}) collective-permute-start(bf16[192,512]{1,0:T(8,128)(2,1)} %combine.1.refs_0_), channel_id=1, source_target_pairs={{0,2},{1,3},{2,0},{3,1},{4,6},{5,7},{6,4},{7,5},{8,10},{9,11},{10,... | collective-permute-start | bytes 589832 | tf_op jit(solution)/shard_map/ppermute | solution.py:157
  247.3 14.1 %collective-permute-start.8 = (bf16[192,512]{1,0:T(8,128)(2,1)}, bf16[192,512]{1,0:T(8,128)(2,1)S(1)}, u32[]{:S(2)}, u32[]{:S(2)}) collective-permute-start(bf16[192,512]{1,0:T(8,128)(2,1)} %combine.1.refs_0_), channel_id=1, source_target_pairs={{0,3},{1,0},{2,1},{3,2},{4,7},{5,4},{6,5},{7,6},{8,11},{9,8},{10,9... | collective-permute-start | bytes 589832 | tf_op jit(solution)/shard_map/ppermute | solution.py:157
  261.3 2.2 copy-start.1
  263.5 0.9 copy-start.2

commit v2 on v1

v2 whole, which is shorter than its diff:
```python
import functools

import jax
import jax.numpy as jnp
from jax import lax
from jax.experimental import pallas as pl
from jax.experimental.pallas import tpu as pltpu
from jax.sharding import PartitionSpec as P

F32 = jnp.float32
BF16 = jnp.bfloat16
VMEM = pl.BlockSpec(memory_space=pltpu.VMEM)
HBM = pl.BlockSpec(memory_space=pltpu.HBM)
SMEM = pl.BlockSpec(memory_space=pltpu.SMEM)
LANES = (((1,), (1,)), ((), ()))
ROWS = (((0,), (0,)), ((), ()))


def slot_rows(ids_ref, experts, pitch):
    top, count = ids_ref.shape
    earlier = (
        lax.broadcasted_iota(jnp.int32, (count, count), 0)
        < lax.broadcasted_iota(jnp.int32, (count, count), 1)
    ).astype(F32).astype(BF16)
    names = lax.broadcasted_iota(jnp.int32, (experts, count), 0)
    seen = jnp.zeros((experts, 1), F32)
    slots = []
    for k in range(top):
        row = ids_ref[k : k + 1, :]
        hit = (names == row).astype(F32)
        before = jnp.dot(hit.astype(BF16), earlier, preferred_element_type=F32)
        rank = jnp.sum(hit * (before + seen), axis=0, keepdims=True)
        seen = seen + jnp.sum(hit, axis=1, keepdims=True)
        slots.append(row * pitch + rank.astype(jnp.int32))
    return slots


def dispatch_kernel(experts, pitch, col_ref, ids_ref, tok_ref, out_ref):
    slots = slot_rows(ids_ref, experts, pitch)
    count = ids_ref.shape[1]
    here = lax.broadcasted_iota(jnp.int32, (experts * pitch, count), 0)
    pick = functools.reduce(jnp.logical_or, [here == s for s in slots])
    pick = pick.astype(F32).astype(BF16)
    out_ref[...] = jnp.dot(pick, tok_ref[...], preferred_element_type=F32).astype(BF16)


def expert_kernel(in_ref, w_hbm, tw_hbm, out_ref, w_ref, tw_ref, hid_ref, w_sem, tw_sem):
    n, _, depth = in_ref.shape
    towers, _, tile = tw_ref.shape
    tiles = w_ref.shape[0]
    per = towers // n

    def w_copy(c):
        cols = pl.ds(pl.multiple_of(c * tile, tile), tile)
        return pltpu.make_async_copy(w_hbm.at[0, :, cols], w_ref.at[c], w_sem.at[c])

    def tw_copy(t):
        return pltpu.make_async_copy(tw_hbm.at[t], tw_ref.at[t], tw_sem.at[t])

    for c in range(tiles):
        w_copy(c).start()
    for t in range(towers):
        tw_copy(t).start()

    @pl.loop(0, tiles)
    def _(c):
        w_copy(c).wait()
        total = None
        for j in range(n):
            part = jnp.dot(
                in_ref[j], w_ref[c, j * depth : (j + 1) * depth, :], preferred_element_type=F32
            )
            total = part if total is None else total + part
        cols = pl.ds(pl.multiple_of(c * tile, tile), tile)
        hid_ref[:, cols] = (total / (1.0 + jnp.exp(-total))).astype(BF16)

    for t in range(towers):
        tw_copy(t).wait()
        out_ref[t // per, :, (t % per) * tile : (t % per + 1) * tile] = jnp.dot(
            hid_ref[...], tw_ref[t], preferred_element_type=F32
        ).astype(BF16)


def combine_kernel(experts, pitch, ids_ref, lev_ref, back_ref, out_ref):
    slots = slot_rows(ids_ref, experts, pitch)
    levels = lev_ref[...].astype(F32)
    gates = levels / jnp.sum(levels, axis=0, keepdims=True)
    here = lax.broadcasted_iota(jnp.int32, (experts * pitch, ids_ref.shape[1]), 0)
    share = sum(jnp.where(here == s, gates[k : k + 1, :], 0.0) for k, s in enumerate(slots))
    high = share.astype(BF16)
    low = (share - high.astype(F32)).astype(BF16)
    rows = back_ref[...]
    z = lax.dot_general(high, rows, ROWS, preferred_element_type=F32)
    z = z + lax.dot_general(low, rows, ROWS, preferred_element_type=F32)
    out_ref[...] = z.astype(BF16)


def from_tower(side_ref, me, t):
    return side_ref[pl.ds(jnp.bitwise_xor(me, t), 1), pl.ds(me, 1), :].reshape(1, -1)


def predict_kernel(towers, me_ref, side_ref, z_ref, pred_ref):
    me = me_ref[0]
    n, count, cols = z_ref.shape
    per = towers // n
    tile = cols // per
    for t in range(towers):
        z = z_ref[t // per, :, (t % per) * tile : (t % per + 1) * tile].astype(F32)
        out_vec = from_tower(side_ref, me, t)[:, -tile:]
        pred_ref[t : t + 1, :] = lax.dot_general(
            out_vec,
            z / (1.0 + jnp.exp(-z)),
            LANES,
            precision=lax.Precision.HIGHEST,
            preferred_element_type=F32,
        )


def gradient_kernel(me_ref, side_ref, z_ref, tw_hbm, grad_ref, tw_ref, acc_ref, tw_sem):
    me = me_ref[0]
    n, count, cols = z_ref.shape
    towers, _, tile = tw_ref.shape
    per = towers // n
    copies = [pltpu.make_async_copy(tw_hbm.at[t], tw_ref.at[t], tw_sem.at[t]) for t in range(towers)]
    for copy in copies:
        copy.start()
    sides = [from_tower(side_ref, me, t) for t in range(towers)]
    cot = jnp.transpose(jnp.concatenate([v[:, :-tile] for v in sides], axis=0))[:count]
    for t in range(towers):
        z = z_ref[t // per, :, (t % per) * tile : (t % per + 1) * tile].astype(F32)
        sig = 1.0 / (1.0 + jnp.exp(-z))
        dz = cot[:, t : t + 1] * sides[t][:, -tile:] * sig * (1.0 + z * (1.0 - sig))
        copies[t].wait()
        part = lax.dot_general(dz.astype(BF16), tw_ref[t], LANES, preferred_element_type=F32)
        if t == 0:
            acc_ref[...] = part
        elif t < towers - 1:
            acc_ref[...] += part
        else:
            grad_ref[...] = (acc_ref[...] + part).astype(BF16)


def body(tokens, expert_ids, gate_levels, expert_weight, tower_weight, tower_out, cotangent):
    experts = lax.axis_size("dp")
    tasks = lax.axis_size("task")
    n = lax.axis_size("mp")
    count, top = expert_ids.shape
    width = tokens.shape[1]
    part = width // n
    towers, units, tile = tower_weight.shape
    cols = towers * tile // n
    cap = max(2, 5 * count * top // (4 * experts))
    pitch = -(-cap // 8) * 8
    rows = experts * pitch
    me = lax.axis_index("mp").astype(jnp.int32).reshape(1)
    ids = expert_ids.T
    levels = gate_levels.T

    side = jnp.concatenate(
        [
            jnp.pad(cotangent.reshape(tasks, count), ((0, 0), (0, 256 - count))),
            jnp.broadcast_to(tower_out, (tasks, tile)),
        ],
        axis=1,
    )
    side = side[None]
    for bit in (1, 2, 4):
        other = lax.ppermute(side, "task", [(i, i ^ bit) for i in range(tasks)])
        side = jnp.concatenate([side, other], axis=0)

    out = pl.pallas_call(
        functools.partial(dispatch_kernel, experts, pitch),
        out_shape=jax.ShapeDtypeStruct((rows, part), BF16),
        grid_spec=pltpu.PrefetchScalarGridSpec(
            num_scalar_prefetch=1,
            grid=(1,),
            in_specs=[
                pl.BlockSpec((top, count), lambda g, m: (0, 0)),
                pl.BlockSpec((count, part), lambda g, m: (0, m[0])),
            ],
            out_specs=pl.BlockSpec((rows, part), lambda g, m: (0, 0)),
        ),
        name="dispatch",
    )(me, ids, tokens)

    def over_dp(a):
        a = a.reshape(experts, pitch, a.shape[1])
        return lax.all_to_all(a, "dp", split_axis=0, concat_axis=0, tiled=True).reshape(rows, -1)

    def over_mp(a):
        return lax.all_to_all(a, "mp", split_axis=0, concat_axis=0, tiled=True)

    def spread(a):
        return over_mp(jnp.broadcast_to(a[None], (n,) + a.shape))

    outs = pl.pallas_call(
        expert_kernel,
        out_shape=jax.ShapeDtypeStruct((n, rows, cols), BF16),
        in_specs=[VMEM, HBM, HBM],
        out_specs=VMEM,
        scratch_shapes=[
            pltpu.VMEM((units // tile, width, tile), BF16),
            pltpu.VMEM((towers, units, tile), BF16),
            pltpu.VMEM((rows, units), BF16),
            pltpu.SemaphoreType.DMA((units // tile,)),
            pltpu.SemaphoreType.DMA((towers,)),
        ],
        compiler_params=pltpu.CompilerParams(vmem_limit_bytes=50 << 20),
        cost_estimate=pl.CostEstimate(
            flops=2 * rows * units * (width + towers * tile),
            bytes_accessed=2 * units * (width + towers * tile),
            transcendentals=rows * units,
        ),
        name="expert",
    )(spread(over_dp(out)), expert_weight, tower_weight)
    total = jnp.sum(over_mp(outs).astype(F32), axis=0)
    back, side = lax.optimization_barrier((over_dp(total.astype(BF16)), side))

    z = pl.pallas_call(
        functools.partial(combine_kernel, experts, pitch),
        out_shape=jax.ShapeDtypeStruct((count, cols), BF16),
        in_specs=[VMEM] * 3,
        out_specs=VMEM,
        compiler_params=pltpu.CompilerParams(vmem_limit_bytes=16 << 20),
        name="combine",
    )(ids, levels, back)
    zs = spread(z)

    task = lax.axis_index("task").astype(jnp.int32).reshape(1)
    pred = pl.pallas_call(
        functools.partial(predict_kernel, towers),
        out_shape=jax.ShapeDtypeStruct((towers, count), F32),
        in_specs=[SMEM, VMEM, VMEM],
        out_specs=VMEM,
        compiler_params=pltpu.CompilerParams(vmem_limit_bytes=16 << 20),
        name="predict",
    )(task, side, zs)
    grad = pl.pallas_call(
        gradient_kernel,
        out_shape=jax.ShapeDtypeStruct((count, units), BF16),
        in_specs=[SMEM, VMEM, VMEM, HBM],
        out_specs=VMEM,
        scratch_shapes=[
            pltpu.VMEM((towers, units, tile), BF16),
            pltpu.VMEM((count, units), F32),
            pltpu.SemaphoreType.DMA((towers,)),
        ],
        compiler_params=pltpu.CompilerParams(vmem_limit_bytes=54 << 20),
        cost_estimate=pl.CostEstimate(
            flops=2 * count * units * towers * tile,
            bytes_accessed=2 * units * towers * tile,
            transcendentals=count * towers * tile,
        ),
        name="gradient",
    )(task, side, zs, tower_weight)
    pred = lax.all_to_all(pred, "task", split_axis=0, concat_axis=0, tiled=True)
    return pred.reshape(1, tasks * count), grad


def solution(mesh):
    return jax.shard_map(
        body,
        mesh=mesh,
        in_specs=(
            P(("dp", "task"), None),
            P(("dp", "task"), None),
            P(("dp", "task"), None),
            P("dp", None, "mp"),
            P(None, "mp", None),
            P("task", None),
            P("task", "dp"),
        ),
        out_specs=(P("task", "dp"), P(("dp", "task"), "mp")),
        check_vma=False,
    )
```

time: 277 us -> 262 us (0.946)
  waiting for transfers between devices: 102 us -> 53.2 us
  blocking collectives: 112 us -> 148 us
  Pallas kernels: 13.5 us -> 21.3 us
  local copies, waits for them, and re-layouts: 9.06 us -> 2.51 us
    all_to_all x2, blocking collectives: 18.8 us -> 54.3 us  [over_mp(): return lax.all_to_all(a, 'mp', split_axis=0, concat_axis=0, tiled=True)]
    ppermute x9 -> x3, waiting for transfers between devices: 38.2 us -> 4.55 us  [body(): other = lax.ppermute(side, 'task', [(i, i ^ bit) for i in range(tasks)])]
    all_to_all x1, waiting for transfers between devices: 64.3 us -> 40.4 us  [over_dp(): lax.all_to_all(a, 'dp', split_axis=0, concat_axis=0, tiled=True)]
    ppermute x9 -> x3, starting transfers between devices: 33.2 us -> 13.3 us  [body(): other = lax.ppermute(side, 'task', [(i, i ^ bit) for i in range(tasks)])]
    all_to_all x0 -> x2, starting transfers between devices: none -> 16.5 us  [the longest x1 13 us: body(): pred = lax.all_to_all(pred, 'task', split_axis=0, concat_axis=0, tiled=True)]
    pallas_call x2 -> x3, Pallas kernels: 8.91 us -> 18.5 us  [the longest x1 12 us: body(): pl.pallas_call(expert_kernel, out_shape=jax.ShapeDtypeStruct((n, rows, co...]
    all_to_all x0 -> x2, waiting for transfers between devices: none -> 8.3 us  [the longest x1 8.3 us: over_mp(): return lax.all_to_all(a, 'mp', split_axis=0, concat_axis=0, tiled=True)]
    unnamed x15 -> x12, local copies, waits for them, and re-layouts: 8.28 us -> 0.02 us
  transfers between devices with their start and end apart: 10 -> 6, of which waited for: 7 -> 5; matrix products, arithmetic and copies ran while one was open for 0% -> 0% of each run, Pallas kernels for 0% -> 2%
where the time goes in v2:
time: 262 us
  blocking collectives  148 us (56%)
  waiting for transfers between devices  53.2 us (20%)
  starting transfers between devices  34.7 us (13%)
  Pallas kernels  21.3 us (8%)
    all_to_all x1, blocking collectives, over_dp(): lax.all_to_all(a, 'dp', split_axis=0, concat_axis=0, tiled=True)  93.6 us
    all_to_all x2, blocking collectives, over_mp(): return lax.all_to_all(a, 'mp', split_axis=0, concat_axis=0, tiled=True)  54.3 us
    all_to_all x1, waiting for transfers between devices, over_dp(): lax.all_to_all(a, 'dp', split_axis=0, concat_axis=0, tiled=True)  40.4 us
    ppermute x3, starting transfers between devices, body(): other = lax.ppermute(side, 'task', [(i, i ^ bit) for i in range(tasks)])  13.3 us
    all_to_all x1, starting transfers between devices, body(): pred = lax.all_to_all(pred, 'task', split_axis=0, concat_axis=0, tiled=True)  13 us
    pallas_call x1, Pallas kernels, body(): pl.pallas_call(expert_kernel, out_shape=jax.ShapeDtypeStruct((n, rows, co...  12 us
    all_to_all x1, waiting for transfers between devices, over_mp(): return lax.all_to_all(a, 'mp', split_axis=0, concat_axis=0, tiled=True)  8.3 us
  transfers between devices with their start and end apart: 6, of which 5 were waited for; matrix products, arithmetic and copies ran while one was open for 0% of the time, Pallas kernels for 2%

profile of v2, /device:TPU:1, one launch (start us, length us, event | category | flops | bytes accessed | tf_op | source)
XLA Modules:
  0.0 261.6 jit_solution(480797201663528835)
XLA Ops:
  0.6 2.2 dispatch.1
  2.8 93.6 %all_to_all.34 = bf16[32,16,512]{2,1,0:T(8,128)(2,1)S(1)} all-to-all(bf16[32,16,512]{2,1,0:T(8,128)(2,1)} %bitcast.18), channel_id=1, replica_groups=mesh['dp'=32,'task'=8,'mp'=4] {'dp'}, dimensions={0} | all-to-all | bytes 1048576 | tf_op jit(solution)/shard_map/all_to_all | solution.py:188
  96.4 0.2 broadcast_in_dim.24
  96.5 28.5 %all_to_all.35.in_ref = bf16[4,512,512]{2,1,0:T(8,128)(2,1)} all-to-all(bf16[4,512,512]{2,1,0:T(8,128)(2,1)S(1)} %broadcast_in_dim.24), channel_id=1, replica_groups=mesh['dp'=32,'task'=8,'mp'=4] {'mp'}, dimensions={0} | all-to-all | bytes 4194304 | tf_op jit(solution)/shard_map/all_to_all | solution.py:191
  125.0 12.0 %expert.1 = bf16[4,512,512]{2,1,0:T(8,128)(2,1)S(1)} custom-call(bf16[4,512,512]{2,1,0:T(8,128)(2,1)} %all_to_all.35.in_ref, bf16[1,2048,1024]{2,1,0:T(8,128)(2,1)} %w_hbm.1, bf16[8,1024,256]{2,1,0:T(8,128)(2,1)} %tw_hbm.3), custom_call_target="tpu_custom_call" | custom-call | flops 4294967296 | bytes 8388608 | tf_op jit(solution)/shard_map/expert/pallas_call | solution.py:196
  137.1 25.8 %all_to_all.36 = bf16[4,512,512]{2,1,0:T(8,128)(2,1)S(1)} all-to-all(bf16[4,512,512]{2,1,0:T(8,128)(2,1)S(1)} %expert.1), channel_id=1, replica_groups=mesh['dp'=32,'task'=8,'mp'=4] {'mp'}, dimensions={0} | all-to-all | bytes 4194304 | tf_op jit(solution)/shard_map/all_to_all | solution.py:191
  162.9 0.0 copy-start.4
  162.9 0.0 copy-start.5
  162.9 0.0 copy-start.2
  162.9 0.0 copy-start.3
  162.9 1.2 reduce_sum.12
  164.1 4.8 %all-to-all-start.3 = ((bf16[32,16,512]{2,1,0:T(8,128)(2,1)}), bf16[32,16,512]{2,1,0:T(8,128)(2,1)S(1)}, u32[]{:S(2)}, u32[]{:S(2)}) async-start(bf16[32,16,512]{2,1,0:T(8,128)(2,1)} %bitcast.5), calls=%async_computation.3 | async-start | bytes 1048576 | tf_op jit(solution)/shard_map/all_to_all | solution.py:188
  169.0 0.0 copy-done.4
  169.0 0.1 reshape.35
  169.1 0.0 copy-done.5
  169.1 5.3 %collective-permute-start = (f32[1,8,512]{2,1,0:T(8,128)S(1)}, f32[1,8,512]{2,1,0:T(8,128)S(1)}, u32[]{:S(2)}, u32[]{:S(2)}) collective-permute-start(f32[1,8,512]{2,1,0:T(8,128)S(1)} %fusion), channel_id=1, source_target_pairs={{0,4},{4,0},{8,12},{12,8},{16,20},{20,16},{24,28},{28,24},{1,5},{5... | collective-permute-start | bytes 49160 | tf_op jit(solution)/shard_map/ppermute | solution.py:168
  174.5 0.8 collective-permute-done
  175.3 3.2 %collective-permute-start.1 = (f32[2,8,512]{2,1,0:T(8,128)S(1)}, f32[2,8,512]{2,1,0:T(8,128)S(1)}, u32[]{:S(2)}, u32[]{:S(2)}) collective-permute-start(f32[2,8,512]{2,1,0:T(8,128)S(1)} %pad_maximum_fusion.2), channel_id=1, source_target_pairs={{0,8},{4,12},{8,0},{12,4},{16,24},{20,28},{24,16},{28,20},{1,9},{5... | collective-permute-start | bytes 98312 | tf_op jit(solution)/shard_map/ppermute | solution.py:168
  178.5 1.7 collective-permute-done.1
  180.2 4.8 %collective-permute-start.2 = (f32[4,8,512]{2,1,0:T(8,128)S(1)}, f32[4,8,512]{2,1,0:T(8,128)S(1)}, u32[]{:S(2)}, u32[]{:S(2)}) collective-permute-start(f32[4,8,512]{2,1,0:T(8,128)S(1)} %pad_maximum_fusion.1), channel_id=1, source_target_pairs={{0,16},{4,20},{8,24},{12,28},{16,0},{20,4},{24,8},{28,12},{1,17},{... | collective-permute-start | bytes 196616 | tf_op jit(solution)/shard_map/ppermute | solution.py:168
  185.0 2.0 collective-permute-done.2
  187.0 0.0 copy-start.1
  187.0 40.4 %all-to-all-done.3 = bf16[32,16,512]{2,1,0:T(8,128)(2,1)S(1)} async-done(((bf16[32,16,512]{2,1,0:T(8,128)(2,1)}), bf16[32,16,512]{2,1,0:T(8,128)(2,1)S(1)}, u32[]{:S(2)}, u32[]{:S(2)}) %all-to-all-start.3) | async-done | bytes 524320 | tf_op jit(solution)/shard_map/all_to_all | solution.py:188
  227.4 0.0 copy-done.2
  227.4 0.0 copy-done.3
  227.4 0.6 combine.1
  228.1 1.0 broadcast_in_dim.28
  229.0 3.5 %all-to-all-start.4 = ((bf16[4,192,512]{2,1,0:T(8,128)(2,1)}), bf16[4,192,512]{2,1,0:T(8,128)(2,1)S(1)}, u32[]{:S(2)}, u32[]{:S(2)}) async-start(bf16[4,192,512]{2,1,0:T(8,128)(2,1)} %broadcast_in_dim.28), calls=%async_computation.4 | async-start | bytes 1572864 | tf_op jit(solution)/shard_map/all_to_all | solution.py:191
  232.5 8.3 %all-to-all-done.4.z_ref = bf16[4,192,512]{2,1,0:T(8,128)(2,1)S(1)} async-done(((bf16[4,192,512]{2,1,0:T(8,128)(2,1)}), bf16[4,192,512]{2,1,0:T(8,128)(2,1)S(1)}, u32[]{:S(2)}, u32[]{:S(2)}) %all-to-all-start.4) | async-done | bytes 786464 | tf_op jit(solution)/shard_map/all_to_all | solution.py:191
  240.8 0.0 copy-start
  240.8 1.5 predict.1
  242.3 0.0 copy-done.1
  242.3 0.6 copy.9
  242.9 13.0 %all-to-all-start.5 = ((f32[8,1,192]{2,1,0:T(1,128)}), f32[8,1,192]{2,1,0:T(1,128)S(1)}, u32[]{:S(2)}, u32[]{:S(2)}) async-start(f32[8,1,192]{2,1,0:T(1,128)} %copy.9), calls=%async_computation.5 | async-start | bytes 16384 | tf_op jit(solution)/shard_map/all_to_all | solution.py:256
  255.9 0.0 copy-done
  255.9 5.0 %gradient.1 = bf16[192,1024]{1,0:T(8,128)(2,1)} custom-call(s32[1]{0:T(128)} %bitcast.me_ref, f32[8,8,512]{2,1,0:T(8,128)} %copy-done.1, bf16[4,192,512]{2,1,0:T(8,128)(2,1)} %copy-done, bf16[8,1024,256]{2,1,0:T(8,128)(2,1)} %tw_hbm.3), custom_call_target="tpu_custom_call" | custom-call | flops 805306368 | bytes 4194304 | tf_op jit(solution)/shard_map/gradient/pallas_call | solution.py:238
  260.9 0.0 all-to-all-done.5
  261.0 0.7 reshape.36
  (7 shorter events, 0.1 us)
Async XLA Ops:
  162.9 6.1 %copy-start.4 = (f32[1,1536]{1,0:T(1,128)S(1)}, f32[1,1536]{1,0:T(1,128)}, u32[]{:S(2)}) copy-start(f32[1,1536]{1,0:T(1,128)} %param.13) | copy-start | bytes 18436
  162.9 6.2 %copy-start.5 = (f32[1,256]{1,0:T(1,128)S(1)}, f32[1,256]{1,0:T(1,128)}, u32[]{:S(2)}) copy-start(f32[1,256]{1,0:T(1,128)} %param.12) | copy-start | bytes 3076
  162.9 64.5 %copy-start.2 = (s32[192,2]{0,1:T(2,128)S(1)}, s32[192,2]{0,1:T(2,128)}, u32[]{:S(2)}) copy-start(s32[192,2]{0,1:T(2,128)} %param.8) | copy-start | bytes 4612
  162.9 64.5 %copy-start.3 = (s32[192,2]{0,1:T(2,128)S(1)}, s32[192,2]{0,1:T(2,128)}, u32[]{:S(2)}) copy-start(s32[192,2]{0,1:T(2,128)} %param.9) | copy-start | bytes 4612
  164.1 63.3 %all-to-all-start.3 = ((bf16[32,16,512]{2,1,0:T(8,128)(2,1)}), bf16[32,16,512]{2,1,0:T(8,128)(2,1)S(1)}, u32[]{:S(2)}, u32[]{:S(2)}) async-start(bf16[32,16,512]{2,1,0:T(8,128)(2,1)} %bitcast.5), calls=%async_computation.3 | async-start | bytes 1048576 | tf_op jit(solution)/shard_map/all_to_all | solution.py:188
  169.1 6.2 %collective-permute-start = (f32[1,8,512]{2,1,0:T(8,128)S(1)}, f32[1,8,512]{2,1,0:T(8,128)S(1)}, u32[]{:S(2)}, u32[]{:S(2)}) collective-permute-start(f32[1,8,512]{2,1,0:T(8,128)S(1)} %fusion), channel_id=1, source_target_pairs={{0,4},{4,0},{8,12},{12,8},{16,20},{20,16},{24,28},{28,24},{1,5},{5... | collective-permute-start | bytes 49160 | tf_op jit(solution)/shard_map/ppermute | solution.py:168
  175.3 4.9 %collective-permute-start.1 = (f32[2,8,512]{2,1,0:T(8,128)S(1)}, f32[2,8,512]{2,1,0:T(8,128)S(1)}, u32[]{:S(2)}, u32[]{:S(2)}) collective-permute-start(f32[2,8,512]{2,1,0:T(8,128)S(1)} %pad_maximum_fusion.2), channel_id=1, source_target_pairs={{0,8},{4,12},{8,0},{12,4},{16,24},{20,28},{24,16},{28,20},{1,9},{5... | collective-permute-start | bytes 98312 | tf_op jit(solution)/shard_map/ppermute | solution.py:168
  180.2 6.8 %collective-permute-start.2 = (f32[4,8,512]{2,1,0:T(8,128)S(1)}, f32[4,8,512]{2,1,0:T(8,128)S(1)}, u32[]{:S(2)}, u32[]{:S(2)}) collective-permute-start(f32[4,8,512]{2,1,0:T(8,128)S(1)} %pad_maximum_fusion.1), channel_id=1, source_target_pairs={{0,16},{4,20},{8,24},{12,28},{16,0},{20,4},{24,8},{28,12},{1,17},{... | collective-permute-start | bytes 196616 | tf_op jit(solution)/shard_map/ppermute | solution.py:168
  187.0 55.2 %copy-start.1 = (f32[8,8,512]{2,1,0:T(8,128)}, f32[8,8,512]{2,1,0:T(8,128)S(1)}, u32[]{:S(2)}) copy-start(f32[8,8,512]{2,1,0:T(8,128)S(1)} %pad_maximum_fusion.side_ref) | copy-start | bytes 393220
  229.0 11.8 %all-to-all-start.4 = ((bf16[4,192,512]{2,1,0:T(8,128)(2,1)}), bf16[4,192,512]{2,1,0:T(8,128)(2,1)S(1)}, u32[]{:S(2)}, u32[]{:S(2)}) async-start(bf16[4,192,512]{2,1,0:T(8,128)(2,1)} %broadcast_in_dim.28), calls=%async_computation.4 | async-start | bytes 1572864 | tf_op jit(solution)/shard_map/all_to_all | solution.py:191
  240.8 15.1 %copy-start = (bf16[4,192,512]{2,1,0:T(8,128)(2,1)}, bf16[4,192,512]{2,1,0:T(8,128)(2,1)S(1)}, u32[]{:S(2)}) copy-start(bf16[4,192,512]{2,1,0:T(8,128)(2,1)S(1)} %all-to-all-done.4.z_ref) | copy-start | bytes 2359300
  242.9 18.0 %all-to-all-start.5 = ((f32[8,1,192]{2,1,0:T(1,128)}), f32[8,1,192]{2,1,0:T(1,128)S(1)}, u32[]{:S(2)}, u32[]{:S(2)}) async-start(f32[8,1,192]{2,1,0:T(1,128)} %copy.9), calls=%async_computation.5 | async-start | bytes 16384 | tf_op jit(solution)/shard_map/all_to_all | solution.py:256

commit v3 on v2

--- a/solution.py
+++ b/solution.py
@@ -44,38 +44,39 @@
     out_ref[...] = jnp.dot(pick, tok_ref[...], preferred_element_type=F32).astype(BF16)
 
 
-def expert_kernel(in_ref, w_hbm, tw_hbm, out_ref, w_ref, tw_ref, hid_ref, w_sem, tw_sem):
+def expert_kernel(in_hbm, w_hbm, tw_hbm, out_ref, in_ref, w_ref, tw_ref, acc_ref, hid_ref, in_sem, w_sem, tw_sem):
     n, _, depth = in_ref.shape
     towers, _, tile = tw_ref.shape
-    tiles = w_ref.shape[0]
     per = towers // n
-
-    def w_copy(c):
-        cols = pl.ds(pl.multiple_of(c * tile, tile), tile)
-        return pltpu.make_async_copy(w_hbm.at[0, :, cols], w_ref.at[c], w_sem.at[c])
-
-    def tw_copy(t):
-        return pltpu.make_async_copy(tw_hbm.at[t], tw_ref.at[t], tw_sem.at[t])
-
-    for c in range(tiles):
-        w_copy(c).start()
+    in_copies = [pltpu.make_async_copy(in_hbm.at[j], in_ref.at[j], in_sem.at[j]) for j in range(n)]
+    w_copies = [
+        pltpu.make_async_copy(w_hbm.at[0, pl.ds(j * depth, depth)], w_ref.at[j], w_sem.at[j])
+        for j in range(n)
+    ]
+    tw_copies = [pltpu.make_async_copy(tw_hbm.at[t], tw_ref.at[t], tw_sem.at[t]) for t in range(towers)]
+    for j in range(n):
+        in_copies[j].start()
+        w_copies[j].start()
+    for copy in tw_copies:
+        copy.start()
+
+    for j in range(n):
+        in_copies[j].wait()
+        w_copies[j].wait()
+
+        @pl.loop(0, w_ref.shape[2] // tile)
+        def _(c):
+            cols = pl.ds(pl.multiple_of(c * tile, tile), tile)
+            total = jnp.dot(in_ref[j], w_ref[j, :, cols], preferred_element_type=F32)
+            if j > 0:
+                total = total + acc_ref[:, cols]
+            if j < n - 1:
+                acc_ref[:, cols] = total
+            else:
+                hid_ref[:, cols] = (total / (1.0 + jnp.exp(-total))).astype(BF16)
+
     for t in range(towers):
-        tw_copy(t).start()
-
-    @pl.loop(0, tiles)
-    def _(c):
-        w_copy(c).wait()
-        total = None
-        for j in range(n):
-            part = jnp.dot(
-                in_ref[j], w_ref[c, j * depth : (j + 1) * depth, :], preferred_element_type=F32
-            )
-            total = part if total is None else total + part
-        cols = pl.ds(pl.multiple_of(c * tile, tile), tile)
-        hid_ref[:, cols] = (total / (1.0 + jnp.exp(-total))).astype(BF16)
-
-    for t in range(towers):
-        tw_copy(t).wait()
+        tw_copies[t].wait()
         out_ref[t // per, :, (t % per) * tile : (t % per + 1) * tile] = jnp.dot(
             hid_ref[...], tw_ref[t], preferred_element_type=F32
         ).astype(BF16)
@@ -92,7 +93,8 @@
     rows = back_ref[...]
     z = lax.dot_general(high, rows, ROWS, preferred_element_type=F32)
     z = z + lax.dot_general(low, rows, ROWS, preferred_element_type=F32)
-    out_ref[...] = z.astype(BF16)
+    for j in range(out_ref.shape[0]):
+        out_ref[j] = z.astype(BF16)
 
 
 def from_tower(side_ref, me, t):
@@ -107,7 +109,7 @@
     for t in range(towers):
         z = z_ref[t // per, :, (t % per) * tile : (t % per + 1) * tile].astype(F32)
         out_vec = from_tower(side_ref, me, t)[:, -tile:]
-        pred_ref[t : t + 1, :] = lax.dot_general(
+        pred_ref[t] = lax.dot_general(
             out_vec,
             z / (1.0 + jnp.exp(-z)),
             LANES,
@@ -196,13 +198,16 @@
     outs = pl.pallas_call(
         expert_kernel,
         out_shape=jax.ShapeDtypeStruct((n, rows, cols), BF16),
-        in_specs=[VMEM, HBM, HBM],
+        in_specs=[HBM] * 3,
         out_specs=VMEM,
         scratch_shapes=[
-            pltpu.VMEM((units // tile, width, tile), BF16),
+            pltpu.VMEM((n, rows, part), BF16),
+            pltpu.VMEM((n, part, units), BF16),
             pltpu.VMEM((towers, units, tile), BF16),
+            pltpu.VMEM((rows, units), F32),
             pltpu.VMEM((rows, units), BF16),
-            pltpu.SemaphoreType.DMA((units // tile,)),
+            pltpu.SemaphoreType.DMA((n,)),
+            pltpu.SemaphoreType.DMA((n,)),
             pltpu.SemaphoreType.DMA((towers,)),
         ],
         compiler_params=pltpu.CompilerParams(vmem_limit_bytes=50 << 20),
@@ -218,18 +223,18 @@
 
     z = pl.pallas_call(
         functools.partial(combine_kernel, experts, pitch),
-        out_shape=jax.ShapeDtypeStruct((count, cols), BF16),
+        out_shape=jax.ShapeDtypeStruct((n, count, cols), BF16),
         in_specs=[VMEM] * 3,
         out_specs=VMEM,
         compiler_params=pltpu.CompilerParams(vmem_limit_bytes=16 << 20),
         name="combine",
     )(ids, levels, back)
-    zs = spread(z)
+    zs = over_mp(z)
 
     task = lax.axis_index("task").astype(jnp.int32).reshape(1)
     pred = pl.pallas_call(
         functools.partial(predict_kernel, towers),
-        out_shape=jax.ShapeDtypeStruct((towers, count), F32),
+        out_shape=jax.ShapeDtypeStruct((towers, 1, count), F32),
         in_specs=[SMEM, VMEM, VMEM],
         out_specs=VMEM,
         compiler_params=pltpu.CompilerParams(vmem_limit_bytes=16 << 20),

time: 262 us -> 263 us (level)
  no operation moved by 1% of the time
where the time goes in v3:
time: 263 us; the launch traced here: 262 us
  blocking collectives  148 us (56%)
  waiting for transfers between devices  53.2 us (20%)
  starting transfers between devices  34.7 us (13%)
  Pallas kernels  23.5 us (9%)
    all_to_all x1, blocking collectives, over_dp(): lax.all_to_all(a, 'dp', split_axis=0, concat_axis=0, tiled=True)  93.6 us
    all_to_all x2, blocking collectives, over_mp(): return lax.all_to_all(a, 'mp', split_axis=0, concat_axis=0, tiled=True)  54.3 us
    all_to_all x1, waiting for transfers between devices, over_dp(): lax.all_to_all(a, 'dp', split_axis=0, concat_axis=0, tiled=True)  40.4 us
    ppermute x3, starting transfers between devices, body(): other = lax.ppermute(side, 'task', [(i, i ^ bit) for i in range(tasks)])  13.3 us
    all_to_all x1, starting transfers between devices, body(): pred = lax.all_to_all(pred, 'task', split_axis=0, concat_axis=0, tiled=True)  13 us
    pallas_call x1, Pallas kernels, body(): pl.pallas_call(expert_kernel, out_shape=jax.ShapeDtypeStruct((n, rows, co...  12.7 us
    all_to_all x1, waiting for transfers between devices, over_mp(): return lax.all_to_all(a, 'mp', split_axis=0, concat_axis=0, tiled=True)  8.3 us
  transfers between devices with their start and end apart: 6, of which 5 were waited for; matrix products, arithmetic and copies ran while one was open for 0% of the time, Pallas kernels for 2%

profile of v3, /device:TPU:1, one launch (start us, length us, event | category | flops | bytes accessed | tf_op | source)
XLA Modules:
  0.0 262.3 jit_solution(4680111694918609363)
XLA Ops:
  0.6 2.2 dispatch.1
  2.8 93.6 %all_to_all.30 = bf16[32,16,512]{2,1,0:T(8,128)(2,1)S(1)} all-to-all(bf16[32,16,512]{2,1,0:T(8,128)(2,1)} %bitcast.16), channel_id=1, replica_groups=mesh['dp'=32,'task'=8,'mp'=4] {'dp'}, dimensions={0} | all-to-all | bytes 1048576 | tf_op jit(solution)/shard_map/all_to_all | solution.py:190
  96.4 0.2 broadcast_in_dim.18
  96.5 28.5 %all_to_all.31.in_hbm = bf16[4,512,512]{2,1,0:T(8,128)(2,1)} all-to-all(bf16[4,512,512]{2,1,0:T(8,128)(2,1)S(1)} %broadcast_in_dim.18), channel_id=1, replica_groups=mesh['dp'=32,'task'=8,'mp'=4] {'mp'}, dimensions={0} | all-to-all | bytes 4194304 | tf_op jit(solution)/shard_map/all_to_all | solution.py:193
  125.0 12.7 %expert.1 = bf16[4,512,512]{2,1,0:T(8,128)(2,1)S(1)} custom-call(bf16[4,512,512]{2,1,0:T(8,128)(2,1)} %all_to_all.31.in_hbm, bf16[1,2048,1024]{2,1,0:T(8,128)(2,1)} %w_hbm.1, bf16[8,1024,256]{2,1,0:T(8,128)(2,1)} %tw_hbm.3), custom_call_target="tpu_custom_call" | custom-call | flops 4294967296 | bytes 8388608 | tf_op jit(solution)/shard_map/expert/pallas_call | solution.py:198
  137.8 25.8 %all_to_all.32 = bf16[4,512,512]{2,1,0:T(8,128)(2,1)S(1)} all-to-all(bf16[4,512,512]{2,1,0:T(8,128)(2,1)S(1)} %expert.1), channel_id=1, replica_groups=mesh['dp'=32,'task'=8,'mp'=4] {'mp'}, dimensions={0} | all-to-all | bytes 4194304 | tf_op jit(solution)/shard_map/all_to_all | solution.py:193
  163.6 0.0 copy-start.4
  163.6 0.0 copy-start.5
  163.6 0.0 copy-start.2
  163.6 0.0 copy-start.3
  163.6 1.2 reduce_sum.12
  164.8 4.9 %all-to-all-start.3 = ((bf16[32,16,512]{2,1,0:T(8,128)(2,1)}), bf16[32,16,512]{2,1,0:T(8,128)(2,1)S(1)}, u32[]{:S(2)}, u32[]{:S(2)}) async-start(bf16[32,16,512]{2,1,0:T(8,128)(2,1)} %bitcast.5), calls=%async_computation.3 | async-start | bytes 1048576 | tf_op jit(solution)/shard_map/all_to_all | solution.py:190
  169.7 0.0 copy-done.4
  169.7 0.1 reshape.31
  169.8 0.0 copy-done.5
  169.8 5.3 %collective-permute-start = (f32[1,8,512]{2,1,0:T(8,128)S(1)}, f32[1,8,512]{2,1,0:T(8,128)S(1)}, u32[]{:S(2)}, u32[]{:S(2)}) collective-permute-start(f32[1,8,512]{2,1,0:T(8,128)S(1)} %fusion), channel_id=1, source_target_pairs={{0,4},{4,0},{8,12},{12,8},{16,20},{20,16},{24,28},{28,24},{1,5},{5... | collective-permute-start | bytes 49160 | tf_op jit(solution)/shard_map/ppermute | solution.py:170
  175.2 0.8 collective-permute-done
  176.0 3.2 %collective-permute-start.1 = (f32[2,8,512]{2,1,0:T(8,128)S(1)}, f32[2,8,512]{2,1,0:T(8,128)S(1)}, u32[]{:S(2)}, u32[]{:S(2)}) collective-permute-start(f32[2,8,512]{2,1,0:T(8,128)S(1)} %pad_maximum_fusion.2), channel_id=1, source_target_pairs={{0,8},{4,12},{8,0},{12,4},{16,24},{20,28},{24,16},{28,20},{1,9},{5... | collective-permute-start | bytes 98312 | tf_op jit(solution)/shard_map/ppermute | solution.py:170
  179.2 1.7 collective-permute-done.1
  180.9 4.8 %collective-permute-start.2 = (f32[4,8,512]{2,1,0:T(8,128)S(1)}, f32[4,8,512]{2,1,0:T(8,128)S(1)}, u32[]{:S(2)}, u32[]{:S(2)}) collective-permute-start(f32[4,8,512]{2,1,0:T(8,128)S(1)} %pad_maximum_fusion.1), channel_id=1, source_target_pairs={{0,16},{4,20},{8,24},{12,28},{16,0},{20,4},{24,8},{28,12},{1,17},{... | collective-permute-start | bytes 196616 | tf_op jit(solution)/shard_map/ppermute | solution.py:170
  185.7 2.0 collective-permute-done.2
  187.7 0.0 copy-start.1
  187.8 40.4 %all-to-all-done.3 = bf16[32,16,512]{2,1,0:T(8,128)(2,1)S(1)} async-done(((bf16[32,16,512]{2,1,0:T(8,128)(2,1)}), bf16[32,16,512]{2,1,0:T(8,128)(2,1)S(1)}, u32[]{:S(2)}, u32[]{:S(2)}) %all-to-all-start.3) | async-done | bytes 524320 | tf_op jit(solution)/shard_map/all_to_all | solution.py:190
  228.1 0.0 copy-done.2
  228.1 0.0 copy-done.3
  228.1 1.5 combine.1
  229.7 3.5 %all-to-all-start.4 = ((bf16[4,192,512]{2,1,0:T(8,128)(2,1)}), bf16[4,192,512]{2,1,0:T(8,128)(2,1)S(1)}, u32[]{:S(2)}, u32[]{:S(2)}) async-start(bf16[4,192,512]{2,1,0:T(8,128)(2,1)} %combine.1), calls=%async_computation.4 | async-start | bytes 1572864 | tf_op jit(solution)/shard_map/all_to_all | solution.py:193
  233.2 8.3 %all-to-all-done.4.z_ref = bf16[4,192,512]{2,1,0:T(8,128)(2,1)S(1)} async-done(((bf16[4,192,512]{2,1,0:T(8,128)(2,1)}), bf16[4,192,512]{2,1,0:T(8,128)(2,1)S(1)}, u32[]{:S(2)}, u32[]{:S(2)}) %all-to-all-start.4) | async-done | bytes 786464 | tf_op jit(solution)/shard_map/all_to_all | solution.py:193
  241.5 0.0 copy-start
  241.5 2.1 predict.1
  243.5 13.0 %all-to-all-start.5 = ((f32[8,1,192]{2,1,0:T(1,128)}), f32[8,1,192]{2,1,0:T(1,128)S(1)}, u32[]{:S(2)}, u32[]{:S(2)}) async-start(f32[8,1,192]{2,1,0:T(1,128)} %predict.1), calls=%async_computation.5 | async-start | bytes 16384 | tf_op jit(solution)/shard_map/all_to_all | solution.py:261
  256.5 0.0 copy-done.1
  256.5 0.0 copy-done
  256.6 5.0 %gradient.1 = bf16[192,1024]{1,0:T(8,128)(2,1)} custom-call(s32[1]{0:T(128)} %bitcast.me_ref, f32[8,8,512]{2,1,0:T(8,128)} %copy-done.1, bf16[4,192,512]{2,1,0:T(8,128)(2,1)} %copy-done, bf16[8,1024,256]{2,1,0:T(8,128)(2,1)} %tw_hbm.3), custom_call_target="tpu_custom_call" | custom-call | flops 805306368 | bytes 4194304 | tf_op jit(solution)/shard_map/gradient/pallas_call | solution.py:243
  261.6 0.0 all-to-all-done.5
  261.6 0.7 reshape.32
  (7 shorter events, 0.1 us)
Async XLA Ops:
  163.6 6.1 %copy-start.4 = (f32[1,1536]{1,0:T(1,128)S(1)}, f32[1,1536]{1,0:T(1,128)}, u32[]{:S(2)}) copy-start(f32[1,1536]{1,0:T(1,128)} %param.13) | copy-start | bytes 18436
  163.6 6.2 %copy-start.5 = (f32[1,256]{1,0:T(1,128)S(1)}, f32[1,256]{1,0:T(1,128)}, u32[]{:S(2)}) copy-start(f32[1,256]{1,0:T(1,128)} %param.12) | copy-start | bytes 3076
  163.6 64.5 %copy-start.2 = (s32[192,2]{0,1:T(2,128)S(1)}, s32[192,2]{0,1:T(2,128)}, u32[]{:S(2)}) copy-start(s32[192,2]{0,1:T(2,128)} %param.8) | copy-start | bytes 4612
  163.6 64.5 %copy-start.3 = (s32[192,2]{0,1:T(2,128)S(1)}, s32[192,2]{0,1:T(2,128)}, u32[]{:S(2)}) copy-start(s32[192,2]{0,1:T(2,128)} %param.9) | copy-start | bytes 4612
  164.8 63.3 %all-to-all-start.3 = ((bf16[32,16,512]{2,1,0:T(8,128)(2,1)}), bf16[32,16,512]{2,1,0:T(8,128)(2,1)S(1)}, u32[]{:S(2)}, u32[]{:S(2)}) async-start(bf16[32,16,512]{2,1,0:T(8,128)(2,1)} %bitcast.5), calls=%async_computation.3 | async-start | bytes 1048576 | tf_op jit(solution)/shard_map/all_to_all | solution.py:190
  169.8 6.2 %collective-permute-start = (f32[1,8,512]{2,1,0:T(8,128)S(1)}, f32[1,8,512]{2,1,0:T(8,128)S(1)}, u32[]{:S(2)}, u32[]{:S(2)}) collective-permute-start(f32[1,8,512]{2,1,0:T(8,128)S(1)} %fusion), channel_id=1, source_target_pairs={{0,4},{4,0},{8,12},{12,8},{16,20},{20,16},{24,28},{28,24},{1,5},{5... | collective-permute-start | bytes 49160 | tf_op jit(solution)/shard_map/ppermute | solution.py:170
  176.0 4.9 %collective-permute-start.1 = (f32[2,8,512]{2,1,0:T(8,128)S(1)}, f32[2,8,512]{2,1,0:T(8,128)S(1)}, u32[]{:S(2)}, u32[]{:S(2)}) collective-permute-start(f32[2,8,512]{2,1,0:T(8,128)S(1)} %pad_maximum_fusion.2), channel_id=1, source_target_pairs={{0,8},{4,12},{8,0},{12,4},{16,24},{20,28},{24,16},{28,20},{1,9},{5... | collective-permute-start | bytes 98312 | tf_op jit(solution)/shard_map/ppermute | solution.py:170
  180.9 6.8 %collective-permute-start.2 = (f32[4,8,512]{2,1,0:T(8,128)S(1)}, f32[4,8,512]{2,1,0:T(8,128)S(1)}, u32[]{:S(2)}, u32[]{:S(2)}) collective-permute-start(f32[4,8,512]{2,1,0:T(8,128)S(1)} %pad_maximum_fusion.1), channel_id=1, source_target_pairs={{0,16},{4,20},{8,24},{12,28},{16,0},{20,4},{24,8},{28,12},{1,17},{... | collective-permute-start | bytes 196616 | tf_op jit(solution)/shard_map/ppermute | solution.py:170
  187.7 68.8 %copy-start.1 = (f32[8,8,512]{2,1,0:T(8,128)}, f32[8,8,512]{2,1,0:T(8,128)S(1)}, u32[]{:S(2)}) copy-start(f32[8,8,512]{2,1,0:T(8,128)S(1)} %pad_maximum_fusion.side_ref) | copy-start | bytes 393220
  229.7 11.8 %all-to-all-start.4 = ((bf16[4,192,512]{2,1,0:T(8,128)(2,1)}), bf16[4,192,512]{2,1,0:T(8,128)(2,1)S(1)}, u32[]{:S(2)}, u32[]{:S(2)}) async-start(bf16[4,192,512]{2,1,0:T(8,128)(2,1)} %combine.1), calls=%async_computation.4 | async-start | bytes 1572864 | tf_op jit(solution)/shard_map/all_to_all | solution.py:193
  241.5 15.1 %copy-start = (bf16[4,192,512]{2,1,0:T(8,128)(2,1)}, bf16[4,192,512]{2,1,0:T(8,128)(2,1)S(1)}, u32[]{:S(2)}) copy-start(bf16[4,192,512]{2,1,0:T(8,128)(2,1)S(1)} %all-to-all-done.4.z_ref) | copy-start | bytes 2359300
  243.5 18.0 %all-to-all-start.5 = ((f32[8,1,192]{2,1,0:T(1,128)}), f32[8,1,192]{2,1,0:T(1,128)S(1)}, u32[]{:S(2)}, u32[]{:S(2)}) async-start(f32[8,1,192]{2,1,0:T(1,128)} %predict.1), calls=%async_computation.5 | async-start | bytes 16384 | tf_op jit(solution)/shard_map/all_to_all | solution.py:261

commit v4 on v3

--- a/solution.py
+++ b/solution.py
@@ -54,15 +54,19 @@
         for j in range(n)
     ]
     tw_copies = [pltpu.make_async_copy(tw_hbm.at[t], tw_ref.at[t], tw_sem.at[t]) for t in range(towers)]
+    steps = [[in_copies[j], w_copies[j]] for j in range(n)] + [[copy] for copy in tw_copies]
+    for step in steps[:2]:
+        for copy in step:
+            copy.start()
+
+    def arrive(i):
+        for copy in steps[i]:
+            copy.wait()
+        for copy in sum(steps[i + 2 : i + 3], []):
+            copy.start()
+
     for j in range(n):
-        in_copies[j].start()
-        w_copies[j].start()
-    for copy in tw_copies:
-        copy.start()
-
-    for j in range(n):
-        in_copies[j].wait()
-        w_copies[j].wait()
+        arrive(j)
 
         @pl.loop(0, w_ref.shape[2] // tile)
         def _(c):
@@ -76,7 +80,7 @@
                 hid_ref[:, cols] = (total / (1.0 + jnp.exp(-total))).astype(BF16)
 
     for t in range(towers):
-        tw_copies[t].wait()
+        arrive(n + t)
         out_ref[t // per, :, (t % per) * tile : (t % per + 1) * tile] = jnp.dot(
             hid_ref[...], tw_ref[t], preferred_element_type=F32
         ).astype(BF16)
@@ -124,7 +128,7 @@
     towers, _, tile = tw_ref.shape
     per = towers // n
     copies = [pltpu.make_async_copy(tw_hbm.at[t], tw_ref.at[t], tw_sem.at[t]) for t in range(towers)]
-    for copy in copies:
+    for copy in copies[:2]:
         copy.start()
     sides = [from_tower(side_ref, me, t) for t in range(towers)]
     cot = jnp.transpose(jnp.concatenate([v[:, :-tile] for v in sides], axis=0))[:count]
@@ -133,6 +137,8 @@
         sig = 1.0 / (1.0 + jnp.exp(-z))
         dz = cot[:, t : t + 1] * sides[t][:, -tile:] * sig * (1.0 + z * (1.0 - sig))
         copies[t].wait()
+        if t + 2 < towers:
+            copies[t + 2].start()
         part = lax.dot_general(dz.astype(BF16), tw_ref[t], LANES, preferred_element_type=F32)
         if t == 0:
             acc_ref[...] = part
@@ -152,8 +158,7 @@
     towers, units, tile = tower_weight.shape
     cols = towers * tile // n
     cap = max(2, 5 * count * top // (4 * experts))
-    pitch = -(-cap // 8) * 8
-    rows = experts * pitch
+    rows = experts * cap
     me = lax.axis_index("mp").astype(jnp.int32).reshape(1)
     ids = expert_ids.T
     levels = gate_levels.T
@@ -171,7 +176,7 @@
         side = jnp.concatenate([side, other], axis=0)
 
     out = pl.pallas_call(
-        functools.partial(dispatch_kernel, experts, pitch),
+        functools.partial(dispatch_kernel, experts, cap),
         out_shape=jax.ShapeDtypeStruct((rows, part), BF16),
         grid_spec=pltpu.PrefetchScalarGridSpec(
             num_scalar_prefetch=1,
@@ -186,7 +191,7 @@
     )(me, ids, tokens)
 
     def over_dp(a):
-        a = a.reshape(experts, pitch, a.shape[1])
+        a = a.reshape(experts, cap, 2, a.shape[1] // 2)
         return lax.all_to_all(a, "dp", split_axis=0, concat_axis=0, tiled=True).reshape(rows, -1)
 
     def over_mp(a):
@@ -222,7 +227,7 @@
     back, side = lax.optimization_barrier((over_dp(total.astype(BF16)), side))
 
     z = pl.pallas_call(
-        functools.partial(combine_kernel, experts, pitch),
+        functools.partial(combine_kernel, experts, cap),
         out_shape=jax.ShapeDtypeStruct((n, count, cols), BF16),
         in_specs=[VMEM] * 3,
         out_specs=VMEM,

time: 263 us -> 258 us (0.981)
  blocking collectives: 148 us -> 142 us
  waiting for transfers between devices: 53.2 us -> 50.5 us
    all_to_all x1, blocking collectives: 93.6 us -> 90.6 us  [over_dp(): lax.all_to_all(a, 'dp', split_axis=0, concat_axis=0, tiled=True)]
    all_to_all x2, blocking collectives: 54.3 us -> 51.5 us  [over_mp(): return lax.all_to_all(a, 'mp', split_axis=0, concat_axis=0, tiled=True)]
    all_to_all x1, waiting for transfers between devices: 40.4 us -> 37.7 us  [over_dp(): lax.all_to_all(a, 'dp', split_axis=0, concat_axis=0, tiled=True)]
  transfers between devices with their start and end apart: 6 -> 6, of which waited for: 5 -> 5; matrix products, arithmetic and copies ran while one was open for 0% -> 0% of each run, Pallas kernels for 2% -> 3%
where the time goes in v4:
time: 258 us; the launch traced here: 257 us
  blocking collectives  142 us (55%)
  waiting for transfers between devices  50.5 us (20%)
  starting transfers between devices  34.5 us (13%)
  Pallas kernels  25.1 us (10%)
  local copies, waits for them, and re-layouts  3.12 us (1%)
    all_to_all x1, blocking collectives, over_dp(): lax.all_to_all(a, 'dp', split_axis=0, concat_axis=0, tiled=True)  90.6 us
    all_to_all x2, blocking collectives, over_mp(): return lax.all_to_all(a, 'mp', split_axis=0, concat_axis=0, tiled=True)  51.5 us
    all_to_all x1, waiting for transfers between devices, over_dp(): lax.all_to_all(a, 'dp', split_axis=0, concat_axis=0, tiled=True)  37.7 us
    ppermute x3, starting transfers between devices, body(): other = lax.ppermute(side, 'task', [(i, i ^ bit) for i in range(tasks)])  13.3 us
    all_to_all x1, starting transfers between devices, body(): pred = lax.all_to_all(pred, 'task', split_axis=0, concat_axis=0, tiled=True)  13 us
    pallas_call x1, Pallas kernels, body(): pl.pallas_call(expert_kernel, out_shape=jax.ShapeDtypeStruct((n, rows, co...  12.5 us
    all_to_all x1, waiting for transfers between devices, over_mp(): return lax.all_to_all(a, 'mp', split_axis=0, concat_axis=0, tiled=True)  8.3 us
    pallas_call x1, Pallas kernels, body(): pl.pallas_call(gradient_kernel, out_shape=jax.ShapeDtypeStruct((count, un...  6.88 us
  transfers between devices with their start and end apart: 6, of which 5 were waited for; matrix products, arithmetic and copies ran while one was open for 0% of the time, Pallas kernels for 3%

profile of v4, /device:TPU:1, one launch (start us, length us, event | category | flops | bytes accessed | tf_op | source)
XLA Modules:
  0.0 256.8 jit_solution(2702562849405364856)
XLA Ops:
  0.6 2.2 dispatch.1
  2.8 1.1 reshape.28
  3.9 90.6 %all_to_all.30 = bf16[32,15,2,256]{3,2,1,0:T(2,128)(2,1)S(1)} all-to-all(bf16[32,15,2,256]{3,2,1,0:T(2,128)(2,1)S(1)} %reshape.28), channel_id=1, replica_groups=mesh['dp'=32,'task'=8,'mp'=4] {'dp'}, dimensions={0} | all-to-all | bytes 983040 | tf_op jit(solution)/shard_map/all_to_all | solution.py:195
  94.5 0.1 copy.9
  94.6 0.1 broadcast_in_dim.18
  94.8 27.0 %all_to_all.31.in_hbm = bf16[4,480,512]{2,1,0:T(8,128)(2,1)S(1)} all-to-all(bf16[4,480,512]{2,1,0:T(8,128)(2,1)S(1)} %broadcast_in_dim.18), channel_id=1, replica_groups=mesh['dp'=32,'task'=8,'mp'=4] {'mp'}, dimensions={0} | all-to-all | bytes 3932160 | tf_op jit(solution)/shard_map/all_to_all | solution.py:198
  121.8 12.5 %expert.1 = bf16[4,480,512]{2,1,0:T(8,128)(2,1)S(1)} custom-call(bf16[4,480,512]{2,1,0:T(8,128)(2,1)S(1)} %all_to_all.31.in_hbm, bf16[1,2048,1024]{2,1,0:T(8,128)(2,1)} %w_hbm.1, bf16[8,1024,256]{2,1,0:T(8,128)(2,1)} %tw_hbm.3), custom_call_target="tpu_custom_call" | custom-call | flops 4026531840 | bytes 8388608 | tf_op jit(solution)/shard_map/expert/pallas_call | solution.py:203
  134.3 24.4 %all_to_all.32 = bf16[4,480,512]{2,1,0:T(8,128)(2,1)S(1)} all-to-all(bf16[4,480,512]{2,1,0:T(8,128)(2,1)S(1)} %expert.1), channel_id=1, replica_groups=mesh['dp'=32,'task'=8,'mp'=4] {'mp'}, dimensions={0} | all-to-all | bytes 3932160 | tf_op jit(solution)/shard_map/all_to_all | solution.py:198
  158.7 0.0 copy-start.4
  158.8 0.0 copy-start.5
  158.8 0.6 reduce_sum.12
  159.4 0.0 copy-start.2
  159.4 0.0 copy-start.3
  159.4 0.9 reshape.29
  160.3 4.7 %all-to-all-start.3 = ((bf16[32,15,2,256]{3,2,1,0:T(2,128)(2,1)}), bf16[32,15,2,256]{3,2,1,0:T(2,128)(2,1)S(1)}, u32[]{:S(2)}, u32[]{:S(2)}) async-start(bf16[32,15,2,256]{3,2,1,0:T(2,128)(2,1)} %reshape.29), calls=%async_computation.3 | async-start | bytes 983040 | tf_op jit(solution)/shard_map/all_to_all | solution.py:195
  164.9 0.0 copy-done.4
  165.0 0.1 reshape.31
  165.1 0.0 copy-done.5
  165.1 5.3 %collective-permute-start = (f32[1,8,512]{2,1,0:T(8,128)S(1)}, f32[1,8,512]{2,1,0:T(8,128)S(1)}, u32[]{:S(2)}, u32[]{:S(2)}) collective-permute-start(f32[1,8,512]{2,1,0:T(8,128)S(1)} %fusion), channel_id=1, source_target_pairs={{0,4},{4,0},{8,12},{12,8},{16,20},{20,16},{24,28},{28,24},{1,5},{5... | collective-permute-start | bytes 49160 | tf_op jit(solution)/shard_map/ppermute | solution.py:175
  170.4 0.8 collective-permute-done
  171.3 3.2 %collective-permute-start.1 = (f32[2,8,512]{2,1,0:T(8,128)S(1)}, f32[2,8,512]{2,1,0:T(8,128)S(1)}, u32[]{:S(2)}, u32[]{:S(2)}) collective-permute-start(f32[2,8,512]{2,1,0:T(8,128)S(1)} %pad_maximum_fusion.2), channel_id=1, source_target_pairs={{0,8},{4,12},{8,0},{12,4},{16,24},{20,28},{24,16},{28,20},{1,9},{5... | collective-permute-start | bytes 98312 | tf_op jit(solution)/shard_map/ppermute | solution.py:175
  174.5 1.7 collective-permute-done.1
  176.2 4.8 %collective-permute-start.2 = (f32[4,8,512]{2,1,0:T(8,128)S(1)}, f32[4,8,512]{2,1,0:T(8,128)S(1)}, u32[]{:S(2)}, u32[]{:S(2)}) collective-permute-start(f32[4,8,512]{2,1,0:T(8,128)S(1)} %pad_maximum_fusion.1), channel_id=1, source_target_pairs={{0,16},{4,20},{8,24},{12,28},{16,0},{20,4},{24,8},{28,12},{1,17},{... | collective-permute-start | bytes 196616 | tf_op jit(solution)/shard_map/ppermute | solution.py:175
  181.0 2.0 collective-permute-done.2
  183.0 0.0 copy-start.1
  183.0 37.7 %all-to-all-done.3 = bf16[32,15,2,256]{3,2,1,0:T(2,128)(2,1)S(1)} async-done(((bf16[32,15,2,256]{3,2,1,0:T(2,128)(2,1)}), bf16[32,15,2,256]{3,2,1,0:T(2,128)(2,1)S(1)}, u32[]{:S(2)}, u32[]{:S(2)}) %all-to-all-start.3) | async-done | bytes 491552 | tf_op jit(solution)/shard_map/all_to_all | solution.py:195
  220.7 0.1 copy.10
  220.8 0.0 copy-done.2
  220.8 0.0 copy-done.3
  220.8 1.5 combine.1
  222.4 3.5 %all-to-all-start.4 = ((bf16[4,192,512]{2,1,0:T(8,128)(2,1)}), bf16[4,192,512]{2,1,0:T(8,128)(2,1)S(1)}, u32[]{:S(2)}, u32[]{:S(2)}) async-start(bf16[4,192,512]{2,1,0:T(8,128)(2,1)} %combine.1), calls=%async_computation.4 | async-start | bytes 1572864 | tf_op jit(solution)/shard_map/all_to_all | solution.py:198
  225.9 8.3 %all-to-all-done.4.z_ref = bf16[4,192,512]{2,1,0:T(8,128)(2,1)S(1)} async-done(((bf16[4,192,512]{2,1,0:T(8,128)(2,1)}), bf16[4,192,512]{2,1,0:T(8,128)(2,1)S(1)}, u32[]{:S(2)}, u32[]{:S(2)}) %all-to-all-start.4) | async-done | bytes 786464 | tf_op jit(solution)/shard_map/all_to_all | solution.py:198
  234.2 0.0 copy-start
  234.2 2.1 predict.1
  236.2 0.0 copy-done.1
  236.2 13.0 %all-to-all-start.5 = ((f32[8,1,192]{2,1,0:T(1,128)}), f32[8,1,192]{2,1,0:T(1,128)S(1)}, u32[]{:S(2)}, u32[]{:S(2)}) async-start(f32[8,1,192]{2,1,0:T(1,128)} %predict.1), calls=%async_computation.5 | async-start | bytes 16384 | tf_op jit(solution)/shard_map/all_to_all | solution.py:266
  249.2 0.0 copy-done
  249.2 6.9 %gradient.1 = bf16[192,1024]{1,0:T(8,128)(2,1)} custom-call(s32[1]{0:T(128)} %bitcast.me_ref, f32[8,8,512]{2,1,0:T(8,128)} %copy-done.1, bf16[4,192,512]{2,1,0:T(8,128)(2,1)} %copy-done, bf16[8,1024,256]{2,1,0:T(8,128)(2,1)} %tw_hbm.3), custom_call_target="tpu_custom_call" | custom-call | flops 805306368 | bytes 4194304 | tf_op jit(solution)/shard_map/gradient/pallas_call | solution.py:248
  256.1 0.0 all-to-all-done.5
  256.1 0.7 reshape.32
  (7 shorter events, 0.1 us)
Async XLA Ops:
  158.7 6.2 %copy-start.4 = (f32[1,1536]{1,0:T(1,128)S(1)}, f32[1,1536]{1,0:T(1,128)}, u32[]{:S(2)}) copy-start(f32[1,1536]{1,0:T(1,128)} %param.13) | copy-start | bytes 18436
  158.8 6.3 %copy-start.5 = (f32[1,256]{1,0:T(1,128)S(1)}, f32[1,256]{1,0:T(1,128)}, u32[]{:S(2)}) copy-start(f32[1,256]{1,0:T(1,128)} %param.12) | copy-start | bytes 3076
  159.4 61.5 %copy-start.2 = (s32[192,2]{0,1:T(2,128)S(1)}, s32[192,2]{0,1:T(2,128)}, u32[]{:S(2)}) copy-start(s32[192,2]{0,1:T(2,128)} %param.8) | copy-start | bytes 4612
  159.4 61.5 %copy-start.3 = (s32[192,2]{0,1:T(2,128)S(1)}, s32[192,2]{0,1:T(2,128)}, u32[]{:S(2)}) copy-start(s32[192,2]{0,1:T(2,128)} %param.9) | copy-start | bytes 4612
  160.3 60.5 %all-to-all-start.3 = ((bf16[32,15,2,256]{3,2,1,0:T(2,128)(2,1)}), bf16[32,15,2,256]{3,2,1,0:T(2,128)(2,1)S(1)}, u32[]{:S(2)}, u32[]{:S(2)}) async-start(bf16[32,15,2,256]{3,2,1,0:T(2,128)(2,1)} %reshape.29), calls=%async_computation.3 | async-start | bytes 983040 | tf_op jit(solution)/shard_map/all_to_all | solution.py:195
  165.1 6.2 %collective-permute-start = (f32[1,8,512]{2,1,0:T(8,128)S(1)}, f32[1,8,512]{2,1,0:T(8,128)S(1)}, u32[]{:S(2)}, u32[]{:S(2)}) collective-permute-start(f32[1,8,512]{2,1,0:T(8,128)S(1)} %fusion), channel_id=1, source_target_pairs={{0,4},{4,0},{8,12},{12,8},{16,20},{20,16},{24,28},{28,24},{1,5},{5... | collective-permute-start | bytes 49160 | tf_op jit(solution)/shard_map/ppermute | solution.py:175
  171.3 4.9 %collective-permute-start.1 = (f32[2,8,512]{2,1,0:T(8,128)S(1)}, f32[2,8,512]{2,1,0:T(8,128)S(1)}, u32[]{:S(2)}, u32[]{:S(2)}) collective-permute-start(f32[2,8,512]{2,1,0:T(8,128)S(1)} %pad_maximum_fusion.2), channel_id=1, source_target_pairs={{0,8},{4,12},{8,0},{12,4},{16,24},{20,28},{24,16},{28,20},{1,9},{5... | collective-permute-start | bytes 98312 | tf_op jit(solution)/shard_map/ppermute | solution.py:175
  176.2 6.8 %collective-permute-start.2 = (f32[4,8,512]{2,1,0:T(8,128)S(1)}, f32[4,8,512]{2,1,0:T(8,128)S(1)}, u32[]{:S(2)}, u32[]{:S(2)}) collective-permute-start(f32[4,8,512]{2,1,0:T(8,128)S(1)} %pad_maximum_fusion.1), channel_id=1, source_target_pairs={{0,16},{4,20},{8,24},{12,28},{16,0},{20,4},{24,8},{28,12},{1,17},{... | collective-permute-start | bytes 196616 | tf_op jit(solution)/shard_map/ppermute | solution.py:175
  183.0 53.2 %copy-start.1 = (f32[8,8,512]{2,1,0:T(8,128)}, f32[8,8,512]{2,1,0:T(8,128)S(1)}, u32[]{:S(2)}) copy-start(f32[8,8,512]{2,1,0:T(8,128)S(1)} %pad_maximum_fusion.side_ref) | copy-start | bytes 393220
  222.4 11.8 %all-to-all-start.4 = ((bf16[4,192,512]{2,1,0:T(8,128)(2,1)}), bf16[4,192,512]{2,1,0:T(8,128)(2,1)S(1)}, u32[]{:S(2)}, u32[]{:S(2)}) async-start(bf16[4,192,512]{2,1,0:T(8,128)(2,1)} %combine.1), calls=%async_computation.4 | async-start | bytes 1572864 | tf_op jit(solution)/shard_map/all_to_all | solution.py:198
  234.2 15.1 %copy-start = (bf16[4,192,512]{2,1,0:T(8,128)(2,1)}, bf16[4,192,512]{2,1,0:T(8,128)(2,1)S(1)}, u32[]{:S(2)}) copy-start(bf16[4,192,512]{2,1,0:T(8,128)(2,1)S(1)} %all-to-all-done.4.z_ref) | copy-start | bytes 2359300
  236.2 19.9 %all-to-all-start.5 = ((f32[8,1,192]{2,1,0:T(1,128)}), f32[8,1,192]{2,1,0:T(1,128)S(1)}, u32[]{:S(2)}, u32[]{:S(2)}) async-start(f32[8,1,192]{2,1,0:T(1,128)} %predict.1), calls=%async_computation.5 | async-start | bytes 16384 | tf_op jit(solution)/shard_map/all_to_all | solution.py:266

commit v5 on v2

--- a/solution.py
+++ b/solution.py
@@ -10,7 +10,6 @@
 F32 = jnp.float32
 BF16 = jnp.bfloat16
 VMEM = pl.BlockSpec(memory_space=pltpu.VMEM)
-HBM = pl.BlockSpec(memory_space=pltpu.HBM)
 SMEM = pl.BlockSpec(memory_space=pltpu.SMEM)
 LANES = (((1,), (1,)), ((), ()))
 ROWS = (((0,), (0,)), ((), ()))
@@ -44,38 +43,26 @@
     out_ref[...] = jnp.dot(pick, tok_ref[...], preferred_element_type=F32).astype(BF16)
 
 
-def expert_kernel(in_ref, w_hbm, tw_hbm, out_ref, w_ref, tw_ref, hid_ref, w_sem, tw_sem):
+def units_kernel(in_ref, w_ref, hid_ref):
     n, _, depth = in_ref.shape
-    towers, _, tile = tw_ref.shape
-    tiles = w_ref.shape[0]
-    per = towers // n
-
-    def w_copy(c):
+    tile = 256
+
+    @pl.loop(0, w_ref.shape[2] // tile)
+    def _(c):
         cols = pl.ds(pl.multiple_of(c * tile, tile), tile)
-        return pltpu.make_async_copy(w_hbm.at[0, :, cols], w_ref.at[c], w_sem.at[c])
-
-    def tw_copy(t):
-        return pltpu.make_async_copy(tw_hbm.at[t], tw_ref.at[t], tw_sem.at[t])
-
-    for c in range(tiles):
-        w_copy(c).start()
-    for t in range(towers):
-        tw_copy(t).start()
-
-    @pl.loop(0, tiles)
-    def _(c):
-        w_copy(c).wait()
         total = None
         for j in range(n):
             part = jnp.dot(
-                in_ref[j], w_ref[c, j * depth : (j + 1) * depth, :], preferred_element_type=F32
+                in_ref[j], w_ref[0, j * depth : (j + 1) * depth, cols], preferred_element_type=F32
             )
             total = part if total is None else total + part
-        cols = pl.ds(pl.multiple_of(c * tile, tile), tile)
         hid_ref[:, cols] = (total / (1.0 + jnp.exp(-total))).astype(BF16)
 
+
+def layers_kernel(hid_ref, tw_ref, out_ref):
+    towers, _, tile = tw_ref.shape
+    per = towers // out_ref.shape[0]
     for t in range(towers):
-        tw_copy(t).wait()
         out_ref[t // per, :, (t % per) * tile : (t % per + 1) * tile] = jnp.dot(
             hid_ref[...], tw_ref[t], preferred_element_type=F32
         ).astype(BF16)
@@ -92,7 +79,8 @@
     rows = back_ref[...]
     z = lax.dot_general(high, rows, ROWS, preferred_element_type=F32)
     z = z + lax.dot_general(low, rows, ROWS, preferred_element_type=F32)
-    out_ref[...] = z.astype(BF16)
+    for j in range(out_ref.shape[0]):
+        out_ref[j] = z.astype(BF16)
 
 
 def from_tower(side_ref, me, t):
@@ -107,7 +95,7 @@
     for t in range(towers):
         z = z_ref[t // per, :, (t % per) * tile : (t % per + 1) * tile].astype(F32)
         out_vec = from_tower(side_ref, me, t)[:, -tile:]
-        pred_ref[t : t + 1, :] = lax.dot_general(
+        pred_ref[t] = lax.dot_general(
             out_vec,
             z / (1.0 + jnp.exp(-z)),
             LANES,
@@ -116,21 +104,17 @@
         )
 
 
-def gradient_kernel(me_ref, side_ref, z_ref, tw_hbm, grad_ref, tw_ref, acc_ref, tw_sem):
+def gradient_kernel(me_ref, side_ref, z_ref, tw_ref, grad_ref, acc_ref):
     me = me_ref[0]
     n, count, cols = z_ref.shape
     towers, _, tile = tw_ref.shape
     per = towers // n
-    copies = [pltpu.make_async_copy(tw_hbm.at[t], tw_ref.at[t], tw_sem.at[t]) for t in range(towers)]
-    for copy in copies:
-        copy.start()
     sides = [from_tower(side_ref, me, t) for t in range(towers)]
     cot = jnp.transpose(jnp.concatenate([v[:, :-tile] for v in sides], axis=0))[:count]
     for t in range(towers):
         z = z_ref[t // per, :, (t % per) * tile : (t % per + 1) * tile].astype(F32)
         sig = 1.0 / (1.0 + jnp.exp(-z))
         dz = cot[:, t : t + 1] * sides[t][:, -tile:] * sig * (1.0 + z * (1.0 - sig))
-        copies[t].wait()
         part = lax.dot_general(dz.astype(BF16), tw_ref[t], LANES, preferred_element_type=F32)
         if t == 0:
             acc_ref[...] = part
@@ -150,8 +134,7 @@
     towers, units, tile = tower_weight.shape
     cols = towers * tile // n
     cap = max(2, 5 * count * top // (4 * experts))
-    pitch = -(-cap // 8) * 8
-    rows = experts * pitch
+    rows = experts * cap
     me = lax.axis_index("mp").astype(jnp.int32).reshape(1)
     ids = expert_ids.T
     levels = gate_levels.T
@@ -169,7 +152,7 @@
         side = jnp.concatenate([side, other], axis=0)
 
     out = pl.pallas_call(
-        functools.partial(dispatch_kernel, experts, pitch),
+        functools.partial(dispatch_kernel, experts, cap),
         out_shape=jax.ShapeDtypeStruct((rows, part), BF16),
         grid_spec=pltpu.PrefetchScalarGridSpec(
             num_scalar_prefetch=1,
@@ -184,7 +167,7 @@
     )(me, ids, tokens)
 
     def over_dp(a):
-        a = a.reshape(experts, pitch, a.shape[1])
+        a = a.reshape(experts, cap, 2, a.shape[1] // 2)
         return lax.all_to_all(a, "dp", split_axis=0, concat_axis=0, tiled=True).reshape(rows, -1)
 
     def over_mp(a):
@@ -193,43 +176,49 @@
     def spread(a):
         return over_mp(jnp.broadcast_to(a[None], (n,) + a.shape))
 
+    hidden = pl.pallas_call(
+        units_kernel,
+        out_shape=jax.ShapeDtypeStruct((rows, units), BF16),
+        in_specs=[VMEM] * 2,
+        out_specs=VMEM,
+        compiler_params=pltpu.CompilerParams(vmem_limit_bytes=24 << 20),
+        cost_estimate=pl.CostEstimate(
+            flops=2 * rows * units * width,
+            bytes_accessed=2 * (units * width + rows * (units + width)),
+            transcendentals=rows * units,
+        ),
+        name="units",
+    )(spread(over_dp(out)), expert_weight)
     outs = pl.pallas_call(
-        expert_kernel,
+        layers_kernel,
         out_shape=jax.ShapeDtypeStruct((n, rows, cols), BF16),
-        in_specs=[VMEM, HBM, HBM],
-        out_specs=VMEM,
-        scratch_shapes=[
-            pltpu.VMEM((units // tile, width, tile), BF16),
-            pltpu.VMEM((towers, units, tile), BF16),
-            pltpu.VMEM((rows, units), BF16),
-            pltpu.SemaphoreType.DMA((units // tile,)),
-            pltpu.SemaphoreType.DMA((towers,)),
-        ],
-        compiler_params=pltpu.CompilerParams(vmem_limit_bytes=50 << 20),
+        in_specs=[VMEM] * 2,
+        out_specs=VMEM,
+        compiler_params=pltpu.CompilerParams(vmem_limit_bytes=24 << 20),
         cost_estimate=pl.CostEstimate(
-            flops=2 * rows * units * (width + towers * tile),
-            bytes_accessed=2 * units * (width + towers * tile),
-            transcendentals=rows * units,
-        ),
-        name="expert",
-    )(spread(over_dp(out)), expert_weight, tower_weight)
+            flops=2 * rows * units * towers * tile,
+            bytes_accessed=2 * (units * towers * tile + rows * (units + towers * tile)),
+            transcendentals=0,
+        ),
+        name="layers",
+    )(hidden, tower_weight)
     total = jnp.sum(over_mp(outs).astype(F32), axis=0)
     back, side = lax.optimization_barrier((over_dp(total.astype(BF16)), side))
 
     z = pl.pallas_call(
-        functools.partial(combine_kernel, experts, pitch),
-        out_shape=jax.ShapeDtypeStruct((count, cols), BF16),
+        functools.partial(combine_kernel, experts, cap),
+        out_shape=jax.ShapeDtypeStruct((n, count, cols), BF16),
         in_specs=[VMEM] * 3,
         out_specs=VMEM,
         compiler_params=pltpu.CompilerParams(vmem_limit_bytes=16 << 20),
         name="combine",
     )(ids, levels, back)
-    zs = spread(z)
+    zs = over_mp(z)
 
     task = lax.axis_index("task").astype(jnp.int32).reshape(1)
     pred = pl.pallas_call(
         functools.partial(predict_kernel, towers),
-        out_shape=jax.ShapeDtypeStruct((towers, count), F32),
+        out_shape=jax.ShapeDtypeStruct((towers, 1, count), F32),
         in_specs=[SMEM, VMEM, VMEM],
         out_specs=VMEM,
         compiler_params=pltpu.CompilerParams(vmem_limit_bytes=16 << 20),
@@ -238,14 +227,10 @@
     grad = pl.pallas_call(
         gradient_kernel,
         out_shape=jax.ShapeDtypeStruct((count, units), BF16),
-        in_specs=[SMEM, VMEM, VMEM, HBM],
-        out_specs=VMEM,
-        scratch_shapes=[
-            pltpu.VMEM((towers, units, tile), BF16),
-            pltpu.VMEM((count, units), F32),
-            pltpu.SemaphoreType.DMA((towers,)),
-        ],
-        compiler_params=pltpu.CompilerParams(vmem_limit_bytes=54 << 20),
+        in_specs=[SMEM] + [VMEM] * 3,
+        out_specs=VMEM,
+        scratch_shapes=[pltpu.VMEM((count, units), F32)],
+        compiler_params=pltpu.CompilerParams(vmem_limit_bytes=24 << 20),
         cost_estimate=pl.CostEstimate(
             flops=2 * count * units * towers * tile,
             bytes_accessed=2 * units * towers * tile,

time: 262 us -> 248 us (0.947)
  Pallas kernels: 21.3 us -> 13.4 us
  blocking collectives: 148 us -> 142 us
  local copies, waits for them, and re-layouts: 2.51 us -> 5.3 us
  waiting for transfers between devices: 53.2 us -> 50.5 us
    pallas_call x3 -> x4, Pallas kernels: 14.8 us -> 8.72 us  [the longest x1 2.86 us: body(): pl.pallas_call(units_kernel, out_shape=jax.ShapeDtypeStruct((rows, units)...]
    all_to_all x1, blocking collectives: 93.6 us -> 90.6 us  [over_dp(): lax.all_to_all(a, 'dp', split_axis=0, concat_axis=0, tiled=True)]
    all_to_all x1, waiting for transfers between devices: 40.4 us -> 37.7 us  [over_dp(): lax.all_to_all(a, 'dp', split_axis=0, concat_axis=0, tiled=True)]
  transfers between devices with their start and end apart: 6 -> 6, of which waited for: 5 -> 5; matrix products, arithmetic and copies ran while one was open for 0% -> 0% of each run, Pallas kernels for 2% -> 1%
where the time goes in v5:
time: 248 us
  blocking collectives  142 us (57%)
  waiting for transfers between devices  50.5 us (20%)
  starting transfers between devices  34.5 us (14%)
  Pallas kernels  13.4 us (5%)
  local copies, waits for them, and re-layouts  5.3 us (2%)
    all_to_all x1, blocking collectives, over_dp(): lax.all_to_all(a, 'dp', split_axis=0, concat_axis=0, tiled=True)  90.6 us
    all_to_all x2, blocking collectives, over_mp(): return lax.all_to_all(a, 'mp', split_axis=0, concat_axis=0, tiled=True)  51.7 us
    all_to_all x1, waiting for transfers between devices, over_dp(): lax.all_to_all(a, 'dp', split_axis=0, concat_axis=0, tiled=True)  37.7 us
    ppermute x3, starting transfers between devices, body(): other = lax.ppermute(side, 'task', [(i, i ^ bit) for i in range(tasks)])  13.3 us
    all_to_all x1, starting transfers between devices, body(): pred = lax.all_to_all(pred, 'task', split_axis=0, concat_axis=0, tiled=True)  13 us
    all_to_all x1, waiting for transfers between devices, over_mp(): return lax.all_to_all(a, 'mp', split_axis=0, concat_axis=0, tiled=True)  8.3 us
  transfers between devices with their start and end apart: 6, of which 5 were waited for; matrix products, arithmetic and copies ran while one was open for 0% of the time, Pallas kernels for 1%

profile of v5, /device:TPU:1, one launch (start us, length us, event | category | flops | bytes accessed | tf_op | source)
XLA Modules:
  0.0 247.5 jit_solution(6121274190353516260)
XLA Ops:
  0.6 2.1 dispatch.1
  2.8 1.1 reshape.28
  3.9 90.6 %all_to_all.30 = bf16[32,15,2,256]{3,2,1,0:T(2,128)(2,1)S(1)} all-to-all(bf16[32,15,2,256]{3,2,1,0:T(2,128)(2,1)S(1)} %reshape.28), channel_id=1, replica_groups=mesh['dp'=32,'task'=8,'mp'=4] {'dp'}, dimensions={0} | all-to-all | bytes 983040 | tf_op jit(solution)/shard_map/all_to_all | solution.py:171
  94.5 0.1 copy.9
  94.6 0.0 copy-start.4
  94.6 0.1 broadcast_in_dim.18
  94.8 27.3 %all_to_all.31.in_ref = bf16[4,480,512]{2,1,0:T(8,128)(2,1)S(1)} all-to-all(bf16[4,480,512]{2,1,0:T(8,128)(2,1)S(1)} %broadcast_in_dim.18), channel_id=1, replica_groups=mesh['dp'=32,'task'=8,'mp'=4] {'mp'}, dimensions={0} | all-to-all | bytes 3932160 | tf_op jit(solution)/shard_map/all_to_all | solution.py:174
  122.1 0.0 copy-done.4
  122.1 0.0 copy-start
  122.1 2.9 %units.1.hid_ref = bf16[480,1024]{1,0:T(8,128)(2,1)S(1)} custom-call(bf16[4,480,512]{2,1,0:T(8,128)(2,1)S(1)} %all_to_all.31.in_ref, bf16[1,2048,1024]{2,1,0:T(8,128)(2,1)S(1)} %copy-done.4), custom_call_target="tpu_custom_call" | custom-call | flops 2013265920 | bytes 7143424 | tf_op jit(solution)/shard_map/units/pallas_call | solution.py:179
  125.0 0.0 copy-done
  125.0 2.2 layers.1
  127.2 24.4 %all_to_all.32 = bf16[4,480,512]{2,1,0:T(8,128)(2,1)S(1)} all-to-all(bf16[4,480,512]{2,1,0:T(8,128)(2,1)S(1)} %layers.1), channel_id=1, replica_groups=mesh['dp'=32,'task'=8,'mp'=4] {'mp'}, dimensions={0} | all-to-all | bytes 3932160 | tf_op jit(solution)/shard_map/all_to_all | solution.py:174
  151.6 0.0 copy-start.5
  151.6 0.0 copy-start.6
  151.6 0.6 reduce_sum.12
  152.2 0.0 copy-start.2
  152.2 0.0 copy-start.3
  152.2 0.9 reshape.29
  153.1 4.7 %all-to-all-start.3 = ((bf16[32,15,2,256]{3,2,1,0:T(2,128)(2,1)}), bf16[32,15,2,256]{3,2,1,0:T(2,128)(2,1)S(1)}, u32[]{:S(2)}, u32[]{:S(2)}) async-start(bf16[32,15,2,256]{3,2,1,0:T(2,128)(2,1)} %reshape.29), calls=%async_computation.3 | async-start | bytes 983040 | tf_op jit(solution)/shard_map/all_to_all | solution.py:171
  157.8 0.0 copy-done.5
  157.9 0.1 reshape.31
  157.9 0.0 copy-done.6
  158.0 5.3 %collective-permute-start = (f32[1,8,512]{2,1,0:T(8,128)S(1)}, f32[1,8,512]{2,1,0:T(8,128)S(1)}, u32[]{:S(2)}, u32[]{:S(2)}) collective-permute-start(f32[1,8,512]{2,1,0:T(8,128)S(1)} %fusion), channel_id=1, source_target_pairs={{0,4},{4,0},{8,12},{12,8},{16,20},{20,16},{24,28},{28,24},{1,5},{5... | collective-permute-start | bytes 49160 | tf_op jit(solution)/shard_map/ppermute | solution.py:151
  163.3 0.8 collective-permute-done
  164.1 3.2 %collective-permute-start.1 = (f32[2,8,512]{2,1,0:T(8,128)S(1)}, f32[2,8,512]{2,1,0:T(8,128)S(1)}, u32[]{:S(2)}, u32[]{:S(2)}) collective-permute-start(f32[2,8,512]{2,1,0:T(8,128)S(1)} %pad_maximum_fusion.2), channel_id=1, source_target_pairs={{0,8},{4,12},{8,0},{12,4},{16,24},{20,28},{24,16},{28,20},{1,9},{5... | collective-permute-start | bytes 98312 | tf_op jit(solution)/shard_map/ppermute | solution.py:151
  167.3 1.7 collective-permute-done.1
  169.1 4.8 %collective-permute-start.2 = (f32[4,8,512]{2,1,0:T(8,128)S(1)}, f32[4,8,512]{2,1,0:T(8,128)S(1)}, u32[]{:S(2)}, u32[]{:S(2)}) collective-permute-start(f32[4,8,512]{2,1,0:T(8,128)S(1)} %pad_maximum_fusion.1), channel_id=1, source_target_pairs={{0,16},{4,20},{8,24},{12,28},{16,0},{20,4},{24,8},{28,12},{1,17},{... | collective-permute-start | bytes 196616 | tf_op jit(solution)/shard_map/ppermute | solution.py:151
  173.9 2.0 collective-permute-done.2
  175.9 37.7 %all-to-all-done.3 = bf16[32,15,2,256]{3,2,1,0:T(2,128)(2,1)S(1)} async-done(((bf16[32,15,2,256]{3,2,1,0:T(2,128)(2,1)}), bf16[32,15,2,256]{3,2,1,0:T(2,128)(2,1)S(1)}, u32[]{:S(2)}, u32[]{:S(2)}) %all-to-all-start.3) | async-done | bytes 491552 | tf_op jit(solution)/shard_map/all_to_all | solution.py:171
  213.6 0.1 copy.10
  213.7 0.0 copy-done.2
  213.7 0.0 copy-done.3
  213.7 1.5 combine.1
  215.2 3.5 %all-to-all-start.4 = ((bf16[4,192,512]{2,1,0:T(8,128)(2,1)}), bf16[4,192,512]{2,1,0:T(8,128)(2,1)S(1)}, u32[]{:S(2)}, u32[]{:S(2)}) async-start(bf16[4,192,512]{2,1,0:T(8,128)(2,1)} %combine.1), calls=%async_computation.4 | async-start | bytes 1572864 | tf_op jit(solution)/shard_map/all_to_all | solution.py:174
  218.7 8.3 %all-to-all-done.4.z_ref = bf16[4,192,512]{2,1,0:T(8,128)(2,1)S(1)} async-done(((bf16[4,192,512]{2,1,0:T(8,128)(2,1)}), bf16[4,192,512]{2,1,0:T(8,128)(2,1)S(1)}, u32[]{:S(2)}, u32[]{:S(2)}) %all-to-all-start.4) | async-done | bytes 786464 | tf_op jit(solution)/shard_map/all_to_all | solution.py:174
  227.0 2.1 predict.1
  229.1 13.0 %all-to-all-start.5 = ((f32[8,1,192]{2,1,0:T(1,128)}), f32[8,1,192]{2,1,0:T(1,128)S(1)}, u32[]{:S(2)}, u32[]{:S(2)}) async-start(f32[8,1,192]{2,1,0:T(1,128)} %predict.1), calls=%async_computation.5 | async-start | bytes 16384 | tf_op jit(solution)/shard_map/all_to_all | solution.py:241
  242.1 0.0 copy-start.1
  242.1 2.2 copy-done.1
  244.3 2.6 %gradient.1 = bf16[192,1024]{1,0:T(8,128)(2,1)} custom-call(s32[1]{0:T(128)} %bitcast.me_ref, f32[8,8,512]{2,1,0:T(8,128)S(1)} %pad_maximum_fusion.side_ref, bf16[4,192,512]{2,1,0:T(8,128)(2,1)S(1)} %all-to-all-done.4.z_ref, bf16[8,1024,256]{2,1,0:T(8,128)(2,1)S(1)} %copy-done.1), custom_call_target="tpu_custom_call" | custom-call | flops 805306368 | bytes 4194304 | tf_op jit(solution)/shard_map/gradient/pallas_call | solution.py:227
  246.8 0.0 all-to-all-done.5
  246.9 0.7 reshape.32
  (7 shorter events, 0.1 us)
Async XLA Ops:
  94.6 27.5 %copy-start.4 = (bf16[1,2048,1024]{2,1,0:T(8,128)(2,1)S(1)}, bf16[1,2048,1024]{2,1,0:T(8,128)(2,1)}, u32[]{:S(2)}) copy-start(bf16[1,2048,1024]{2,1,0:T(8,128)(2,1)} %w_ref.1) | copy-start | bytes 12582916
  122.1 2.9 %copy-start = (bf16[8,1024,256]{2,1,0:T(8,128)(2,1)S(1)}, bf16[8,1024,256]{2,1,0:T(8,128)(2,1)}, u32[]{:S(2)}) copy-start(bf16[8,1024,256]{2,1,0:T(8,128)(2,1)} %tw_ref.3) | copy-start | bytes 12582916
  151.6 6.2 %copy-start.5 = (f32[1,1536]{1,0:T(1,128)S(1)}, f32[1,1536]{1,0:T(1,128)}, u32[]{:S(2)}) copy-start(f32[1,1536]{1,0:T(1,128)} %param.13) | copy-start | bytes 18436
  151.6 6.3 %copy-start.6 = (f32[1,256]{1,0:T(1,128)S(1)}, f32[1,256]{1,0:T(1,128)}, u32[]{:S(2)}) copy-start(f32[1,256]{1,0:T(1,128)} %param.12) | copy-start | bytes 3076
  152.2 61.4 %copy-start.2 = (s32[192,2]{0,1:T(2,128)S(1)}, s32[192,2]{0,1:T(2,128)}, u32[]{:S(2)}) copy-start(s32[192,2]{0,1:T(2,128)} %param.8) | copy-start | bytes 4612
  152.2 61.4 %copy-start.3 = (s32[192,2]{0,1:T(2,128)S(1)}, s32[192,2]{0,1:T(2,128)}, u32[]{:S(2)}) copy-start(s32[192,2]{0,1:T(2,128)} %param.9) | copy-start | bytes 4612
  153.1 60.4 %all-to-all-start.3 = ((bf16[32,15,2,256]{3,2,1,0:T(2,128)(2,1)}), bf16[32,15,2,256]{3,2,1,0:T(2,128)(2,1)S(1)}, u32[]{:S(2)}, u32[]{:S(2)}) async-start(bf16[32,15,2,256]{3,2,1,0:T(2,128)(2,1)} %reshape.29), calls=%async_computation.3 | async-start | bytes 983040 | tf_op jit(solution)/shard_map/all_to_all | solution.py:171
  158.0 6.2 %collective-permute-start = (f32[1,8,512]{2,1,0:T(8,128)S(1)}, f32[1,8,512]{2,1,0:T(8,128)S(1)}, u32[]{:S(2)}, u32[]{:S(2)}) collective-permute-start(f32[1,8,512]{2,1,0:T(8,128)S(1)} %fusion), channel_id=1, source_target_pairs={{0,4},{4,0},{8,12},{12,8},{16,20},{20,16},{24,28},{28,24},{1,5},{5... | collective-permute-start | bytes 49160 | tf_op jit(solution)/shard_map/ppermute | solution.py:151
  164.1 4.9 %collective-permute-start.1 = (f32[2,8,512]{2,1,0:T(8,128)S(1)}, f32[2,8,512]{2,1,0:T(8,128)S(1)}, u32[]{:S(2)}, u32[]{:S(2)}) collective-permute-start(f32[2,8,512]{2,1,0:T(8,128)S(1)} %pad_maximum_fusion.2), channel_id=1, source_target_pairs={{0,8},{4,12},{8,0},{12,4},{16,24},{20,28},{24,16},{28,20},{1,9},{5... | collective-permute-start | bytes 98312 | tf_op jit(solution)/shard_map/ppermute | solution.py:151
  169.1 6.8 %collective-permute-start.2 = (f32[4,8,512]{2,1,0:T(8,128)S(1)}, f32[4,8,512]{2,1,0:T(8,128)S(1)}, u32[]{:S(2)}, u32[]{:S(2)}) collective-permute-start(f32[4,8,512]{2,1,0:T(8,128)S(1)} %pad_maximum_fusion.1), channel_id=1, source_target_pairs={{0,16},{4,20},{8,24},{12,28},{16,0},{20,4},{24,8},{28,12},{1,17},{... | collective-permute-start | bytes 196616 | tf_op jit(solution)/shard_map/ppermute | solution.py:151
  215.2 11.8 %all-to-all-start.4 = ((bf16[4,192,512]{2,1,0:T(8,128)(2,1)}), bf16[4,192,512]{2,1,0:T(8,128)(2,1)S(1)}, u32[]{:S(2)}, u32[]{:S(2)}) async-start(bf16[4,192,512]{2,1,0:T(8,128)(2,1)} %combine.1), calls=%async_computation.4 | async-start | bytes 1572864 | tf_op jit(solution)/shard_map/all_to_all | solution.py:174
  229.1 17.8 %all-to-all-start.5 = ((f32[8,1,192]{2,1,0:T(1,128)}), f32[8,1,192]{2,1,0:T(1,128)S(1)}, u32[]{:S(2)}, u32[]{:S(2)}) async-start(f32[8,1,192]{2,1,0:T(1,128)} %predict.1), calls=%async_computation.5 | async-start | bytes 16384 | tf_op jit(solution)/shard_map/all_to_all | solution.py:241
  242.1 2.2 copy-start.1

commit v6 on v5

--- a/solution.py
+++ b/solution.py
@@ -92,16 +92,17 @@
     n, count, cols = z_ref.shape
     per = towers // n
     tile = cols // per
+    lane = lax.broadcasted_iota(jnp.int32, (count, 128), 1)
+    sums = jnp.zeros((count, 128), F32)
     for t in range(towers):
         z = z_ref[t // per, :, (t % per) * tile : (t % per + 1) * tile].astype(F32)
         out_vec = from_tower(side_ref, me, t)[:, -tile:]
-        pred_ref[t] = lax.dot_general(
-            out_vec,
-            z / (1.0 + jnp.exp(-z)),
-            LANES,
-            precision=lax.Precision.HIGHEST,
-            preferred_element_type=F32,
-        )
+        pred = jnp.sum(z / (1.0 + jnp.exp(-z)) * out_vec, axis=1, keepdims=True)
+        sums = jnp.where(lane == t, pred, sums)
+    sums = jnp.concatenate([sums, jnp.zeros((-count % 128, 128), F32)], axis=0)
+    rows = jnp.transpose(sums)
+    for t in range(towers):
+        pred_ref[t] = rows[t : t + 1, :count]
 
 
 def gradient_kernel(me_ref, side_ref, z_ref, tw_ref, grad_ref, acc_ref):
@@ -203,7 +204,8 @@
         name="layers",
     )(hidden, tower_weight)
     total = jnp.sum(over_mp(outs).astype(F32), axis=0)
-    back, side = lax.optimization_barrier((over_dp(total.astype(BF16)), side))
+    task = lax.axis_index("task").astype(jnp.int32).reshape(1)
+    back, side, task = lax.optimization_barrier((over_dp(total.astype(BF16)), side, task))
 
     z = pl.pallas_call(
         functools.partial(combine_kernel, experts, cap),
@@ -215,7 +217,6 @@
     )(ids, levels, back)
     zs = over_mp(z)
 
-    task = lax.axis_index("task").astype(jnp.int32).reshape(1)
     pred = pl.pallas_call(
         functools.partial(predict_kernel, towers),
         out_shape=jax.ShapeDtypeStruct((towers, 1, count), F32),

time: 248 us -> 245 us (0.988)
  blocking collectives: 142 us -> 153 us
  waiting for transfers between devices: 50.5 us -> 42.2 us
  starting transfers between devices: 34.5 us -> 31 us
    all_to_all x2 -> x3, blocking collectives: 51.7 us -> 62.5 us  [over_mp(): return lax.all_to_all(a, 'mp', split_axis=0, concat_axis=0, tiled=True)]
    all_to_all x1 -> x0, waiting for transfers between devices: 8.3 us -> none  [over_mp(): return lax.all_to_all(a, 'mp', split_axis=0, concat_axis=0, tiled=True)]
    all_to_all x1 -> x0, starting transfers between devices: 3.49 us -> none  [over_mp(): return lax.all_to_all(a, 'mp', split_axis=0, concat_axis=0, tiled=True)]
  transfers between devices with their start and end apart: 6 -> 5, of which waited for: 5 -> 4; matrix products, arithmetic and copies ran while one was open for 0% -> 0% of each run, Pallas kernels for 1% -> 1%
where the time goes in v6:
time: 245 us
  blocking collectives  153 us (62%)
  waiting for transfers between devices  42.2 us (17%)
  starting transfers between devices  31 us (13%)
  Pallas kernels  11.6 us (5%)
  local copies, waits for them, and re-layouts  5.31 us (2%)
    all_to_all x1, blocking collectives, over_dp(): lax.all_to_all(a, 'dp', split_axis=0, concat_axis=0, tiled=True)  90.6 us
    all_to_all x3, blocking collectives, over_mp(): return lax.all_to_all(a, 'mp', split_axis=0, concat_axis=0, tiled=True)  62.5 us
    all_to_all x1, waiting for transfers between devices, over_dp(): lax.all_to_all(a, 'dp', split_axis=0, concat_axis=0, tiled=True)  37.7 us
    ppermute x3, starting transfers between devices, body(): other = lax.ppermute(side, 'task', [(i, i ^ bit) for i in range(tasks)])  13.3 us
    all_to_all x1, starting transfers between devices, body(): pred = lax.all_to_all(pred, 'task', split_axis=0, concat_axis=0, tiled=True)  13 us
  transfers between devices with their start and end apart: 5, of which 4 were waited for; matrix products, arithmetic and copies ran while one was open for 0% of the time, Pallas kernels for 1%

profile of v6, /device:TPU:1, one launch (start us, length us, event | category | flops | bytes accessed | tf_op | source)
XLA Modules:
  0.0 244.7 jit_solution(7555055767488951873)
XLA Ops:
  0.6 2.2 dispatch.1
  2.8 1.1 reshape.27
  3.9 90.6 %all_to_all.30 = bf16[32,15,2,256]{3,2,1,0:T(2,128)(2,1)S(1)} all-to-all(bf16[32,15,2,256]{3,2,1,0:T(2,128)(2,1)S(1)} %reshape.27), channel_id=1, replica_groups=mesh['dp'=32,'task'=8,'mp'=4] {'dp'}, dimensions={0} | all-to-all | bytes 983040 | tf_op jit(solution)/shard_map/all_to_all | solution.py:172
  94.5 0.1 copy.9
  94.6 0.0 copy-start.4
  94.6 0.1 broadcast_in_dim.18
  94.8 27.3 %all_to_all.31.in_ref = bf16[4,480,512]{2,1,0:T(8,128)(2,1)S(1)} all-to-all(bf16[4,480,512]{2,1,0:T(8,128)(2,1)S(1)} %broadcast_in_dim.18), channel_id=1, replica_groups=mesh['dp'=32,'task'=8,'mp'=4] {'mp'}, dimensions={0} | all-to-all | bytes 3932160 | tf_op jit(solution)/shard_map/all_to_all | solution.py:175
  122.1 0.0 copy-done.4
  122.1 0.0 copy-start
  122.1 2.9 %units.1.hid_ref = bf16[480,1024]{1,0:T(8,128)(2,1)S(1)} custom-call(bf16[4,480,512]{2,1,0:T(8,128)(2,1)S(1)} %all_to_all.31.in_ref, bf16[1,2048,1024]{2,1,0:T(8,128)(2,1)S(1)} %copy-done.4), custom_call_target="tpu_custom_call" | custom-call | flops 2013265920 | bytes 7143424 | tf_op jit(solution)/shard_map/units/pallas_call | solution.py:180
  125.0 0.0 copy-done
  125.0 2.2 layers.1
  127.2 24.4 %all_to_all.32 = bf16[4,480,512]{2,1,0:T(8,128)(2,1)S(1)} all-to-all(bf16[4,480,512]{2,1,0:T(8,128)(2,1)S(1)} %layers.1), channel_id=1, replica_groups=mesh['dp'=32,'task'=8,'mp'=4] {'mp'}, dimensions={0} | all-to-all | bytes 3932160 | tf_op jit(solution)/shard_map/all_to_all | solution.py:175
  151.6 0.0 copy-start.5
  151.6 0.0 copy-start.6
  151.6 0.6 reduce_sum.12
  152.2 0.0 copy-start.2
  152.2 0.0 copy-start.3
  152.2 0.9 reshape.28
  153.1 4.7 %all-to-all-start.3 = ((bf16[32,15,2,256]{3,2,1,0:T(2,128)(2,1)}), bf16[32,15,2,256]{3,2,1,0:T(2,128)(2,1)S(1)}, u32[]{:S(2)}, u32[]{:S(2)}) async-start(bf16[32,15,2,256]{3,2,1,0:T(2,128)(2,1)} %reshape.28), calls=%async_computation.3 | async-start | bytes 983040 | tf_op jit(solution)/shard_map/all_to_all | solution.py:172
  157.8 0.0 copy-done.5
  157.9 0.1 reshape.30
  157.9 0.0 copy-done.6
  158.0 5.3 %collective-permute-start = (f32[1,8,512]{2,1,0:T(8,128)S(1)}, f32[1,8,512]{2,1,0:T(8,128)S(1)}, u32[]{:S(2)}, u32[]{:S(2)}) collective-permute-start(f32[1,8,512]{2,1,0:T(8,128)S(1)} %fusion), channel_id=1, source_target_pairs={{0,4},{4,0},{8,12},{12,8},{16,20},{20,16},{24,28},{28,24},{1,5},{5... | collective-permute-start | bytes 49160 | tf_op jit(solution)/shard_map/ppermute | solution.py:152
  163.3 0.8 collective-permute-done
  164.1 3.2 %collective-permute-start.1 = (f32[2,8,512]{2,1,0:T(8,128)S(1)}, f32[2,8,512]{2,1,0:T(8,128)S(1)}, u32[]{:S(2)}, u32[]{:S(2)}) collective-permute-start(f32[2,8,512]{2,1,0:T(8,128)S(1)} %pad_maximum_fusion.2), channel_id=1, source_target_pairs={{0,8},{4,12},{8,0},{12,4},{16,24},{20,28},{24,16},{28,20},{1,9},{5... | collective-permute-start | bytes 98312 | tf_op jit(solution)/shard_map/ppermute | solution.py:152
  167.3 1.7 collective-permute-done.1
  169.1 4.8 %collective-permute-start.2 = (f32[4,8,512]{2,1,0:T(8,128)S(1)}, f32[4,8,512]{2,1,0:T(8,128)S(1)}, u32[]{:S(2)}, u32[]{:S(2)}) collective-permute-start(f32[4,8,512]{2,1,0:T(8,128)S(1)} %pad_maximum_fusion.1), channel_id=1, source_target_pairs={{0,16},{4,20},{8,24},{12,28},{16,0},{20,4},{24,8},{28,12},{1,17},{... | collective-permute-start | bytes 196616 | tf_op jit(solution)/shard_map/ppermute | solution.py:152
  173.9 2.0 collective-permute-done.2
  175.9 37.7 %all-to-all-done.3 = bf16[32,15,2,256]{3,2,1,0:T(2,128)(2,1)S(1)} async-done(((bf16[32,15,2,256]{3,2,1,0:T(2,128)(2,1)}), bf16[32,15,2,256]{3,2,1,0:T(2,128)(2,1)S(1)}, u32[]{:S(2)}, u32[]{:S(2)}) %all-to-all-start.3) | async-done | bytes 491552 | tf_op jit(solution)/shard_map/all_to_all | solution.py:172
  213.6 0.1 copy.10
  213.7 0.0 copy-done.2
  213.7 0.0 copy-done.3
  213.7 0.6 combine.1
  214.3 10.7 %all_to_all.33.z_ref = bf16[4,192,512]{2,1,0:T(8,128)(2,1)S(1)} all-to-all(bf16[4,192,512]{2,1,0:T(8,128)(2,1)S(1)} %combine.1), channel_id=1, replica_groups=mesh['dp'=32,'task'=8,'mp'=4] {'mp'}, dimensions={0} | all-to-all | bytes 1572864 | tf_op jit(solution)/shard_map/all_to_all | solution.py:175
  225.1 1.2 predict.1
  226.3 13.0 %all-to-all-start.5 = ((f32[8,1,192]{2,1,0:T(1,128)}), f32[8,1,192]{2,1,0:T(1,128)S(1)}, u32[]{:S(2)}, u32[]{:S(2)}) async-start(f32[8,1,192]{2,1,0:T(1,128)} %predict.1), calls=%async_computation.5 | async-start | bytes 16384 | tf_op jit(solution)/shard_map/all_to_all | solution.py:242
  239.3 0.0 copy-start.1
  239.3 2.2 copy-done.1
  241.5 2.6 %gradient.1 = bf16[192,1024]{1,0:T(8,128)(2,1)} custom-call(s32[1]{0:T(128)} %bitcast.4.me_ref, f32[8,8,512]{2,1,0:T(8,128)S(1)} %pad_maximum_fusion.side_ref, bf16[4,192,512]{2,1,0:T(8,128)(2,1)S(1)} %all_to_all.33.z_ref, bf16[8,1024,256]{2,1,0:T(8,128)(2,1)S(1)} %copy-done.1), custom_call_target="tpu_custom_call" | custom-call | flops 805306368 | bytes 4194304 | tf_op jit(solution)/shard_map/gradient/pallas_call | solution.py:228
  244.0 0.0 all-to-all-done.5
  244.1 0.7 reshape.32
  (7 shorter events, 0.1 us)
Async XLA Ops:
  94.6 27.5 %copy-start.4 = (bf16[1,2048,1024]{2,1,0:T(8,128)(2,1)S(1)}, bf16[1,2048,1024]{2,1,0:T(8,128)(2,1)}, u32[]{:S(2)}) copy-start(bf16[1,2048,1024]{2,1,0:T(8,128)(2,1)} %w_ref.1) | copy-start | bytes 12582916
  122.1 2.9 %copy-start = (bf16[8,1024,256]{2,1,0:T(8,128)(2,1)S(1)}, bf16[8,1024,256]{2,1,0:T(8,128)(2,1)}, u32[]{:S(2)}) copy-start(bf16[8,1024,256]{2,1,0:T(8,128)(2,1)} %tw_ref.3) | copy-start | bytes 12582916
  151.6 6.2 %copy-start.5 = (f32[1,1536]{1,0:T(1,128)S(1)}, f32[1,1536]{1,0:T(1,128)}, u32[]{:S(2)}) copy-start(f32[1,1536]{1,0:T(1,128)} %param.13) | copy-start | bytes 18436
  151.6 6.3 %copy-start.6 = (f32[1,256]{1,0:T(1,128)S(1)}, f32[1,256]{1,0:T(1,128)}, u32[]{:S(2)}) copy-start(f32[1,256]{1,0:T(1,128)} %param.12) | copy-start | bytes 3076
  152.2 61.5 %copy-start.2 = (s32[192,2]{0,1:T(2,128)S(1)}, s32[192,2]{0,1:T(2,128)}, u32[]{:S(2)}) copy-start(s32[192,2]{0,1:T(2,128)} %param.8) | copy-start | bytes 4612
  152.2 61.5 %copy-start.3 = (s32[192,2]{0,1:T(2,128)S(1)}, s32[192,2]{0,1:T(2,128)}, u32[]{:S(2)}) copy-start(s32[192,2]{0,1:T(2,128)} %param.9) | copy-start | bytes 4612
  153.1 60.5 %all-to-all-start.3 = ((bf16[32,15,2,256]{3,2,1,0:T(2,128)(2,1)}), bf16[32,15,2,256]{3,2,1,0:T(2,128)(2,1)S(1)}, u32[]{:S(2)}, u32[]{:S(2)}) async-start(bf16[32,15,2,256]{3,2,1,0:T(2,128)(2,1)} %reshape.28), calls=%async_computation.3 | async-start | bytes 983040 | tf_op jit(solution)/shard_map/all_to_all | solution.py:172
  158.0 6.2 %collective-permute-start = (f32[1,8,512]{2,1,0:T(8,128)S(1)}, f32[1,8,512]{2,1,0:T(8,128)S(1)}, u32[]{:S(2)}, u32[]{:S(2)}) collective-permute-start(f32[1,8,512]{2,1,0:T(8,128)S(1)} %fusion), channel_id=1, source_target_pairs={{0,4},{4,0},{8,12},{12,8},{16,20},{20,16},{24,28},{28,24},{1,5},{5... | collective-permute-start | bytes 49160 | tf_op jit(solution)/shard_map/ppermute | solution.py:152
  164.1 4.9 %collective-permute-start.1 = (f32[2,8,512]{2,1,0:T(8,128)S(1)}, f32[2,8,512]{2,1,0:T(8,128)S(1)}, u32[]{:S(2)}, u32[]{:S(2)}) collective-permute-start(f32[2,8,512]{2,1,0:T(8,128)S(1)} %pad_maximum_fusion.2), channel_id=1, source_target_pairs={{0,8},{4,12},{8,0},{12,4},{16,24},{20,28},{24,16},{28,20},{1,9},{5... | collective-permute-start | bytes 98312 | tf_op jit(solution)/shard_map/ppermute | solution.py:152
  169.1 6.8 %collective-permute-start.2 = (f32[4,8,512]{2,1,0:T(8,128)S(1)}, f32[4,8,512]{2,1,0:T(8,128)S(1)}, u32[]{:S(2)}, u32[]{:S(2)}) collective-permute-start(f32[4,8,512]{2,1,0:T(8,128)S(1)} %pad_maximum_fusion.1), channel_id=1, source_target_pairs={{0,16},{4,20},{8,24},{12,28},{16,0},{20,4},{24,8},{28,12},{1,17},{... | collective-permute-start | bytes 196616 | tf_op jit(solution)/shard_map/ppermute | solution.py:152
  226.3 17.7 %all-to-all-start.5 = ((f32[8,1,192]{2,1,0:T(1,128)}), f32[8,1,192]{2,1,0:T(1,128)S(1)}, u32[]{:S(2)}, u32[]{:S(2)}) async-start(f32[8,1,192]{2,1,0:T(1,128)} %predict.1), calls=%async_computation.5 | async-start | bytes 16384 | tf_op jit(solution)/shard_map/all_to_all | solution.py:242
  239.3 2.2 copy-start.1

commit v7 on v6

--- a/solution.py
+++ b/solution.py
@@ -34,13 +34,23 @@
     return slots
 
 
+def by_tiles(rows, out_ref):
+    groups, halves, high, wide = out_ref.shape
+    for h in range(halves):
+        out_ref[:, h] = rows[:, h * wide : (h + 1) * wide].reshape(groups, high, wide).astype(BF16)
+
+
+def sum_kernel(in_ref, out_ref):
+    by_tiles(sum(in_ref[j].astype(F32) for j in range(in_ref.shape[0])), out_ref)
+
+
 def dispatch_kernel(experts, pitch, col_ref, ids_ref, tok_ref, out_ref):
     slots = slot_rows(ids_ref, experts, pitch)
     count = ids_ref.shape[1]
     here = lax.broadcasted_iota(jnp.int32, (experts * pitch, count), 0)
     pick = functools.reduce(jnp.logical_or, [here == s for s in slots])
     pick = pick.astype(F32).astype(BF16)
-    out_ref[...] = jnp.dot(pick, tok_ref[...], preferred_element_type=F32).astype(BF16)
+    by_tiles(jnp.dot(pick, tok_ref[...], preferred_element_type=F32), out_ref)
 
 
 def units_kernel(in_ref, w_ref, hid_ref):
@@ -154,7 +164,7 @@
 
     out = pl.pallas_call(
         functools.partial(dispatch_kernel, experts, cap),
-        out_shape=jax.ShapeDtypeStruct((rows, part), BF16),
+        out_shape=jax.ShapeDtypeStruct((rows // 8, 2, 8, part // 2), BF16),
         grid_spec=pltpu.PrefetchScalarGridSpec(
             num_scalar_prefetch=1,
             grid=(1,),
@@ -162,13 +172,13 @@
                 pl.BlockSpec((top, count), lambda g, m: (0, 0)),
                 pl.BlockSpec((count, part), lambda g, m: (0, m[0])),
             ],
-            out_specs=pl.BlockSpec((rows, part), lambda g, m: (0, 0)),
+            out_specs=pl.BlockSpec((rows // 8, 2, 8, part // 2), lambda g, m: (0, 0, 0, 0)),
         ),
         name="dispatch",
     )(me, ids, tokens)
 
     def over_dp(a):
-        a = a.reshape(experts, cap, 2, a.shape[1] // 2)
+        a = a.transpose(0, 2, 1, 3).reshape(experts, cap, 2, a.shape[3])
         return lax.all_to_all(a, "dp", split_axis=0, concat_axis=0, tiled=True).reshape(rows, -1)
 
     def over_mp(a):
@@ -203,9 +213,16 @@
         ),
         name="layers",
     )(hidden, tower_weight)
-    total = jnp.sum(over_mp(outs).astype(F32), axis=0)
+    total = pl.pallas_call(
+        sum_kernel,
+        out_shape=jax.ShapeDtypeStruct((rows // 8, 2, 8, cols // 2), BF16),
+        in_specs=[VMEM],
+        out_specs=VMEM,
+        compiler_params=pltpu.CompilerParams(vmem_limit_bytes=16 << 20),
+        name="total",
+    )(over_mp(outs))
     task = lax.axis_index("task").astype(jnp.int32).reshape(1)
-    back, side, task = lax.optimization_barrier((over_dp(total.astype(BF16)), side, task))
+    back, side, task = lax.optimization_barrier((over_dp(total), side, task))
 
     z = pl.pallas_call(
         functools.partial(combine_kernel, experts, cap),

time: 245 us -> 245 us (level)
    transpose x0 -> x2, local copies, waits for them, and re-layouts: none -> 2.58 us  [over_dp(): a = a.transpose(0, 2, 1, 3).reshape(experts, cap, 2, a.shape[3])]
where the time goes in v7:
time: 245 us
  blocking collectives  153 us (62%)
  waiting for transfers between devices  42.2 us (17%)
  starting transfers between devices  31 us (13%)
  Pallas kernels  11.8 us (5%)
  local copies, waits for them, and re-layouts  5.85 us (2%)
    all_to_all x1, blocking collectives, over_dp(): lax.all_to_all(a, 'dp', split_axis=0, concat_axis=0, tiled=True)  90.6 us
    all_to_all x3, blocking collectives, over_mp(): return lax.all_to_all(a, 'mp', split_axis=0, concat_axis=0, tiled=True)  62.5 us
    all_to_all x1, waiting for transfers between devices, over_dp(): lax.all_to_all(a, 'dp', split_axis=0, concat_axis=0, tiled=True)  37.7 us
    ppermute x3, starting transfers between devices, body(): other = lax.ppermute(side, 'task', [(i, i ^ bit) for i in range(tasks)])  13.3 us
    all_to_all x1, starting transfers between devices, body(): pred = lax.all_to_all(pred, 'task', split_axis=0, concat_axis=0, tiled=True)  13 us
  transfers between devices with their start and end apart: 5, of which 4 were waited for; matrix products, arithmetic and copies ran while one was open for 0% of the time, Pallas kernels for 1%

profile of v7, /device:TPU:1, one launch (start us, length us, event | category | flops | bytes accessed | tf_op | source)
XLA Modules:
  0.0 244.9 jit_solution(7219323181247010852)
XLA Ops:
  0.6 2.2 dispatch.1
  2.8 1.4 copy.9
  4.2 90.6 %all_to_all.30 = bf16[32,15,2,256]{3,2,1,0:T(2,128)(2,1)S(1)} all-to-all(bf16[32,15,2,256]{3,2,1,0:T(2,128)(2,1)S(1)} %bitcast.25), channel_id=1, replica_groups=mesh['dp'=32,'task'=8,'mp'=4] {'dp'}, dimensions={0} | all-to-all | bytes 983040 | tf_op jit(solution)/shard_map/all_to_all | solution.py:182
  94.8 0.1 copy.11
  94.9 0.0 copy-start.4
  94.9 0.1 broadcast_in_dim.18
  95.1 27.3 %all_to_all.31.in_ref = bf16[4,480,512]{2,1,0:T(8,128)(2,1)S(1)} all-to-all(bf16[4,480,512]{2,1,0:T(8,128)(2,1)S(1)} %broadcast_in_dim.18), channel_id=1, replica_groups=mesh['dp'=32,'task'=8,'mp'=4] {'mp'}, dimensions={0} | all-to-all | bytes 3932160 | tf_op jit(solution)/shard_map/all_to_all | solution.py:185
  122.4 0.0 copy-done.4
  122.4 0.0 copy-start
  122.4 2.9 %units.1.hid_ref = bf16[480,1024]{1,0:T(8,128)(2,1)S(1)} custom-call(bf16[4,480,512]{2,1,0:T(8,128)(2,1)S(1)} %all_to_all.31.in_ref, bf16[1,2048,1024]{2,1,0:T(8,128)(2,1)S(1)} %copy-done.4), custom_call_target="tpu_custom_call" | custom-call | flops 2013265920 | bytes 7143424 | tf_op jit(solution)/shard_map/units/pallas_call | solution.py:190
  125.2 0.0 copy-done
  125.2 2.2 layers.1
  127.4 24.4 %all_to_all.32.in_ref = bf16[4,480,512]{2,1,0:T(8,128)(2,1)S(1)} all-to-all(bf16[4,480,512]{2,1,0:T(8,128)(2,1)S(1)} %layers.1), channel_id=1, replica_groups=mesh['dp'=32,'task'=8,'mp'=4] {'mp'}, dimensions={0} | all-to-all | bytes 3932160 | tf_op jit(solution)/shard_map/all_to_all | solution.py:185
  151.9 0.0 copy-start.5
  151.9 0.0 copy-start.6
  151.9 0.2 total.1
  152.1 0.0 copy-start.2
  152.1 0.0 copy-start.3
  152.2 1.2 copy.10
  153.3 4.7 %all-to-all-start.3 = ((bf16[32,15,2,256]{3,2,1,0:T(2,128)(2,1)}), bf16[32,15,2,256]{3,2,1,0:T(2,128)(2,1)S(1)}, u32[]{:S(2)}, u32[]{:S(2)}) async-start(bf16[32,15,2,256]{3,2,1,0:T(2,128)(2,1)} %bitcast.5), calls=%async_computation.3 | async-start | bytes 983040 | tf_op jit(solution)/shard_map/all_to_all | solution.py:182
  158.0 0.0 copy-done.5
  158.1 0.1 reshape.30
  158.1 0.0 copy-done.6
  158.1 5.3 %collective-permute-start = (f32[1,8,512]{2,1,0:T(8,128)S(1)}, f32[1,8,512]{2,1,0:T(8,128)S(1)}, u32[]{:S(2)}, u32[]{:S(2)}) collective-permute-start(f32[1,8,512]{2,1,0:T(8,128)S(1)} %fusion), channel_id=1, source_target_pairs={{0,4},{4,0},{8,12},{12,8},{16,20},{20,16},{24,28},{28,24},{1,5},{5... | collective-permute-start | bytes 49160 | tf_op jit(solution)/shard_map/ppermute | solution.py:162
  163.5 0.8 collective-permute-done
  164.3 3.2 %collective-permute-start.1 = (f32[2,8,512]{2,1,0:T(8,128)S(1)}, f32[2,8,512]{2,1,0:T(8,128)S(1)}, u32[]{:S(2)}, u32[]{:S(2)}) collective-permute-start(f32[2,8,512]{2,1,0:T(8,128)S(1)} %pad_maximum_fusion.2), channel_id=1, source_target_pairs={{0,8},{4,12},{8,0},{12,4},{16,24},{20,28},{24,16},{28,20},{1,9},{5... | collective-permute-start | bytes 98312 | tf_op jit(solution)/shard_map/ppermute | solution.py:162
  167.5 1.7 collective-permute-done.1
  169.3 4.8 %collective-permute-start.2 = (f32[4,8,512]{2,1,0:T(8,128)S(1)}, f32[4,8,512]{2,1,0:T(8,128)S(1)}, u32[]{:S(2)}, u32[]{:S(2)}) collective-permute-start(f32[4,8,512]{2,1,0:T(8,128)S(1)} %pad_maximum_fusion.1), channel_id=1, source_target_pairs={{0,16},{4,20},{8,24},{12,28},{16,0},{20,4},{24,8},{28,12},{1,17},{... | collective-permute-start | bytes 196616 | tf_op jit(solution)/shard_map/ppermute | solution.py:162
  174.1 2.0 collective-permute-done.2
  176.1 37.7 %all-to-all-done.3 = bf16[32,15,2,256]{3,2,1,0:T(2,128)(2,1)S(1)} async-done(((bf16[32,15,2,256]{3,2,1,0:T(2,128)(2,1)}), bf16[32,15,2,256]{3,2,1,0:T(2,128)(2,1)S(1)}, u32[]{:S(2)}, u32[]{:S(2)}) %all-to-all-start.3) | async-done | bytes 491552 | tf_op jit(solution)/shard_map/all_to_all | solution.py:182
  213.8 0.1 copy.12
  213.8 0.0 copy-done.2
  213.9 0.0 copy-done.3
  213.9 0.6 combine.1
  214.5 10.7 %all_to_all.33.z_ref = bf16[4,192,512]{2,1,0:T(8,128)(2,1)S(1)} all-to-all(bf16[4,192,512]{2,1,0:T(8,128)(2,1)S(1)} %combine.1), channel_id=1, replica_groups=mesh['dp'=32,'task'=8,'mp'=4] {'mp'}, dimensions={0} | all-to-all | bytes 1572864 | tf_op jit(solution)/shard_map/all_to_all | solution.py:185
  225.3 1.2 predict.1
  226.4 13.0 %all-to-all-start.5 = ((f32[8,1,192]{2,1,0:T(1,128)}), f32[8,1,192]{2,1,0:T(1,128)S(1)}, u32[]{:S(2)}, u32[]{:S(2)}) async-start(f32[8,1,192]{2,1,0:T(1,128)} %predict.1), calls=%async_computation.5 | async-start | bytes 16384 | tf_op jit(solution)/shard_map/all_to_all | solution.py:259
  239.5 0.0 copy-start.1
  239.5 2.2 copy-done.1
  241.6 2.6 %gradient.1 = bf16[192,1024]{1,0:T(8,128)(2,1)} custom-call(s32[1]{0:T(128)} %bitcast.8.me_ref, f32[8,8,512]{2,1,0:T(8,128)S(1)} %pad_maximum_fusion.side_ref, bf16[4,192,512]{2,1,0:T(8,128)(2,1)S(1)} %all_to_all.33.z_ref, bf16[8,1024,256]{2,1,0:T(8,128)(2,1)S(1)} %copy-done.1), custom_call_target="tpu_custom_call" | custom-call | flops 805306368 | bytes 4194304 | tf_op jit(solution)/shard_map/gradient/pallas_call | solution.py:245
  244.2 0.0 all-to-all-done.5
  244.2 0.7 reshape.32
  (7 shorter events, 0.1 us)
Async XLA Ops:
  94.9 27.5 %copy-start.4 = (bf16[1,2048,1024]{2,1,0:T(8,128)(2,1)S(1)}, bf16[1,2048,1024]{2,1,0:T(8,128)(2,1)}, u32[]{:S(2)}) copy-start(bf16[1,2048,1024]{2,1,0:T(8,128)(2,1)} %w_ref.1) | copy-start | bytes 12582916
  122.4 2.9 %copy-start = (bf16[8,1024,256]{2,1,0:T(8,128)(2,1)S(1)}, bf16[8,1024,256]{2,1,0:T(8,128)(2,1)}, u32[]{:S(2)}) copy-start(bf16[8,1024,256]{2,1,0:T(8,128)(2,1)} %tw_ref.3) | copy-start | bytes 12582916
  151.9 6.1 %copy-start.5 = (f32[1,1536]{1,0:T(1,128)S(1)}, f32[1,1536]{1,0:T(1,128)}, u32[]{:S(2)}) copy-start(f32[1,1536]{1,0:T(1,128)} %param.13) | copy-start | bytes 18436
  151.9 6.2 %copy-start.6 = (f32[1,256]{1,0:T(1,128)S(1)}, f32[1,256]{1,0:T(1,128)}, u32[]{:S(2)}) copy-start(f32[1,256]{1,0:T(1,128)} %param.12) | copy-start | bytes 3076
  152.1 61.7 %copy-start.2 = (s32[192,2]{0,1:T(2,128)S(1)}, s32[192,2]{0,1:T(2,128)}, u32[]{:S(2)}) copy-start(s32[192,2]{0,1:T(2,128)} %param.8) | copy-start | bytes 4612
  152.1 61.7 %copy-start.3 = (s32[192,2]{0,1:T(2,128)S(1)}, s32[192,2]{0,1:T(2,128)}, u32[]{:S(2)}) copy-start(s32[192,2]{0,1:T(2,128)} %param.9) | copy-start | bytes 4612
  153.3 60.4 %all-to-all-start.3 = ((bf16[32,15,2,256]{3,2,1,0:T(2,128)(2,1)}), bf16[32,15,2,256]{3,2,1,0:T(2,128)(2,1)S(1)}, u32[]{:S(2)}, u32[]{:S(2)}) async-start(bf16[32,15,2,256]{3,2,1,0:T(2,128)(2,1)} %bitcast.5), calls=%async_computation.3 | async-start | bytes 983040 | tf_op jit(solution)/shard_map/all_to_all | solution.py:182
  158.1 6.2 %collective-permute-start = (f32[1,8,512]{2,1,0:T(8,128)S(1)}, f32[1,8,512]{2,1,0:T(8,128)S(1)}, u32[]{:S(2)}, u32[]{:S(2)}) collective-permute-start(f32[1,8,512]{2,1,0:T(8,128)S(1)} %fusion), channel_id=1, source_target_pairs={{0,4},{4,0},{8,12},{12,8},{16,20},{20,16},{24,28},{28,24},{1,5},{5... | collective-permute-start | bytes 49160 | tf_op jit(solution)/shard_map/ppermute | solution.py:162
  164.3 4.9 %collective-permute-start.1 = (f32[2,8,512]{2,1,0:T(8,128)S(1)}, f32[2,8,512]{2,1,0:T(8,128)S(1)}, u32[]{:S(2)}, u32[]{:S(2)}) collective-permute-start(f32[2,8,512]{2,1,0:T(8,128)S(1)} %pad_maximum_fusion.2), channel_id=1, source_target_pairs={{0,8},{4,12},{8,0},{12,4},{16,24},{20,28},{24,16},{28,20},{1,9},{5... | collective-permute-start | bytes 98312 | tf_op jit(solution)/shard_map/ppermute | solution.py:162
  169.3 6.8 %collective-permute-start.2 = (f32[4,8,512]{2,1,0:T(8,128)S(1)}, f32[4,8,512]{2,1,0:T(8,128)S(1)}, u32[]{:S(2)}, u32[]{:S(2)}) collective-permute-start(f32[4,8,512]{2,1,0:T(8,128)S(1)} %pad_maximum_fusion.1), channel_id=1, source_target_pairs={{0,16},{4,20},{8,24},{12,28},{16,0},{20,4},{24,8},{28,12},{1,17},{... | collective-permute-start | bytes 196616 | tf_op jit(solution)/shard_map/ppermute | solution.py:162
  226.4 17.7 %all-to-all-start.5 = ((f32[8,1,192]{2,1,0:T(1,128)}), f32[8,1,192]{2,1,0:T(1,128)S(1)}, u32[]{:S(2)}, u32[]{:S(2)}) async-start(f32[8,1,192]{2,1,0:T(1,128)} %predict.1), calls=%async_computation.5 | async-start | bytes 16384 | tf_op jit(solution)/shard_map/all_to_all | solution.py:259
  239.5 2.2 copy-start.1

commit v8 on v7

--- a/solution.py
+++ b/solution.py
@@ -174,6 +174,7 @@
             ],
             out_specs=pl.BlockSpec((rows // 8, 2, 8, part // 2), lambda g, m: (0, 0, 0, 0)),
         ),
+        compiler_params=pltpu.CompilerParams(vmem_limit_bytes=16 << 20),
         name="dispatch",
     )(me, ids, tokens)
 

time: 245 us -> 245 us (level)
  no operation moved by 1% of the time
where the time goes in v8:
time: 245 us; the launch traced here: 244 us
  blocking collectives  153 us (62%)
  waiting for transfers between devices  42.2 us (17%)
  starting transfers between devices  31 us (13%)
  Pallas kernels  10.1 us (4%)
  local copies, waits for them, and re-layouts  6.65 us (3%)
    all_to_all x1, blocking collectives, over_dp(): lax.all_to_all(a, 'dp', split_axis=0, concat_axis=0, tiled=True)  90.6 us
    all_to_all x3, blocking collectives, over_mp(): return lax.all_to_all(a, 'mp', split_axis=0, concat_axis=0, tiled=True)  62.4 us
    all_to_all x1, waiting for transfers between devices, over_dp(): lax.all_to_all(a, 'dp', split_axis=0, concat_axis=0, tiled=True)  37.7 us
    ppermute x3, starting transfers between devices, body(): other = lax.ppermute(side, 'task', [(i, i ^ bit) for i in range(tasks)])  13.3 us
    all_to_all x1, starting transfers between devices, body(): pred = lax.all_to_all(pred, 'task', split_axis=0, concat_axis=0, tiled=True)  13 us
  transfers between devices with their start and end apart: 5, of which 4 were waited for; matrix products, arithmetic and copies ran while one was open for 0% of the time, Pallas kernels for 1%

profile of v8, /device:TPU:1, one launch (start us, length us, event | category | flops | bytes accessed | tf_op | source)
XLA Modules:
  0.0 244.0 jit_solution(8708760482138037731)
XLA Ops:
  0.6 0.0 copy-start.2
  0.6 1.1 copy-done.2
  1.8 0.0 copy-start.3
  1.8 0.7 copy-done.3
  2.4 0.4 dispatch.1
  2.9 0.4 copy.9
  3.3 90.6 %all_to_all.30 = bf16[32,15,2,256]{3,2,1,0:T(2,128)(2,1)S(1)} all-to-all(bf16[32,15,2,256]{3,2,1,0:T(2,128)(2,1)S(1)} %bitcast.25), channel_id=1, replica_groups=mesh['dp'=32,'task'=8,'mp'=4] {'dp'}, dimensions={0} | all-to-all | bytes 983040 | tf_op jit(solution)/shard_map/all_to_all | solution.py:183
  93.9 0.1 copy.11
  94.0 0.0 copy-start.6
  94.0 0.1 broadcast_in_dim.18
  94.1 27.3 %all_to_all.31.in_ref = bf16[4,480,512]{2,1,0:T(8,128)(2,1)S(1)} all-to-all(bf16[4,480,512]{2,1,0:T(8,128)(2,1)S(1)} %broadcast_in_dim.18), channel_id=1, replica_groups=mesh['dp'=32,'task'=8,'mp'=4] {'mp'}, dimensions={0} | all-to-all | bytes 3932160 | tf_op jit(solution)/shard_map/all_to_all | solution.py:186
  121.4 0.0 copy-done.6
  121.4 0.0 copy-start
  121.4 2.9 %units.1.hid_ref = bf16[480,1024]{1,0:T(8,128)(2,1)S(1)} custom-call(bf16[4,480,512]{2,1,0:T(8,128)(2,1)S(1)} %all_to_all.31.in_ref, bf16[1,2048,1024]{2,1,0:T(8,128)(2,1)S(1)} %copy-done.6), custom_call_target="tpu_custom_call" | custom-call | flops 2013265920 | bytes 7143424 | tf_op jit(solution)/shard_map/units/pallas_call | solution.py:191
  124.3 0.0 copy-done
  124.3 2.2 layers.1
  126.5 24.4 %all_to_all.32.in_ref = bf16[4,480,512]{2,1,0:T(8,128)(2,1)S(1)} all-to-all(bf16[4,480,512]{2,1,0:T(8,128)(2,1)S(1)} %layers.1), channel_id=1, replica_groups=mesh['dp'=32,'task'=8,'mp'=4] {'mp'}, dimensions={0} | all-to-all | bytes 3932160 | tf_op jit(solution)/shard_map/all_to_all | solution.py:186
  150.9 0.0 copy-start.7
  150.9 0.0 copy-start.8
  150.9 0.2 total.1
  151.2 0.0 copy-start.4
  151.2 0.0 copy-start.5
  151.2 1.2 copy.10
  152.4 4.7 %all-to-all-start.3 = ((bf16[32,15,2,256]{3,2,1,0:T(2,128)(2,1)}), bf16[32,15,2,256]{3,2,1,0:T(2,128)(2,1)S(1)}, u32[]{:S(2)}, u32[]{:S(2)}) async-start(bf16[32,15,2,256]{3,2,1,0:T(2,128)(2,1)} %bitcast.5), calls=%async_computation.3 | async-start | bytes 983040 | tf_op jit(solution)/shard_map/all_to_all | solution.py:183
  157.1 0.0 copy-done.7
  157.1 0.1 reshape.30
  157.2 0.0 copy-done.8
  157.2 5.3 %collective-permute-start = (f32[1,8,512]{2,1,0:T(8,128)S(1)}, f32[1,8,512]{2,1,0:T(8,128)S(1)}, u32[]{:S(2)}, u32[]{:S(2)}) collective-permute-start(f32[1,8,512]{2,1,0:T(8,128)S(1)} %fusion), channel_id=1, source_target_pairs={{0,4},{4,0},{8,12},{12,8},{16,20},{20,16},{24,28},{28,24},{1,5},{5... | collective-permute-start | bytes 49160 | tf_op jit(solution)/shard_map/ppermute | solution.py:162
  162.6 0.8 collective-permute-done
  163.4 3.2 %collective-permute-start.1 = (f32[2,8,512]{2,1,0:T(8,128)S(1)}, f32[2,8,512]{2,1,0:T(8,128)S(1)}, u32[]{:S(2)}, u32[]{:S(2)}) collective-permute-start(f32[2,8,512]{2,1,0:T(8,128)S(1)} %pad_maximum_fusion.2), channel_id=1, source_target_pairs={{0,8},{4,12},{8,0},{12,4},{16,24},{20,28},{24,16},{28,20},{1,9},{5... | collective-permute-start | bytes 98312 | tf_op jit(solution)/shard_map/ppermute | solution.py:162
  166.6 1.7 collective-permute-done.1
  168.3 4.8 %collective-permute-start.2 = (f32[4,8,512]{2,1,0:T(8,128)S(1)}, f32[4,8,512]{2,1,0:T(8,128)S(1)}, u32[]{:S(2)}, u32[]{:S(2)}) collective-permute-start(f32[4,8,512]{2,1,0:T(8,128)S(1)} %pad_maximum_fusion.1), channel_id=1, source_target_pairs={{0,16},{4,20},{8,24},{12,28},{16,0},{20,4},{24,8},{28,12},{1,17},{... | collective-permute-start | bytes 196616 | tf_op jit(solution)/shard_map/ppermute | solution.py:162
  173.2 2.0 collective-permute-done.2
  175.2 37.7 %all-to-all-done.3 = bf16[32,15,2,256]{3,2,1,0:T(2,128)(2,1)S(1)} async-done(((bf16[32,15,2,256]{3,2,1,0:T(2,128)(2,1)}), bf16[32,15,2,256]{3,2,1,0:T(2,128)(2,1)S(1)}, u32[]{:S(2)}, u32[]{:S(2)}) %all-to-all-start.3) | async-done | bytes 491552 | tf_op jit(solution)/shard_map/all_to_all | solution.py:183
  212.9 0.1 copy.12
  213.0 0.0 copy-done.4
  213.0 0.0 copy-done.5
  213.0 0.6 combine.1
  213.6 10.7 %all_to_all.33.z_ref = bf16[4,192,512]{2,1,0:T(8,128)(2,1)S(1)} all-to-all(bf16[4,192,512]{2,1,0:T(8,128)(2,1)S(1)} %combine.1), channel_id=1, replica_groups=mesh['dp'=32,'task'=8,'mp'=4] {'mp'}, dimensions={0} | all-to-all | bytes 1572864 | tf_op jit(solution)/shard_map/all_to_all | solution.py:186
  224.4 1.2 predict.1
  225.6 13.0 %all-to-all-start.5 = ((f32[8,1,192]{2,1,0:T(1,128)}), f32[8,1,192]{2,1,0:T(1,128)S(1)}, u32[]{:S(2)}, u32[]{:S(2)}) async-start(f32[8,1,192]{2,1,0:T(1,128)} %predict.1), calls=%async_computation.5 | async-start | bytes 16384 | tf_op jit(solution)/shard_map/all_to_all | solution.py:260
  238.5 0.0 copy-start.1
  238.5 2.2 copy-done.1
  240.7 2.6 %gradient.1 = bf16[192,1024]{1,0:T(8,128)(2,1)} custom-call(s32[1]{0:T(128)} %bitcast.8.me_ref, f32[8,8,512]{2,1,0:T(8,128)S(1)} %pad_maximum_fusion.side_ref, bf16[4,192,512]{2,1,0:T(8,128)(2,1)S(1)} %all_to_all.33.z_ref, bf16[8,1024,256]{2,1,0:T(8,128)(2,1)S(1)} %copy-done.1), custom_call_target="tpu_custom_call" | custom-call | flops 805306368 | bytes 4194304 | tf_op jit(solution)/shard_map/gradient/pallas_call | solution.py:246
  243.3 0.0 all-to-all-done.5
  243.3 0.7 reshape.32
  (7 shorter events, 0.1 us)
Async XLA Ops:
  0.6 1.1 copy-start.2
  1.8 0.7 copy-start.3
  94.0 27.4 %copy-start.6 = (bf16[1,2048,1024]{2,1,0:T(8,128)(2,1)S(1)}, bf16[1,2048,1024]{2,1,0:T(8,128)(2,1)}, u32[]{:S(2)}) copy-start(bf16[1,2048,1024]{2,1,0:T(8,128)(2,1)} %w_ref.1) | copy-start | bytes 12582916
  121.4 2.9 %copy-start = (bf16[8,1024,256]{2,1,0:T(8,128)(2,1)S(1)}, bf16[8,1024,256]{2,1,0:T(8,128)(2,1)}, u32[]{:S(2)}) copy-start(bf16[8,1024,256]{2,1,0:T(8,128)(2,1)} %tw_ref.3) | copy-start | bytes 12582916
  150.9 6.2 %copy-start.7 = (f32[1,1536]{1,0:T(1,128)S(1)}, f32[1,1536]{1,0:T(1,128)}, u32[]{:S(2)}) copy-start(f32[1,1536]{1,0:T(1,128)} %param.13) | copy-start | bytes 18436
  150.9 6.3 %copy-start.8 = (f32[1,256]{1,0:T(1,128)S(1)}, f32[1,256]{1,0:T(1,128)}, u32[]{:S(2)}) copy-start(f32[1,256]{1,0:T(1,128)} %param.12) | copy-start | bytes 3076
  151.2 61.8 %copy-start.4 = (s32[192,2]{0,1:T(2,128)S(1)}, s32[192,2]{0,1:T(2,128)}, u32[]{:S(2)}) copy-start(s32[192,2]{0,1:T(2,128)} %param.8) | copy-start | bytes 4612
  151.2 61.8 %copy-start.5 = (s32[192,2]{0,1:T(2,128)S(1)}, s32[192,2]{0,1:T(2,128)}, u32[]{:S(2)}) copy-start(s32[192,2]{0,1:T(2,128)} %param.9) | copy-start | bytes 4612
  152.4 60.5 %all-to-all-start.3 = ((bf16[32,15,2,256]{3,2,1,0:T(2,128)(2,1)}), bf16[32,15,2,256]{3,2,1,0:T(2,128)(2,1)S(1)}, u32[]{:S(2)}, u32[]{:S(2)}) async-start(bf16[32,15,2,256]{3,2,1,0:T(2,128)(2,1)} %bitcast.5), calls=%async_computation.3 | async-start | bytes 983040 | tf_op jit(solution)/shard_map/all_to_all | solution.py:183
  157.2 6.2 %collective-permute-start = (f32[1,8,512]{2,1,0:T(8,128)S(1)}, f32[1,8,512]{2,1,0:T(8,128)S(1)}, u32[]{:S(2)}, u32[]{:S(2)}) collective-permute-start(f32[1,8,512]{2,1,0:T(8,128)S(1)} %fusion), channel_id=1, source_target_pairs={{0,4},{4,0},{8,12},{12,8},{16,20},{20,16},{24,28},{28,24},{1,5},{5... | collective-permute-start | bytes 49160 | tf_op jit(solution)/shard_map/ppermute | solution.py:162
  163.4 4.9 %collective-permute-start.1 = (f32[2,8,512]{2,1,0:T(8,128)S(1)}, f32[2,8,512]{2,1,0:T(8,128)S(1)}, u32[]{:S(2)}, u32[]{:S(2)}) collective-permute-start(f32[2,8,512]{2,1,0:T(8,128)S(1)} %pad_maximum_fusion.2), channel_id=1, source_target_pairs={{0,8},{4,12},{8,0},{12,4},{16,24},{20,28},{24,16},{28,20},{1,9},{5... | collective-permute-start | bytes 98312 | tf_op jit(solution)/shard_map/ppermute | solution.py:162
  168.3 6.8 %collective-permute-start.2 = (f32[4,8,512]{2,1,0:T(8,128)S(1)}, f32[4,8,512]{2,1,0:T(8,128)S(1)}, u32[]{:S(2)}, u32[]{:S(2)}) collective-permute-start(f32[4,8,512]{2,1,0:T(8,128)S(1)} %pad_maximum_fusion.1), channel_id=1, source_target_pairs={{0,16},{4,20},{8,24},{12,28},{16,0},{20,4},{24,8},{28,12},{1,17},{... | collective-permute-start | bytes 196616 | tf_op jit(solution)/shard_map/ppermute | solution.py:162
  225.6 17.7 %all-to-all-start.5 = ((f32[8,1,192]{2,1,0:T(1,128)}), f32[8,1,192]{2,1,0:T(1,128)S(1)}, u32[]{:S(2)}, u32[]{:S(2)}) async-start(f32[8,1,192]{2,1,0:T(1,128)} %predict.1), calls=%async_computation.5 | async-start | bytes 16384 | tf_op jit(solution)/shard_map/all_to_all | solution.py:260
  238.5 2.2 copy-start.1

commit v9 on v8

--- a/solution.py
+++ b/solution.py
@@ -44,7 +44,7 @@
     by_tiles(sum(in_ref[j].astype(F32) for j in range(in_ref.shape[0])), out_ref)
 
 
-def dispatch_kernel(experts, pitch, col_ref, ids_ref, tok_ref, out_ref):
+def dispatch_kernel(experts, pitch, ids_ref, tok_ref, out_ref):
     slots = slot_rows(ids_ref, experts, pitch)
     count = ids_ref.shape[1]
     here = lax.broadcasted_iota(jnp.int32, (experts * pitch, count), 0)
@@ -146,7 +146,6 @@
     cols = towers * tile // n
     cap = max(2, 5 * count * top // (4 * experts))
     rows = experts * cap
-    me = lax.axis_index("mp").astype(jnp.int32).reshape(1)
     ids = expert_ids.T
     levels = gate_levels.T
 
@@ -165,18 +164,11 @@
     out = pl.pallas_call(
         functools.partial(dispatch_kernel, experts, cap),
         out_shape=jax.ShapeDtypeStruct((rows // 8, 2, 8, part // 2), BF16),
-        grid_spec=pltpu.PrefetchScalarGridSpec(
-            num_scalar_prefetch=1,
-            grid=(1,),
-            in_specs=[
-                pl.BlockSpec((top, count), lambda g, m: (0, 0)),
-                pl.BlockSpec((count, part), lambda g, m: (0, m[0])),
-            ],
-            out_specs=pl.BlockSpec((rows // 8, 2, 8, part // 2), lambda g, m: (0, 0, 0, 0)),
-        ),
+        in_specs=[VMEM] * 2,
+        out_specs=VMEM,
         compiler_params=pltpu.CompilerParams(vmem_limit_bytes=16 << 20),
         name="dispatch",
-    )(me, ids, tokens)
+    )(ids, lax.dynamic_slice_in_dim(tokens, lax.axis_index("mp") * part, part, axis=1))
 
     def over_dp(a):
         a = a.transpose(0, 2, 1, 3).reshape(experts, cap, 2, a.shape[3])

time: 245 us -> 245 us (level)
  no operation moved by 1% of the time
where the time goes in v9:
time: 245 us; the launch traced here: 244 us
  blocking collectives  153 us (62%)
  waiting for transfers between devices  42.2 us (17%)
  starting transfers between devices  31.1 us (13%)
  Pallas kernels  10.1 us (4%)
  local copies, waits for them, and re-layouts  6.66 us (3%)
    all_to_all x1, blocking collectives, over_dp(): lax.all_to_all(a, 'dp', split_axis=0, concat_axis=0, tiled=True)  90.6 us
    all_to_all x3, blocking collectives, over_mp(): return lax.all_to_all(a, 'mp', split_axis=0, concat_axis=0, tiled=True)  62.4 us
    all_to_all x1, waiting for transfers between devices, over_dp(): lax.all_to_all(a, 'dp', split_axis=0, concat_axis=0, tiled=True)  37.7 us
    ppermute x3, starting transfers between devices, body(): other = lax.ppermute(side, 'task', [(i, i ^ bit) for i in range(tasks)])  13.4 us
    all_to_all x1, starting transfers between devices, body(): pred = lax.all_to_all(pred, 'task', split_axis=0, concat_axis=0, tiled=True)  13 us
  transfers between devices with their start and end apart: 5, of which 4 were waited for; matrix products, arithmetic and copies ran while one was open for 0% of the time, Pallas kernels for 1%

profile of v9, /device:TPU:1, one launch (start us, length us, event | category | flops | bytes accessed | tf_op | source)
XLA Modules:
  0.0 244.0 jit_solution(6264052710727658102)
XLA Ops:
  0.6 0.0 copy-start
  0.6 1.1 copy-done
  1.8 0.0 copy-start.3
  1.8 0.7 copy-done.3
  2.5 0.4 dispatch.1
  2.9 0.4 copy.9
  3.3 90.6 %all_to_all.30 = bf16[32,15,2,256]{3,2,1,0:T(2,128)(2,1)S(1)} all-to-all(bf16[32,15,2,256]{3,2,1,0:T(2,128)(2,1)S(1)} %bitcast.24), channel_id=1, replica_groups=mesh['dp'=32,'task'=8,'mp'=4] {'dp'}, dimensions={0} | all-to-all | bytes 983040 | tf_op jit(solution)/shard_map/all_to_all | solution.py:175
  93.9 0.1 copy.11
  94.0 0.0 copy-start.6
  94.0 0.1 broadcast_in_dim.18
  94.2 27.3 %all_to_all.31.in_ref = bf16[4,480,512]{2,1,0:T(8,128)(2,1)S(1)} all-to-all(bf16[4,480,512]{2,1,0:T(8,128)(2,1)S(1)} %broadcast_in_dim.18), channel_id=1, replica_groups=mesh['dp'=32,'task'=8,'mp'=4] {'mp'}, dimensions={0} | all-to-all | bytes 3932160 | tf_op jit(solution)/shard_map/all_to_all | solution.py:178
  121.4 0.0 copy-done.6
  121.4 0.0 copy-start.1
  121.4 2.9 %units.1.hid_ref = bf16[480,1024]{1,0:T(8,128)(2,1)S(1)} custom-call(bf16[4,480,512]{2,1,0:T(8,128)(2,1)S(1)} %all_to_all.31.in_ref, bf16[1,2048,1024]{2,1,0:T(8,128)(2,1)S(1)} %copy-done.6), custom_call_target="tpu_custom_call" | custom-call | flops 2013265920 | bytes 7143424 | tf_op jit(solution)/shard_map/units/pallas_call | solution.py:183
  124.3 0.0 copy-done.1
  124.3 2.2 layers.1
  126.5 24.4 %all_to_all.32.in_ref = bf16[4,480,512]{2,1,0:T(8,128)(2,1)S(1)} all-to-all(bf16[4,480,512]{2,1,0:T(8,128)(2,1)S(1)} %layers.1), channel_id=1, replica_groups=mesh['dp'=32,'task'=8,'mp'=4] {'mp'}, dimensions={0} | all-to-all | bytes 3932160 | tf_op jit(solution)/shard_map/all_to_all | solution.py:178
  150.9 0.0 copy-start.7
  150.9 0.0 copy-start.8
  150.9 0.2 total.1
  151.2 0.0 copy-start.4
  151.2 0.0 copy-start.5
  151.2 1.2 copy.10
  152.4 4.7 %all-to-all-start.3 = ((bf16[32,15,2,256]{3,2,1,0:T(2,128)(2,1)}), bf16[32,15,2,256]{3,2,1,0:T(2,128)(2,1)S(1)}, u32[]{:S(2)}, u32[]{:S(2)}) async-start(bf16[32,15,2,256]{3,2,1,0:T(2,128)(2,1)} %bitcast.4), calls=%async_computation.3 | async-start | bytes 983040 | tf_op jit(solution)/shard_map/all_to_all | solution.py:175
  157.1 0.0 copy-done.7
  157.2 0.1 reshape.26
  157.2 0.0 copy-done.8
  157.2 5.3 %collective-permute-start = (f32[1,8,512]{2,1,0:T(8,128)S(1)}, f32[1,8,512]{2,1,0:T(8,128)S(1)}, u32[]{:S(2)}, u32[]{:S(2)}) collective-permute-start(f32[1,8,512]{2,1,0:T(8,128)S(1)} %fusion), channel_id=1, source_target_pairs={{0,4},{4,0},{8,12},{12,8},{16,20},{20,16},{24,28},{28,24},{1,5},{5... | collective-permute-start | bytes 49160 | tf_op jit(solution)/shard_map/ppermute | solution.py:161
  162.6 0.8 collective-permute-done
  163.4 3.2 %collective-permute-start.1 = (f32[2,8,512]{2,1,0:T(8,128)S(1)}, f32[2,8,512]{2,1,0:T(8,128)S(1)}, u32[]{:S(2)}, u32[]{:S(2)}) collective-permute-start(f32[2,8,512]{2,1,0:T(8,128)S(1)} %pad_maximum_fusion.2), channel_id=1, source_target_pairs={{0,8},{4,12},{8,0},{12,4},{16,24},{20,28},{24,16},{28,20},{1,9},{5... | collective-permute-start | bytes 98312 | tf_op jit(solution)/shard_map/ppermute | solution.py:161
  166.6 1.7 collective-permute-done.1
  168.4 4.8 %collective-permute-start.2 = (f32[4,8,512]{2,1,0:T(8,128)S(1)}, f32[4,8,512]{2,1,0:T(8,128)S(1)}, u32[]{:S(2)}, u32[]{:S(2)}) collective-permute-start(f32[4,8,512]{2,1,0:T(8,128)S(1)} %pad_maximum_fusion.1), channel_id=1, source_target_pairs={{0,16},{4,20},{8,24},{12,28},{16,0},{20,4},{24,8},{28,12},{1,17},{... | collective-permute-start | bytes 196616 | tf_op jit(solution)/shard_map/ppermute | solution.py:161
  173.2 2.0 collective-permute-done.2
  175.2 37.7 %all-to-all-done.3 = bf16[32,15,2,256]{3,2,1,0:T(2,128)(2,1)S(1)} async-done(((bf16[32,15,2,256]{3,2,1,0:T(2,128)(2,1)}), bf16[32,15,2,256]{3,2,1,0:T(2,128)(2,1)S(1)}, u32[]{:S(2)}, u32[]{:S(2)}) %all-to-all-start.3) | async-done | bytes 491552 | tf_op jit(solution)/shard_map/all_to_all | solution.py:175
  212.9 0.1 copy.12
  213.0 0.0 copy-done.4
  213.0 0.0 copy-done.5
  213.0 0.6 combine.1
  213.6 10.7 %all_to_all.33.z_ref = bf16[4,192,512]{2,1,0:T(8,128)(2,1)S(1)} all-to-all(bf16[4,192,512]{2,1,0:T(8,128)(2,1)S(1)} %combine.1), channel_id=1, replica_groups=mesh['dp'=32,'task'=8,'mp'=4] {'mp'}, dimensions={0} | all-to-all | bytes 1572864 | tf_op jit(solution)/shard_map/all_to_all | solution.py:178
  224.4 1.2 predict.1
  225.6 13.0 %all-to-all-start.5 = ((f32[8,1,192]{2,1,0:T(1,128)}), f32[8,1,192]{2,1,0:T(1,128)S(1)}, u32[]{:S(2)}, u32[]{:S(2)}) async-start(f32[8,1,192]{2,1,0:T(1,128)} %predict.1), calls=%async_computation.5 | async-start | bytes 16384 | tf_op jit(solution)/shard_map/all_to_all | solution.py:252
  238.6 0.0 copy-start.2
  238.6 2.2 copy-done.2
  240.8 2.6 %gradient.1 = bf16[192,1024]{1,0:T(8,128)(2,1)} custom-call(s32[1]{0:T(128)} %bitcast.7.me_ref, f32[8,8,512]{2,1,0:T(8,128)S(1)} %pad_maximum_fusion.side_ref, bf16[4,192,512]{2,1,0:T(8,128)(2,1)S(1)} %all_to_all.33.z_ref, bf16[8,1024,256]{2,1,0:T(8,128)(2,1)S(1)} %copy-done.2), custom_call_target="tpu_custom_call" | custom-call | flops 805306368 | bytes 4194304 | tf_op jit(solution)/shard_map/gradient/pallas_call | solution.py:238
  243.3 0.0 all-to-all-done.5
  243.3 0.7 reshape.28
  (8 shorter events, 0.1 us)
Async XLA Ops:
  0.6 1.1 copy-start
  1.8 0.7 copy-start.3
  94.0 27.4 %copy-start.6 = (bf16[1,2048,1024]{2,1,0:T(8,128)(2,1)S(1)}, bf16[1,2048,1024]{2,1,0:T(8,128)(2,1)}, u32[]{:S(2)}) copy-start(bf16[1,2048,1024]{2,1,0:T(8,128)(2,1)} %w_ref.1) | copy-start | bytes 12582916
  121.4 2.9 %copy-start.1 = (bf16[8,1024,256]{2,1,0:T(8,128)(2,1)S(1)}, bf16[8,1024,256]{2,1,0:T(8,128)(2,1)}, u32[]{:S(2)}) copy-start(bf16[8,1024,256]{2,1,0:T(8,128)(2,1)} %tw_ref.3) | copy-start | bytes 12582916
  150.9 6.2 %copy-start.7 = (f32[1,1536]{1,0:T(1,128)S(1)}, f32[1,1536]{1,0:T(1,128)}, u32[]{:S(2)}) copy-start(f32[1,1536]{1,0:T(1,128)} %param.13) | copy-start | bytes 18436
  150.9 6.3 %copy-start.8 = (f32[1,256]{1,0:T(1,128)S(1)}, f32[1,256]{1,0:T(1,128)}, u32[]{:S(2)}) copy-start(f32[1,256]{1,0:T(1,128)} %param.12) | copy-start | bytes 3076
  151.2 61.8 %copy-start.4 = (s32[192,2]{0,1:T(2,128)S(1)}, s32[192,2]{0,1:T(2,128)}, u32[]{:S(2)}) copy-start(s32[192,2]{0,1:T(2,128)} %param.8) | copy-start | bytes 4612
  151.2 61.8 %copy-start.5 = (s32[192,2]{0,1:T(2,128)S(1)}, s32[192,2]{0,1:T(2,128)}, u32[]{:S(2)}) copy-start(s32[192,2]{0,1:T(2,128)} %param.9) | copy-start | bytes 4612
  152.4 60.5 %all-to-all-start.3 = ((bf16[32,15,2,256]{3,2,1,0:T(2,128)(2,1)}), bf16[32,15,2,256]{3,2,1,0:T(2,128)(2,1)S(1)}, u32[]{:S(2)}, u32[]{:S(2)}) async-start(bf16[32,15,2,256]{3,2,1,0:T(2,128)(2,1)} %bitcast.4), calls=%async_computation.3 | async-start | bytes 983040 | tf_op jit(solution)/shard_map/all_to_all | solution.py:175
  157.2 6.2 %collective-permute-start = (f32[1,8,512]{2,1,0:T(8,128)S(1)}, f32[1,8,512]{2,1,0:T(8,128)S(1)}, u32[]{:S(2)}, u32[]{:S(2)}) collective-permute-start(f32[1,8,512]{2,1,0:T(8,128)S(1)} %fusion), channel_id=1, source_target_pairs={{0,4},{4,0},{8,12},{12,8},{16,20},{20,16},{24,28},{28,24},{1,5},{5... | collective-permute-start | bytes 49160 | tf_op jit(solution)/shard_map/ppermute | solution.py:161
  163.4 4.9 %collective-permute-start.1 = (f32[2,8,512]{2,1,0:T(8,128)S(1)}, f32[2,8,512]{2,1,0:T(8,128)S(1)}, u32[]{:S(2)}, u32[]{:S(2)}) collective-permute-start(f32[2,8,512]{2,1,0:T(8,128)S(1)} %pad_maximum_fusion.2), channel_id=1, source_target_pairs={{0,8},{4,12},{8,0},{12,4},{16,24},{20,28},{24,16},{28,20},{1,9},{5... | collective-permute-start | bytes 98312 | tf_op jit(solution)/shard_map/ppermute | solution.py:161
  168.4 6.8 %collective-permute-start.2 = (f32[4,8,512]{2,1,0:T(8,128)S(1)}, f32[4,8,512]{2,1,0:T(8,128)S(1)}, u32[]{:S(2)}, u32[]{:S(2)}) collective-permute-start(f32[4,8,512]{2,1,0:T(8,128)S(1)} %pad_maximum_fusion.1), channel_id=1, source_target_pairs={{0,16},{4,20},{8,24},{12,28},{16,0},{20,4},{24,8},{28,12},{1,17},{... | collective-permute-start | bytes 196616 | tf_op jit(solution)/shard_map/ppermute | solution.py:161
  225.6 17.7 %all-to-all-start.5 = ((f32[8,1,192]{2,1,0:T(1,128)}), f32[8,1,192]{2,1,0:T(1,128)S(1)}, u32[]{:S(2)}, u32[]{:S(2)}) async-start(f32[8,1,192]{2,1,0:T(1,128)} %predict.1), calls=%async_computation.5 | async-start | bytes 16384 | tf_op jit(solution)/shard_map/all_to_all | solution.py:252
  238.6 2.2 copy-start.2

commit v10 on v8

--- a/solution.py
+++ b/solution.py
@@ -57,9 +57,8 @@
     n, _, depth = in_ref.shape
     tile = 256
 
-    @pl.loop(0, w_ref.shape[2] // tile)
-    def _(c):
-        cols = pl.ds(pl.multiple_of(c * tile, tile), tile)
+    for c in range(w_ref.shape[2] // tile):
+        cols = slice(c * tile, (c + 1) * tile)
         total = None
         for j in range(n):
             part = jnp.dot(

time: 245 us -> 244 us (level)
  no operation moved by 1% of the time
where the time goes in v10:
time: 244 us
  blocking collectives  153 us (63%)
  waiting for transfers between devices  42.2 us (17%)
  starting transfers between devices  31.1 us (13%)
  Pallas kernels  9.64 us (4%)
  local copies, waits for them, and re-layouts  6.65 us (3%)
    all_to_all x1, blocking collectives, over_dp(): lax.all_to_all(a, 'dp', split_axis=0, concat_axis=0, tiled=True)  90.6 us
    all_to_all x3, blocking collectives, over_mp(): return lax.all_to_all(a, 'mp', split_axis=0, concat_axis=0, tiled=True)  62.4 us
    all_to_all x1, waiting for transfers between devices, over_dp(): lax.all_to_all(a, 'dp', split_axis=0, concat_axis=0, tiled=True)  37.7 us
    ppermute x3, starting transfers between devices, body(): other = lax.ppermute(side, 'task', [(i, i ^ bit) for i in range(tasks)])  13.3 us
    all_to_all x1, starting transfers between devices, body(): pred = lax.all_to_all(pred, 'task', split_axis=0, concat_axis=0, tiled=True)  13 us
  transfers between devices with their start and end apart: 5, of which 4 were waited for; matrix products, arithmetic and copies ran while one was open for 0% of the time, Pallas kernels for 1%

profile of v10, /device:TPU:1, one launch (start us, length us, event | category | flops | bytes accessed | tf_op | source)
XLA Modules:
  0.0 243.5 jit_solution(9182310458131305795)
XLA Ops:
  0.6 0.0 copy-start.2
  0.6 1.1 copy-done.2
  1.8 0.0 copy-start.3
  1.8 0.7 copy-done.3
  2.4 0.4 dispatch.1
  2.9 0.4 copy.9
  3.3 90.6 %all_to_all.30 = bf16[32,15,2,256]{3,2,1,0:T(2,128)(2,1)S(1)} all-to-all(bf16[32,15,2,256]{3,2,1,0:T(2,128)(2,1)S(1)} %bitcast.25), channel_id=1, replica_groups=mesh['dp'=32,'task'=8,'mp'=4] {'dp'}, dimensions={0} | all-to-all | bytes 983040 | tf_op jit(solution)/shard_map/all_to_all | solution.py:182
  93.9 0.1 copy.11
  94.0 0.0 copy-start.6
  94.0 0.1 broadcast_in_dim.18
  94.1 27.3 %all_to_all.31.in_ref = bf16[4,480,512]{2,1,0:T(8,128)(2,1)S(1)} all-to-all(bf16[4,480,512]{2,1,0:T(8,128)(2,1)S(1)} %broadcast_in_dim.18), channel_id=1, replica_groups=mesh['dp'=32,'task'=8,'mp'=4] {'mp'}, dimensions={0} | all-to-all | bytes 3932160 | tf_op jit(solution)/shard_map/all_to_all | solution.py:185
  121.4 0.0 copy-done.6
  121.4 0.0 copy-start
  121.4 2.4 units.1.hid_ref
  123.8 0.0 copy-done
  123.8 2.2 layers.1
  126.0 24.4 %all_to_all.32.in_ref = bf16[4,480,512]{2,1,0:T(8,128)(2,1)S(1)} all-to-all(bf16[4,480,512]{2,1,0:T(8,128)(2,1)S(1)} %layers.1), channel_id=1, replica_groups=mesh['dp'=32,'task'=8,'mp'=4] {'mp'}, dimensions={0} | all-to-all | bytes 3932160 | tf_op jit(solution)/shard_map/all_to_all | solution.py:185
  150.5 0.0 copy-start.7
  150.5 0.0 copy-start.8
  150.5 0.2 total.1
  150.7 0.0 copy-start.4
  150.7 0.0 copy-start.5
  150.7 1.2 copy.10
  151.9 4.7 %all-to-all-start.3 = ((bf16[32,15,2,256]{3,2,1,0:T(2,128)(2,1)}), bf16[32,15,2,256]{3,2,1,0:T(2,128)(2,1)S(1)}, u32[]{:S(2)}, u32[]{:S(2)}) async-start(bf16[32,15,2,256]{3,2,1,0:T(2,128)(2,1)} %bitcast.5), calls=%async_computation.3 | async-start | bytes 983040 | tf_op jit(solution)/shard_map/all_to_all | solution.py:182
  156.6 0.0 copy-done.7
  156.7 0.1 reshape.30
  156.8 0.0 copy-done.8
  156.8 5.3 %collective-permute-start = (f32[1,8,512]{2,1,0:T(8,128)S(1)}, f32[1,8,512]{2,1,0:T(8,128)S(1)}, u32[]{:S(2)}, u32[]{:S(2)}) collective-permute-start(f32[1,8,512]{2,1,0:T(8,128)S(1)} %fusion), channel_id=1, source_target_pairs={{0,4},{4,0},{8,12},{12,8},{16,20},{20,16},{24,28},{28,24},{1,5},{5... | collective-permute-start | bytes 49160 | tf_op jit(solution)/shard_map/ppermute | solution.py:161
  162.1 0.8 collective-permute-done
  162.9 3.2 %collective-permute-start.1 = (f32[2,8,512]{2,1,0:T(8,128)S(1)}, f32[2,8,512]{2,1,0:T(8,128)S(1)}, u32[]{:S(2)}, u32[]{:S(2)}) collective-permute-start(f32[2,8,512]{2,1,0:T(8,128)S(1)} %pad_maximum_fusion.2), channel_id=1, source_target_pairs={{0,8},{4,12},{8,0},{12,4},{16,24},{20,28},{24,16},{28,20},{1,9},{5... | collective-permute-start | bytes 98312 | tf_op jit(solution)/shard_map/ppermute | solution.py:161
  166.1 1.7 collective-permute-done.1
  167.9 4.8 %collective-permute-start.2 = (f32[4,8,512]{2,1,0:T(8,128)S(1)}, f32[4,8,512]{2,1,0:T(8,128)S(1)}, u32[]{:S(2)}, u32[]{:S(2)}) collective-permute-start(f32[4,8,512]{2,1,0:T(8,128)S(1)} %pad_maximum_fusion.1), channel_id=1, source_target_pairs={{0,16},{4,20},{8,24},{12,28},{16,0},{20,4},{24,8},{28,12},{1,17},{... | collective-permute-start | bytes 196616 | tf_op jit(solution)/shard_map/ppermute | solution.py:161
  172.7 2.0 collective-permute-done.2
  174.7 37.7 %all-to-all-done.3 = bf16[32,15,2,256]{3,2,1,0:T(2,128)(2,1)S(1)} async-done(((bf16[32,15,2,256]{3,2,1,0:T(2,128)(2,1)}), bf16[32,15,2,256]{3,2,1,0:T(2,128)(2,1)S(1)}, u32[]{:S(2)}, u32[]{:S(2)}) %all-to-all-start.3) | async-done | bytes 491552 | tf_op jit(solution)/shard_map/all_to_all | solution.py:182
  212.4 0.1 copy.12
  212.5 0.0 copy-done.4
  212.5 0.0 copy-done.5
  212.5 0.6 combine.1
  213.1 10.7 %all_to_all.33.z_ref = bf16[4,192,512]{2,1,0:T(8,128)(2,1)S(1)} all-to-all(bf16[4,192,512]{2,1,0:T(8,128)(2,1)S(1)} %combine.1), channel_id=1, replica_groups=mesh['dp'=32,'task'=8,'mp'=4] {'mp'}, dimensions={0} | all-to-all | bytes 1572864 | tf_op jit(solution)/shard_map/all_to_all | solution.py:185
  223.9 1.2 predict.1
  225.1 13.0 %all-to-all-start.5 = ((f32[8,1,192]{2,1,0:T(1,128)}), f32[8,1,192]{2,1,0:T(1,128)S(1)}, u32[]{:S(2)}, u32[]{:S(2)}) async-start(f32[8,1,192]{2,1,0:T(1,128)} %predict.1), calls=%async_computation.5 | async-start | bytes 16384 | tf_op jit(solution)/shard_map/all_to_all | solution.py:259
  238.1 0.0 copy-start.1
  238.1 2.2 copy-done.1
  240.3 2.6 %gradient.1 = bf16[192,1024]{1,0:T(8,128)(2,1)} custom-call(s32[1]{0:T(128)} %bitcast.8.me_ref, f32[8,8,512]{2,1,0:T(8,128)S(1)} %pad_maximum_fusion.side_ref, bf16[4,192,512]{2,1,0:T(8,128)(2,1)S(1)} %all_to_all.33.z_ref, bf16[8,1024,256]{2,1,0:T(8,128)(2,1)S(1)} %copy-done.1), custom_call_target="tpu_custom_call" | custom-call | flops 805306368 | bytes 4194304 | tf_op jit(solution)/shard_map/gradient/pallas_call | solution.py:245
  242.8 0.0 all-to-all-done.5
  242.9 0.7 reshape.32
  (7 shorter events, 0.1 us)
Async XLA Ops:
  0.6 1.1 copy-start.2
  1.8 0.7 copy-start.3
  94.0 27.4 %copy-start.6 = (bf16[1,2048,1024]{2,1,0:T(8,128)(2,1)S(1)}, bf16[1,2048,1024]{2,1,0:T(8,128)(2,1)}, u32[]{:S(2)}) copy-start(bf16[1,2048,1024]{2,1,0:T(8,128)(2,1)} %w_ref.1) | copy-start | bytes 12582916
  121.4 2.4 copy-start
  150.5 6.2 %copy-start.7 = (f32[1,1536]{1,0:T(1,128)S(1)}, f32[1,1536]{1,0:T(1,128)}, u32[]{:S(2)}) copy-start(f32[1,1536]{1,0:T(1,128)} %param.13) | copy-start | bytes 18436
  150.5 6.3 %copy-start.8 = (f32[1,256]{1,0:T(1,128)S(1)}, f32[1,256]{1,0:T(1,128)}, u32[]{:S(2)}) copy-start(f32[1,256]{1,0:T(1,128)} %param.12) | copy-start | bytes 3076
  150.7 61.8 %copy-start.4 = (s32[192,2]{0,1:T(2,128)S(1)}, s32[192,2]{0,1:T(2,128)}, u32[]{:S(2)}) copy-start(s32[192,2]{0,1:T(2,128)} %param.8) | copy-start | bytes 4612
  150.7 61.8 %copy-start.5 = (s32[192,2]{0,1:T(2,128)S(1)}, s32[192,2]{0,1:T(2,128)}, u32[]{:S(2)}) copy-start(s32[192,2]{0,1:T(2,128)} %param.9) | copy-start | bytes 4612
  151.9 60.5 %all-to-all-start.3 = ((bf16[32,15,2,256]{3,2,1,0:T(2,128)(2,1)}), bf16[32,15,2,256]{3,2,1,0:T(2,128)(2,1)S(1)}, u32[]{:S(2)}, u32[]{:S(2)}) async-start(bf16[32,15,2,256]{3,2,1,0:T(2,128)(2,1)} %bitcast.5), calls=%async_computation.3 | async-start | bytes 983040 | tf_op jit(solution)/shard_map/all_to_all | solution.py:182
  156.8 6.2 %collective-permute-start = (f32[1,8,512]{2,1,0:T(8,128)S(1)}, f32[1,8,512]{2,1,0:T(8,128)S(1)}, u32[]{:S(2)}, u32[]{:S(2)}) collective-permute-start(f32[1,8,512]{2,1,0:T(8,128)S(1)} %fusion), channel_id=1, source_target_pairs={{0,4},{4,0},{8,12},{12,8},{16,20},{20,16},{24,28},{28,24},{1,5},{5... | collective-permute-start | bytes 49160 | tf_op jit(solution)/shard_map/ppermute | solution.py:161
  162.9 4.9 %collective-permute-start.1 = (f32[2,8,512]{2,1,0:T(8,128)S(1)}, f32[2,8,512]{2,1,0:T(8,128)S(1)}, u32[]{:S(2)}, u32[]{:S(2)}) collective-permute-start(f32[2,8,512]{2,1,0:T(8,128)S(1)} %pad_maximum_fusion.2), channel_id=1, source_target_pairs={{0,8},{4,12},{8,0},{12,4},{16,24},{20,28},{24,16},{28,20},{1,9},{5... | collective-permute-start | bytes 98312 | tf_op jit(solution)/shard_map/ppermute | solution.py:161
  167.9 6.8 %collective-permute-start.2 = (f32[4,8,512]{2,1,0:T(8,128)S(1)}, f32[4,8,512]{2,1,0:T(8,128)S(1)}, u32[]{:S(2)}, u32[]{:S(2)}) collective-permute-start(f32[4,8,512]{2,1,0:T(8,128)S(1)} %pad_maximum_fusion.1), channel_id=1, source_target_pairs={{0,16},{4,20},{8,24},{12,28},{16,0},{20,4},{24,8},{28,12},{1,17},{... | collective-permute-start | bytes 196616 | tf_op jit(solution)/shard_map/ppermute | solution.py:161
  225.1 17.7 %all-to-all-start.5 = ((f32[8,1,192]{2,1,0:T(1,128)}), f32[8,1,192]{2,1,0:T(1,128)S(1)}, u32[]{:S(2)}, u32[]{:S(2)}) async-start(f32[8,1,192]{2,1,0:T(1,128)} %predict.1), calls=%async_computation.5 | async-start | bytes 16384 | tf_op jit(solution)/shard_map/all_to_all | solution.py:259
  238.1 2.2 copy-start.1
